TPU v7x, 32 devices: a whole 2x2x4 slice. The times are simulated.
32 devices in a mesh: seq: 4 (over z), head: 8 (over y, x, core).
Axes of the slice: x: 2, y: 2, z: 4, core: 2. Of those that a mesh axis runs over, the one named last changes fastest.
Arguments:
- x_in: bfloat16 [2048, 8192], P('seq', 'head'), may hold values from -6 to 6
- z_in: bfloat16 [2048, 8192], P('seq', 'head'), may hold values from -6 to 6
- bc_in: bfloat16 [2048, 2048], P('seq'), may hold values from -6 to 6
- conv_x: float32 [4, 8192], P(None, 'head'), may hold values from -3 to 3
- conv_bc: float32 [4, 2048], replicated, may hold values from -3 to 3
- dt: float32 [128, 2048], P('head', 'seq'), may hold values from 0 to 3, as said below
- a_log: float32 [128], P('head'), may hold values from -2 to 1, as said below
- skip_d: float32 [128], P('head'), may hold values from 0.5 to 1.5
- norm_gain: float32 [8192], P('head'), may hold values from 0.5 to 1.5
- seg_ids: int32 [2048], P('seq'), may hold values from 0 to 3, as said below
Outputs:
- mixed: bfloat16 [2048, 8192], P('seq', 'head')
Inputs may be any that keep to these rules, and one draw needn't show every extreme that they name: `a_log`: log of a decay rate of order one. `dt`: positive step sizes. `seg_ids`: document numbers never fall along the window, every document is nonempty, and the longest document holds exactly 1024 tokens.
All inputs are finite; a program needn't handle non-finite values.
Results may differ from a plain program's by a relative error of at most 0.0051.
Values may be sent and summed in bfloat16 or wider, within the bound.
No kernel may reach another device: no remote copies, remote signals or barrier semaphores. Data moves between devices by JAX's collectives and lax.ppermute only.
A program may use at most 64 MiB of HBM per device.

v0:
```python
import jax
import jax.numpy as jnp
from jax import lax
from jax.sharding import PartitionSpec as P

HEADS = 128
HEAD_DIM = 64
STATE = 128
GROUPS = 8
KERNEL = 4
SPAN = 128


def shifted(value, axis, steps):
    count = lax.axis_size(axis)
    first, last = (max(0, -steps), min(count, count - steps))
    return lax.ppermute(value, axis, [(source, source + steps) for source in range(first, last)])


def carried_in(x, axis, combine, identity):
    peers, place = (lax.axis_size(axis), lax.axis_index(axis))
    everything = jax.tree.map(
        lambda part, kind: lax.all_gather(part.astype(kind), axis), x, (jnp.bfloat16, jnp.bfloat16)
    )
    start = jax.tree.map(
        lambda part, zero: jnp.broadcast_to(jnp.asarray(zero, part.dtype), part.shape), x, identity
    )

    def hop(k, before):
        reached = k < place
        new = combine(
            before, jax.tree.map(lambda part, own: part[k].astype(own.dtype), everything, x)
        )
        return jax.tree.map(lambda a, b: jnp.where(reached, a, b), new, before)

    return lax.fori_loop(0, peers, hop, start)


def conv_silu(data, tail, weight, seg_float, tail_seg):
    rows = data.shape[0]
    padded = jnp.concatenate([tail, data], 0)
    seg_pad = jnp.concatenate([tail_seg.astype(jnp.float32), seg_float], 0)
    total = jnp.zeros(data.shape, jnp.float32)
    for offset in range(KERNEL):
        window = padded[offset : offset + rows].astype(jnp.float32)
        same_doc = (seg_pad[offset : offset + rows] == seg_float)[:, None]
        total = total + jnp.where(same_doc, window, 0.0) * weight[offset]
    return jax.nn.silu(total).astype(jnp.bfloat16)


def per_device(x_in, z_in, bc_in, conv_x, conv_bc, dt, a_log, skip_d, norm_gain, seg_ids):
    tok_rows = x_in.shape[0]
    local_heads = dt.shape[0]
    per_group = HEADS // GROUPS
    head_index = lax.axis_index("head")
    group = head_index * local_heads // per_group
    b_part = lax.dynamic_slice_in_dim(bc_in, group * STATE, STATE, 1)
    c_part = lax.dynamic_slice_in_dim(bc_in, GROUPS * STATE + group * STATE, STATE, 1)
    bc_mine = jnp.concatenate([b_part, c_part], 1)
    taps_b = lax.dynamic_slice_in_dim(conv_bc, group * STATE, STATE, 1)
    taps_c = lax.dynamic_slice_in_dim(conv_bc, GROUPS * STATE + group * STATE, STATE, 1)
    taps_mine = jnp.concatenate([taps_b, taps_c], 1)
    margin = KERNEL - 1
    tail_x, tail_bc, tail_seg = shifted(
        (
            x_in[tok_rows - margin :],
            bc_mine[tok_rows - margin :],
            seg_ids[tok_rows - margin :].astype(jnp.bfloat16),
        ),
        "seq",
        1,
    )
    seg_float = seg_ids.astype(jnp.float32)
    first_shard = lax.axis_index("seq") == 0
    tail_seg = jnp.where(first_shard, jnp.full(tail_seg.shape, -1.0, jnp.bfloat16), tail_seg)
    x_conv = conv_silu(x_in, tail_x, conv_x, seg_float, tail_seg)
    bc_conv = conv_silu(bc_mine, tail_bc, taps_mine, seg_float, tail_seg)
    prev_seg = tail_seg[margin - 1].astype(jnp.float32)
    spans = tok_rows // SPAN
    x_blocks = x_conv.reshape(spans, SPAN, local_heads, HEAD_DIM)
    b_blocks = bc_conv[:, :STATE].reshape(spans, SPAN, STATE)
    c_blocks = bc_conv[:, STATE:].reshape(spans, SPAN, STATE)
    dt_blocks = dt.reshape(local_heads, spans, SPAN).transpose(1, 0, 2)
    seg_blocks = seg_float.reshape(spans, SPAN)
    seg_before = jnp.concatenate([prev_seg[None], seg_blocks[:-1, -1]])
    rates = jnp.exp(a_log)
    log_decay = jnp.cumsum(-dt_blocks * rates[None, :, None], axis=2)
    causal = jnp.tril(jnp.ones((SPAN, SPAN), bool))
    same_doc = ((seg_blocks[:, :, None] == seg_blocks[:, None, :]) & causal[None])[:, None]
    spread = log_decay[:, :, :, None] - log_decay[:, :, None, :]
    decay = jnp.where(same_doc, jnp.exp(jnp.where(same_doc, spread, 0.0)), 0.0)
    scores = jnp.einsum("ctn,csn->cts", c_blocks, b_blocks, preferred_element_type=jnp.float32)
    weight_tensors = (scores[:, None] * decay * dt_blocks[:, :, None, :]).astype(jnp.bfloat16)
    y_diag = jnp.einsum(
        "chts,cshp->cthp", weight_tensors, x_blocks, preferred_element_type=jnp.float32
    )
    same_end = (seg_blocks == seg_blocks[:, -1:]).astype(jnp.float32)
    to_end = jnp.exp(log_decay[:, :, -1:] - log_decay) * dt_blocks * same_end[:, None, :]
    x_weighted = (x_blocks.astype(jnp.float32) * to_end.transpose(0, 2, 1)[..., None]).astype(
        jnp.bfloat16
    )
    fresh = jnp.einsum("cshp,csn->chpn", x_weighted, b_blocks, preferred_element_type=jnp.float32)
    keep = (
        jnp.exp(log_decay[:, :, -1])
        * (seg_blocks[:, -1] == seg_before).astype(jnp.float32)[:, None]
    )

    def local_step(carry, item):
        state, factor = carry
        keep_block, fresh_block = item
        return (
            (keep_block[:, None, None] * state + fresh_block, keep_block * factor),
            (state, factor),
        )

    zero_state = jnp.zeros((local_heads, HEAD_DIM, STATE), jnp.float32)
    (total_state, total_keep), (entering, factors) = lax.scan(
        local_step, (zero_state, jnp.ones((local_heads,), jnp.float32)), (keep, fresh)
    )

    def combine(earlier, later):
        return (earlier[0] * later[0], later[0][:, None, None] * earlier[1] + later[1])

    incoming = carried_in(
        (total_keep, total_state),
        "seq",
        combine,
        (jnp.ones_like(total_keep), jnp.zeros_like(total_state)),
    )[1]
    starts = entering + factors[:, :, None, None] * incoming[None]
    alive = (seg_blocks == seg_before[:, None]).astype(jnp.float32)
    y_carry = jnp.einsum(
        "ctn,chpn->cthp", c_blocks.astype(jnp.float32), starts, precision=lax.Precision.HIGHEST
    )
    y_carry = y_carry * (jnp.exp(log_decay).transpose(0, 2, 1) * alive[:, :, None])[..., None]
    summed = (y_diag + y_carry).reshape(tok_rows, local_heads, HEAD_DIM)
    summed = summed + skip_d[None, :, None] * x_conv.reshape(
        tok_rows, local_heads, HEAD_DIM
    ).astype(jnp.float32)
    gated = summed * jax.nn.silu(z_in.reshape(tok_rows, local_heads, HEAD_DIM).astype(jnp.float32))
    squares = jnp.sum(gated * gated, axis=(1, 2))
    gathered = lax.all_gather(squares[None], "head", axis=0, tiled=True)
    total_squares = jnp.sum(gathered, axis=0)
    mean_sq = total_squares / (HEADS * HEAD_DIM)
    normalized_output = (gated * lax.rsqrt(mean_sq + 1e-05)[:, None, None]).reshape(
        tok_rows, local_heads * HEAD_DIM
    )
    return (normalized_output * norm_gain).astype(jnp.bfloat16)


def solution(mesh):
    in_specs = (
        P("seq", "head"),
        P("seq", "head"),
        P("seq", None),
        P(None, "head"),
        P(),
        P("head", "seq"),
        P("head"),
        P("head"),
        P("head"),
        P("seq"),
    )
    out_specs = P("seq", "head")
    return jax.shard_map(
        per_device, mesh=mesh, in_specs=in_specs, out_specs=out_specs, check_vma=False
    )
```

profile of v0, /device:TPU:0, one launch (start us, length us, event | category | flops | bytes accessed | tf_op | source)
XLA Modules:
  0.0 97.1 jit_solution(2739810109216518925)
XLA Ops:
  7.6 5.0 %collective-permute-start.2 = (bf16[3,256]{1,0:T(4,128)(2,1)S(1)}, bf16[3,256]{1,0:T(4,128)(2,1)S(1)}, u32[]{:S(2)}, u32[]{:S(2)}) collective-permute-start(bf16[3,256]{1,0:T(4,128)(2,1)S(1)} %fusion.36), channel_id=1, source_target_pairs={{0,8},{8,16},{16,24},{1,9},{9,17},{17,25},{2,10},{10,18},{18,26},{... | collective-permute-start | bytes 4616 | tf_op jit(solution)/shard_map/ppermute | solution.py:17
  13.4 3.5 %collective-permute-start = (bf16[3]{0:T(256)(128)(2,1)S(1)}, bf16[3]{0:T(256)(128)(2,1)S(1)}, u32[]{:S(2)}, u32[]{:S(2)}) collective-permute-start(bf16[3]{0:T(256)(128)(2,1)S(1)} %slice.84), channel_id=1, source_target_pairs={{0,8},{8,16},{16,24},{1,9},{9,17},{17,25},{2,10},{10,18},{18,26},{... | collective-permute-start | bytes 26 | tf_op jit(solution)/shard_map/ppermute | solution.py:17
  17.8 3.5 %collective-permute-start.1 = (bf16[3,1024]{0,1:T(8,128)(2,1)S(1)}, bf16[3,1024]{0,1:T(8,128)(2,1)S(1)}, u32[]{:S(2)}, u32[]{:S(2)}) collective-permute-start(bf16[3,1024]{0,1:T(8,128)(2,1)S(1)} %copy.69), channel_id=1, source_target_pairs={{0,8},{8,16},{16,24},{1,9},{9,17},{17,25},{2,10},{10,18},{18,26},{... | collective-permute-start | bytes 18440 | tf_op jit(solution)/shard_map/ppermute | solution.py:17
  21.4 1.5 %copy.70 = bf16[512,1024]{0,1:T(8,128)(2,1)S(1)} copy(bf16[512,1024]{1,0:T(8,128)(2,1)} %param.14) | data formatting | bytes 2097152 | tf_op args[0]
  23.9 1.1 %reduce_window_sum.11 = f32[4,16,128]{2,1,0:T(8,128)S(1)} reduce-window(f32[4,16,128]{2,1,0:T(8,128)S(1)} %negate_multiply_fusion, f32[]{:T(128)} %constant.81.clone.1), window={size=1x1x128 pad=0_0x0_0x127_0}, to_apply=%region_0.1 | reduce-window | flops 1040384 | bytes 65540 | tf_op jit(solution)/shard_map/jit(cumsum)/reduce_window_sum | solution.py:87
  28.0 2.5 %multiply_convert_fusion.2 = bf16[512,1024]{0,1:T(8,128)(2,1)S(1)} fusion(bf16[512,1024]{0,1:T(8,128)(2,1)S(1)} %copy.70, bf16[3,1024]{0,1:T(8,128)(2,1)S(1)} %collective-permute-done.1, f32[1024]{0:T(1024)S(1)} %bitcast.111, f32[1024]{0:T(1024)S(1)} %bitcast.112, f32[1024]{0:T(1024)S(1)} %bitcast.110, f32[1024]{0:T(1024)S(1)} %bitcast.109, ...), kind=kLoop, calls=%fused_computation.33 | loop fusion | flops 15204352 | bytes 2121728 | tf_op jit(solution)/shard_map/convert_element_type | solution.py:48
  30.6 1.3 %reshape.117 = bf16[4,128,16,64]{1,0,3,2:T(4,128)(2,1)} reshape(bf16[512,1024]{0,1:T(8,128)(2,1)S(1)} %multiply_convert_fusion.2) | data formatting | bytes 2097152 | tf_op jit(solution)/shard_map/reshape | solution.py:80
  31.9 1.6 %fusion.27 = f32[4,16,64,128]{3,2,1,0:T(8,128)S(1)} fusion(bf16[4,128,128,1]{2,1,3,0:T(8,128)(2,1)S(1)} %bitcast.105, f32[4,128,16]{1,2,0:T(8,128)S(1)} %fusion.35, bf16[4,128,16,64]{1,0,3,2:T(4,128)(2,1)} %reshape.117), kind=kOutput, calls=%fused_computation.41 | convolution fusion | flops 135790592 | bytes 3309568 | tf_op jit(solution)/shard_map/cshp,csn->chpn/dot_general | solution.py:102
  33.5 4.1 %while.31 = (s32[]{:T(128)}, f32[16,64,128]{2,1,0:T(8,128)S(1)}, f32[16]{0:T(128)S(1)}, f32[4,16,64,128]{3,2,1,0:T(8,128)}, f32[4,16]{1,0:T(4,128)S(1)}, /*index...) while((s32[]{:T(128)}, f32[16,64,128]{2,1,0:T(8,128)S(1)}, ...), condition=%wide.region_2.3_spmd.clone, body=%wide.region_1.2_spmd.clone.sunk | while | flops 524323 | bytes 2622581 | solution.py:117
  38.5 1.5 %copy.77 = bf16[512,1024]{0,1:T(8,128)(2,1)S(1)} copy(bf16[512,1024]{1,0:T(8,128)(2,1)} %param.15) | data formatting | bytes 2097152 | tf_op args[1]
  40.0 1.7 %reshape.125 = f32[4,128,16,64]{1,0,3,2:T(4,128)} reshape(bf16[512,1024]{0,1:T(8,128)(2,1)S(1)} %copy.77) | data formatting | bytes 3145728 | tf_op jit(solution)/shard_map/convert_element_type | solution.py:140
  43.9 9.7 %all-reduce = bf16[64]{0:T(256)(128)(2,1)S(1)} all-reduce(bf16[64]{0:T(256)(128)(2,1)S(1)} %dynamic-update-slice), channel_id=2, replica_groups=mesh['seq'=4,'head'=8] {'seq'}, use_global_device_ids=true, to_apply=%add | all-reduce | flops 64 | bytes 256
  53.6 3.2 %fusion.4 = f32[4,16,64,128]{3,2,1,0:T(8,128)} fusion(f32[4,16,128]{2,1,0:T(8,128)S(1)} %bitcast_bitcast_fusion.1, f32[4,16,128]{2,1,0:T(8,128)S(1)} %reduce_window_sum.11, f32[4,128,128]{2,1,0:T(8,128)S(1)} %fusion.45, pred[4,128,128]{2,1,0:T(8,128)(4,1)S(1)} %compare_and_fusion, bf16[4,128,16,64]{1,0,3,2:T(4,128)(2,1)S(1)} %copy-done.3), kind=kOutput, calls=%fused_computation.13 | convolution fusion | flops 140509184 | bytes 3538944 | tf_op jit(solution)/shard_map/chts,cshp->cthp/dot_general | solution.py:94
  56.8 8.5 %all-gather.5.cloned.1.call-done = bf16[64,64,128]{2,1,0:T(8,128)(2,1)} async-done(((bf16[16,64,128]{2,1,0:T(8,128)(2,1)}), bf16[64,64,128]{2,1,0:T(8,128)(2,1)}) %all-gather.5.cloned.1.call-update) | async-done | bytes 1048592 | tf_op jit(solution)/shard_map/all_gather | solution.py:23
  65.3 4.5 %while.32 = (s32[]{:T(128)}, f32[16,64,128]{2,1,0:T(8,128)S(1)}, s32[]{:T(128)}, bf16[4,16]{1,0:T(4,128)(2,1)S(1)}, bf16[4,16,64,128]{3,2,1,0:T(8,128)(2,1)}, /*index=5*/s32[]{:T(128)}, s32[]{:T(128)}) while((s32[]{:T(128)}, f32[16,64,128]{2,1,0:T(8,128)S(1)}, s32[]{:T(128)}, bf16[4,16]{1,0:T(4,128)(2,1)S(1)}, ...), condition=%wide.region_4.5_spmd.clone, body=%wide.region_3.4_spmd.clone.sunk | while | flops 655380 | bytes 1310985 | solution.py:36
  65.3 1.1 %fusion.56 = f32[16,64,128]{2,1,0:T(8,128)S(1)} fusion(f32[16,64,128]{2,1,0:T(8,128)S(1)} %get-tuple-element.359, bf16[4,16,64,128]{3,2,1,0:T(8,128)(2,1)} %get-tuple-element.369, s32[]{:T(128)} %get-tuple-element.358, f32[16]{0:T(128)S(1)} %bitcast_convert_fusion.2, pred[]{:T(512)S(6)} %compare.9, pred[]{:T(512)S(6)} %lt.37), kind=kLoop, calls=%fused_computation.8.clone.1 | loop fusion | flops 655360 | bytes 1310790 | tf_op jit(solution)/shard_map/while/body/eval_jaxpr/jit(_where)/select_n | solution.py:34
  66.4 1.1 %fusion.56 = f32[16,64,128]{2,1,0:T(8,128)S(1)} fusion(f32[16,64,128]{2,1,0:T(8,128)S(1)} %get-tuple-element.359, bf16[4,16,64,128]{3,2,1,0:T(8,128)(2,1)} %get-tuple-element.369, s32[]{:T(128)} %get-tuple-element.358, f32[16]{0:T(128)S(1)} %bitcast_convert_fusion.2, pred[]{:T(512)S(6)} %compare.9, pred[]{:T(512)S(6)} %lt.37), kind=kLoop, calls=%fused_computation.8.clone.1 | loop fusion | flops 655360 | bytes 1310790 | tf_op jit(solution)/shard_map/while/body/eval_jaxpr/jit(_where)/select_n | solution.py:34
  67.5 1.1 %fusion.56 = f32[16,64,128]{2,1,0:T(8,128)S(1)} fusion(f32[16,64,128]{2,1,0:T(8,128)S(1)} %get-tuple-element.359, bf16[4,16,64,128]{3,2,1,0:T(8,128)(2,1)} %get-tuple-element.369, s32[]{:T(128)} %get-tuple-element.358, f32[16]{0:T(128)S(1)} %bitcast_convert_fusion.2, pred[]{:T(512)S(6)} %compare.9, pred[]{:T(512)S(6)} %lt.37), kind=kLoop, calls=%fused_computation.8.clone.1 | loop fusion | flops 655360 | bytes 1310790 | tf_op jit(solution)/shard_map/while/body/eval_jaxpr/jit(_where)/select_n | solution.py:34
  68.7 1.1 %fusion.56 = f32[16,64,128]{2,1,0:T(8,128)S(1)} fusion(f32[16,64,128]{2,1,0:T(8,128)S(1)} %get-tuple-element.359, bf16[4,16,64,128]{3,2,1,0:T(8,128)(2,1)} %get-tuple-element.369, s32[]{:T(128)} %get-tuple-element.358, f32[16]{0:T(128)S(1)} %bitcast_convert_fusion.2, pred[]{:T(512)S(6)} %compare.9, pred[]{:T(512)S(6)} %lt.37), kind=kLoop, calls=%fused_computation.8.clone.1 | loop fusion | flops 655360 | bytes 1310790 | tf_op jit(solution)/shard_map/while/body/eval_jaxpr/jit(_where)/select_n | solution.py:34
  69.8 4.9 %fusion.9 = (f32[4,128]{1,0:T(4,128)S(1)}, f32[4,128,16,64]{1,3,2,0:T(8,128)S(1)}) fusion(f32[4,128,16,64]{1,0,3,2:T(4,128)} %reshape.125, f32[16]{0:T(128)S(1)} %copy-done.7, bf16[4,128,16,64]{1,0,3,2:T(4,128)(2,1)S(1)} %copy-done.3, f32[4,128,16]{1,2,0:T(8,128)S(1)} %multiply_bitcast_fusion, bf16[4,128,128,1]{2,1,3,0:T(8,128)(2,1)S(1)} %bitcast.108, ...), kind=kOutput, calls=%fused_computation.18 | convolution fusion | flops 812645888 | bytes 10127680 | tf_op jit(solution)/shard_map/ctn,chpn->cthp/dot_general | solution.py:132
  74.7 2.8 %copy.76 = f32[4,128,16,64]{1,0,3,2:T(4,128)} copy(f32[4,128,16,64]{1,3,2,0:T(8,128)S(1)} %get-tuple-element.243) | data formatting | bytes 4194304 | tf_op jit(solution)/shard_map/add | solution.py:136
  77.5 8.9 %all-gather.2 = f32[8,1,512]{2,1,0:T(1,128)S(1)} all-gather(f32[1,1,512]{2,1,0:T(1,128)S(1)} %bitcast.117), channel_id=1, replica_groups=mesh['seq'=4,'head'=8] {'head'}, dimensions={0}, use_global_device_ids=true | all-gather | bytes 18432 | tf_op jit(solution)/shard_map/all_gather | solution.py:142
  86.4 2.5 %fusion.13 = bf16[512,1024]{0,1:T(8,128)(2,1)S(1)} fusion(f32[128,8,4,128]{3,2,1,0:T(4,128)} %bitcast.103, bf16[512,1024]{0,1:T(8,128)(2,1)S(1)} %copy-done.2, f32[1024]{0:T(1024)S(1)} %copy-done.6, f32[512]{0:T(512)S(1)} %add_rsqrt_fusion, f32[1024]{0:T(1024)S(1)} %mul.328, bf16[512,1024]{0,1:T(8,128)(2,1)S(1)} %copy.77), kind=kLoop, calls=%fused_computation.23 | loop fusion | flops 6291456 | bytes 5253120 | tf_op jit(solution)/shard_map/convert_element_type | solution.py:148
  88.9 1.3 %copy.80 = bf16[512,1024]{1,0:T(8,128)(2,1)} copy(bf16[512,1024]{0,1:T(8,128)(2,1)S(1)} %fusion.13) | data formatting | bytes 2097152 | tf_op jit(solution)/shard_map/convert_element_type | solution.py:148
  (90 shorter events, 12.5 us)
Async XLA Ops:
  6.5 17.3 %copy-start = (f32[16,512]{1,0:T(8,128)S(1)}, f32[16,512]{1,0:T(8,128)}, u32[]{:S(2)}) copy-start(f32[16,512]{1,0:T(8,128)} %param.19) | copy-start | bytes 98308
  6.5 18.8 %copy-start.4 = (s32[512]{0:T(512)S(1)}, s32[512]{0:T(512)}, u32[]{:S(2)}) copy-start(s32[512]{0:T(512)} %param.23) | copy-start | bytes 6148
  6.5 17.1 %copy-start.5 = (f32[4,1024]{1,0:T(4,128)S(1)}, f32[4,1024]{1,0:T(4,128)}, u32[]{:S(2)}) copy-start(f32[4,1024]{1,0:T(4,128)} %param.17) | copy-start | bytes 49156
  6.5 17.1 %copy-start.8 = (f32[16]{0:T(128)S(1)}, f32[16]{0:T(128)}, u32[]{:S(2)}) copy-start(f32[16]{0:T(128)} %param.20) | copy-start | bytes 196
  6.5 58.7 %all-gather.5.cloned.1.call-start = ((), (), s32[]{:S(2)}) async-start(), calls=%async_computation | async-start | bytes 1310720 | tf_op jit(solution)/shard_map/all_gather | solution.py:23
  7.6 19.5 %collective-permute-start.2 = (bf16[3,256]{1,0:T(4,128)(2,1)S(1)}, bf16[3,256]{1,0:T(4,128)(2,1)S(1)}, u32[]{:S(2)}, u32[]{:S(2)}) collective-permute-start(bf16[3,256]{1,0:T(4,128)(2,1)S(1)} %fusion.36), channel_id=1, source_target_pairs={{0,8},{8,16},{16,24},{1,9},{9,17},{17,25},{2,10},{10,18},{18,26},{... | collective-permute-start | bytes 4616 | tf_op jit(solution)/shard_map/ppermute | solution.py:17
  13.4 11.8 %collective-permute-start = (bf16[3]{0:T(256)(128)(2,1)S(1)}, bf16[3]{0:T(256)(128)(2,1)S(1)}, u32[]{:S(2)}, u32[]{:S(2)}) collective-permute-start(bf16[3]{0:T(256)(128)(2,1)S(1)} %slice.84), channel_id=1, source_target_pairs={{0,8},{8,16},{16,24},{1,9},{9,17},{17,25},{2,10},{10,18},{18,26},{... | collective-permute-start | bytes 26 | tf_op jit(solution)/shard_map/ppermute | solution.py:17
  17.8 10.1 %collective-permute-start.1 = (bf16[3,1024]{0,1:T(8,128)(2,1)S(1)}, bf16[3,1024]{0,1:T(8,128)(2,1)S(1)}, u32[]{:S(2)}, u32[]{:S(2)}) collective-permute-start(bf16[3,1024]{0,1:T(8,128)(2,1)S(1)} %copy.69), channel_id=1, source_target_pairs={{0,8},{8,16},{16,24},{1,9},{9,17},{17,25},{2,10},{10,18},{18,26},{... | collective-permute-start | bytes 18440 | tf_op jit(solution)/shard_map/ppermute | solution.py:17
  30.6 1.3 %copy-start.1 = (bf16[512,1024]{0,1:T(8,128)(2,1)}, bf16[512,1024]{0,1:T(8,128)(2,1)S(1)}, u32[]{:S(2)}) copy-start(bf16[512,1024]{0,1:T(8,128)(2,1)S(1)} %multiply_convert_fusion.2) | copy-start | bytes 3145732
  40.0 1.8 %copy-start.7 = (f32[16]{0:T(128)S(1)}, f32[16]{0:T(128)}, u32[]{:S(2)}) copy-start(f32[16]{0:T(128)} %param.21) | copy-start | bytes 196
  40.0 1.9 %copy-start.9 = (u32[32]{0:T(128)S(1)}, u32[32]{0:T(128)}, u32[]{:S(2)}) copy-start(u32[32]{0:T(128)} %constant.97) | copy-start | bytes 388
  40.0 13.6 %copy-start.3 = (bf16[4,128,16,64]{1,0,3,2:T(4,128)(2,1)S(1)}, bf16[4,128,16,64]{1,0,3,2:T(4,128)(2,1)}, u32[]{:S(2)}) copy-start(bf16[4,128,16,64]{1,0,3,2:T(4,128)(2,1)} %reshape.117) | copy-start | bytes 3145732
  74.7 11.7 %copy-start.2 = (bf16[512,1024]{0,1:T(8,128)(2,1)S(1)}, bf16[512,1024]{0,1:T(8,128)(2,1)}, u32[]{:S(2)}) copy-start(bf16[512,1024]{0,1:T(8,128)(2,1)} %copy-done.1) | copy-start | bytes 3145732
  74.7 11.7 %copy-start.6 = (f32[1024]{0:T(1024)S(1)}, f32[1024]{0:T(1024)}, u32[]{:S(2)}) copy-start(f32[1024]{0:T(1024)} %param.22) | copy-start | bytes 12292
Sparse Core Ops, SparseCore 0:
  38.6 26.6 all-gather.4
where the time goes:
time: 97.6 us; the launch traced here: 97.1 us
  blocking collectives  18.5 us (19%)
  other arithmetic  17.8 us (18%)
  local copies, waits for them, and re-layouts  15.1 us (15%)
  between operations  15.1 us (15%)
  starting transfers between devices  12 us (12%)
  matrix products  9.94 us (10%)
  waiting for transfers between devices  8.49 us (9%)
    ppermute x3, starting transfers between devices, shifted(): lax.ppermute(value, axis, [(source, source + steps) for source in range(f...  11.9 us
    unnamed x1, blocking collectives  9.67 us
    all_gather x1, blocking collectives, per_device(): gathered = lax.all_gather(squares[None], 'head', axis=0, tiled=True)  8.86 us
    all_gather x1, waiting for transfers between devices, carried_in(): lax.all_gather(part.astype(kind), axis)  8.46 us
    dot_general x1, matrix products, per_device(): jnp.einsum('ctn,chpn->cthp', c_blocks.astype(jnp.float32), starts, precis...  4.94 us
    select_n x4, other arithmetic, hop(): return jax.tree.map(lambda a, b: jnp.where(reached, a, b), new, before)  4.36 us
    unnamed x25, local copies, waits for them, and re-layouts  3.98 us
    dynamic_update_slice x4, other arithmetic, per_device(): lax.scan(local_step, (zero_state, jnp.ones((local_heads,), jnp.float32)),...  3.37 us
  transfers between devices with their start and end apart: 4, of which 1 were waited for; matrix products, arithmetic and copies ran while one was open for 16% of the time, Pallas kernels for 0%

commit v1 on v0

v1 whole, which is shorter than its diff:
```python
import functools
import jax
import jax.numpy as jnp
from jax import lax
from jax.experimental import pallas as pl
from jax.experimental.pallas import tpu as pltpu
from jax.sharding import PartitionSpec as P

HEADS = 128
HEAD_DIM = 64
STATE = 128
GROUPS = 8
KERNEL = 4
SPAN = 128
LOG2E = 1.4426950408889634
TINY = 1e-37
TAIL = 16
f32 = jnp.float32
bf16 = jnp.bfloat16


def mm(a, b, ca=1, cb=0):
    return lax.dot_general(a, b, (((ca,), (cb,)), ((), ())), preferred_element_type=f32)


def iota(shape, axis):
    return lax.broadcasted_iota(jnp.int32, shape, axis)


def split(value, parts):
    pieces = []
    for _ in range(parts):
        piece = value.astype(bf16)
        pieces.append(piece)
        value = value - piece.astype(f32)
    return jnp.concatenate(pieces, 0)


def expander(heads, parts, width, first):
    row = iota((parts * heads, width), 0) & (heads - 1)
    col = (iota((parts * heads, width), 1) >> 6) + first
    return jnp.where(row == col, 1.0, 0.0).astype(bf16)


def silu_from_half(half):
    return half + half * jnp.tanh(half)


def blk(b):
    return slice(b * SPAN, (b + 1) * SPAN)


def to_column(row):
    n = row.shape[1]
    rows = jnp.where(iota((16, n), 0) == 0, row, 0.0).astype(bf16)
    return mm(rows, jnp.ones((16, 128), bf16), 0, 0)


def chunk_state(hp, first, x, taps, shift, bt, rows, kcols, drop, xc, lstate, krows, msg):
    tokens, wc = x.shape
    nb = tokens // SPAN
    kr = mm(split(kcols, 3), expander(hp, 3, wc, first), 0, 0)[:16]
    krows[...] = kr
    tile = 256 if wc % 256 == 0 else wc
    ex = expander(hp, 2, wc, first)
    for j in range(wc // tile):
        js = slice(j * tile, (j + 1) * tile)
        state = None
        for b in range(nb):
            if b == 0:
                sh = mm(shift[0 : 3 * SPAN, SPAN:], x[blk(0), js])
            else:
                sh = mm(
                    shift[3 * SPAN * b : 3 * SPAN * (b + 1), :],
                    x[(b - 1) * SPAN : (b + 1) * SPAN, js],
                )
            half = sh[0:SPAN] * taps[0:1, js] + sh[SPAN : 2 * SPAN] * taps[1:2, js]
            half = half + sh[2 * SPAN :] * taps[2:3, js]
            half = half + x[blk(b), js].astype(f32) * taps[3:4, js]
            act = silu_from_half(half)
            if b == 0:
                act = jnp.where(iota(act.shape, 0).astype(f32) < drop, 0.0, act)
            act = act.astype(bf16)
            xc[blk(b), js] = act
            to_end = mm(split(rows[3 * hp : 4 * hp, blk(b)], 2), ex[:, js], 0, 0)
            weighted = (act.astype(f32) * to_end).astype(bf16)
            fresh = mm(bt[:, blk(b)], weighted)
            state = fresh if b == 0 else state * kr[b : b + 1, js] + fresh
            if b < nb - 1:
                hi = state.astype(bf16)
                lstate[2 * SPAN * b : 2 * SPAN * b + SPAN, js] = hi
                lstate[2 * SPAN * b + SPAN : 2 * SPAN * (b + 1), js] = (
                    state - hi.astype(f32)
                ).astype(bf16)
        msg[0:STATE, js] = state.astype(bf16)


def first_kernel(
    heads, hp, nch,
    x_any, bc_any, tapbc_any, tapx, dt_ref, alog_ref, skip_ref, seg_ref,
    msg, xc, lstate, krows, bcc, bt, rows, kcols, shift, xhead, bchead, taps_bc,
    xbuf, bcbuf, xtail, sems,
):
    tokens, wc = xbuf.shape
    nb = tokens // SPAN
    group = lax.axis_index("head") * heads // (HEADS // GROUPS)
    col_b = pl.multiple_of(group * STATE, STATE)
    col_c = pl.multiple_of((group + GROUPS) * STATE, STATE)
    width = nch * wc
    copies = [
        pltpu.make_async_copy(bc_any.at[:, pl.ds(col_b, STATE)], bcbuf.at[:, 0:STATE], sems.at[0]),
        pltpu.make_async_copy(bc_any.at[:, pl.ds(col_c, STATE)], bcbuf.at[:, STATE:], sems.at[1]),
        pltpu.make_async_copy(tapbc_any.at[:, pl.ds(col_b, STATE)], taps_bc.at[:, 0:STATE], sems.at[2]),
        pltpu.make_async_copy(tapbc_any.at[:, pl.ds(col_c, STATE)], taps_bc.at[:, STATE:], sems.at[3]),
        pltpu.make_async_copy(x_any.at[:, 0:wc], xbuf, sems.at[4]),
        pltpu.make_async_copy(x_any.at[tokens - TAIL :, :], xtail, sems.at[5]),
        pltpu.make_async_copy(x_any.at[0:TAIL, :], xhead, sems.at[6]),
    ]
    for copy in copies:
        copy.start()
    seg = seg_ref[...].astype(f32)
    seg_first = seg[:, 0:1]
    seg_last = [seg[:, (b + 1) * SPAN - 1 : (b + 1) * SPAN] for b in range(nb)]
    eye = iota((hp, hp), 0) == iota((hp, hp), 1)
    rate = jnp.exp(jnp.sum(jnp.where(eye, alog_ref[...], 0.0), axis=1, keepdims=True))
    skip = jnp.sum(jnp.where(eye, skip_ref[...], 0.0), axis=1, keepdims=True)
    dt = dt_ref[...]
    parts = split(dt * (rate * -LOG2E), 3)
    tri = jnp.where(iota((SPAN, SPAN), 0) <= iota((SPAN, SPAN), 1), 1.0, 0.0).astype(bf16)
    sums = mm(jnp.concatenate([parts[:, blk(b)] for b in range(nb)], 0), tri)
    lane = iota((hp, SPAN), 1)
    lane1 = iota((1, SPAN), 1)
    before = jnp.zeros((hp, 1), f32)
    kc = jnp.where(lane == 11, skip, 0.0)
    for b in range(nb):
        three = sums[3 * hp * b : 3 * hp * (b + 1)]
        cum = three[0:hp] + three[hp : 2 * hp] + three[2 * hp :]
        last = cum[:, SPAN - 1 : SPAN]
        segb, dtb = seg[:, blk(b)], dt[:, blk(b)]
        total = cum + before
        rows[0:hp, blk(b)] = cum
        rows[hp : 2 * hp, blk(b)] = jnp.exp2(total) * jnp.where(segb == seg_first, 1.0, 0.0)
        if b > 0:
            rows[2 * hp : 3 * hp, blk(b)] = jnp.exp2(cum) * jnp.where(segb == seg_last[b - 1], 1.0, 0.0)
            keep = jnp.exp2(last) * jnp.where(seg_last[b] == seg_last[b - 1], 1.0, 0.0)
            kc = kc + jnp.where(lane == b, keep, 0.0)
        else:
            rows[2 * hp : 3 * hp, blk(b)] = jnp.zeros((hp, SPAN), f32)
            is_drop = jnp.where((lane1 < KERNEL - 1) & (segb == seg_first), 1.0, 0.0)
            drop = jnp.sum(is_drop, axis=1, keepdims=True)
            early = jnp.exp2(jnp.where(lane < KERNEL - 1, -cum, 0.0)) * dtb * is_drop
            kc = kc + pltpu.roll(early, 8, 1)
        rows[3 * hp : 4 * hp, blk(b)] = jnp.exp2(last - cum) * dtb * jnp.where(segb == seg_last[b], 1.0, 0.0)
        rows[4 * hp : 5 * hp, blk(b)] = cum - jnp.log2(jnp.maximum(dtb, TINY))
        before = before + last
    fend = jnp.exp2(before) * jnp.where(seg_last[-1] == seg_first, 1.0, 0.0)
    kc = kc + jnp.where(lane == 0, fend, 0.0) + jnp.where(lane == 16, drop, 0.0)
    kcols[...] = kc
    delta = iota((SPAN, SPAN), 1) - iota((SPAN, SPAN), 0)
    for b in range(nb):
        segcol = to_column(seg[:, blk(b)])
        same = segcol == seg[:, blk(b)]
        for k in range(KERNEL - 1):
            back = KERNEL - 1 - k
            r = slice(3 * SPAN * b + SPAN * k, 3 * SPAN * b + SPAN * (k + 1))
            shift[r, SPAN:] = jnp.where((delta == -back) & same, 1.0, 0.0).astype(bf16)
            if b > 0:
                same_prev = segcol == seg[:, blk(b - 1)]
                shift[r, 0:SPAN] = jnp.where((delta == SPAN - back) & same_prev, 1.0, 0.0).astype(bf16)
            else:
                shift[r, 0:SPAN] = jnp.zeros((SPAN, SPAN), bf16)
    for copy in copies[:4]:
        copy.wait()
    bchead[...] = bcbuf[0:TAIL, :]
    tb = taps_bc[...] * 0.5
    for b in range(nb):
        if b == 0:
            sh = mm(shift[0 : 3 * SPAN, SPAN:], bcbuf[blk(0), :])
        else:
            sh = mm(shift[3 * SPAN * b : 3 * SPAN * (b + 1), :], bcbuf[(b - 1) * SPAN : (b + 1) * SPAN, :])
        half = sh[0:SPAN] * tb[0:1] + sh[SPAN : 2 * SPAN] * tb[1:2]
        half = half + sh[2 * SPAN :] * tb[2:3] + bcbuf[blk(b), :].astype(f32) * tb[3:4]
        act = silu_from_half(half).astype(bf16)
        bcc[blk(b), :] = act
        bt[:, blk(b)] = act[:, 0:STATE].T
    for copy in copies[4:]:
        copy.wait()
    chunk_state(
        hp, 0, xbuf, tapx[:, 0:wc] * 0.5, shift, bt, rows, kc, drop, xc, lstate, krows, msg
    )
    lane_last = iota((1, SPAN), 1)
    is_tail = jnp.where((lane_last >= SPAN - (KERNEL - 1)) & (seg[:, blk(nb - 1)] == seg_last[-1]), 1.0, 0.0)
    first_valid = 8.0 - jnp.sum(is_tail, axis=1, keepdims=True)

    def tail_of(value):
        rows8 = value.astype(f32)[8:16]
        return jnp.where(iota(rows8.shape, 0).astype(f32) >= first_valid, rows8, 0.0)

    tile0 = tail_of(xtail[:, 0:wc])
    if nch == 2:
        tile0 = tile0 + pltpu.roll(tail_of(xtail[:, wc:]), 4, 0)
    tile0 = jnp.where(iota(tile0.shape, 0) == 0, seg_last[-1] + 1.0, tile0)
    tail_bc = tail_of(bcbuf[tokens - TAIL :, :])
    tile1 = tail_bc[:, 0:STATE] + pltpu.roll(tail_bc[:, STATE:], 4, 0)
    if wc > STATE:
        tile1 = jnp.concatenate([tile1, jnp.zeros((8, wc - STATE), f32)], 1)
    msg[STATE:, :] = jnp.concatenate([tile0, tile1], 0).astype(bf16)


def next_kernel(hp, first, x_any, tapx, shift, bt, rows, kcols, msg, xc, lstate, krows, xbuf, sem):
    wc = xbuf.shape[1]
    copy = pltpu.make_async_copy(x_any.at[:, wc : 2 * wc], xbuf, sem)
    copy.start()
    copy.wait()
    chunk_state(
        hp, first, xbuf, tapx[:, wc : 2 * wc] * 0.5, shift, bt, rows, kcols[...],
        kcols[0:1, 16:17], xc, lstate, krows, msg,
    )


def early_conv(halo, head, taps):
    rows = jnp.concatenate([halo, head.astype(f32)[0:8]], 0)
    half = rows[5:13] * taps[0:1]
    for k in range(1, KERNEL):
        half = half + rows[5 + k : 13 + k] * taps[k : k + 1]
    return silu_from_half(half)


def relay_state(krows, recv, b8, xw8, flag):
    base = recv.astype(f32) * flag + mm(b8, xw8, 0, 0)
    return (base * krows[0:1]).astype(bf16)


def relay_first(nch, recv, xhead, bchead, tapx, taps_bc, seg_ref, bcc, *refs):
    krows = refs[:nch]
    out, xw8_ref, x8_ref, b8_ref, c8_ref, flag_ref = refs[nch:]
    wc = out.shape[1]
    tile = recv[STATE:, :].astype(f32)
    tile0, tile1 = tile[0:8], tile[8:16, 0:STATE]
    seg = seg_ref[:, 0:SPAN].astype(f32)
    seg_first = seg[:, 0:1]
    lane = iota((1, SPAN), 1)
    drop = jnp.sum(
        jnp.where((lane < KERNEL - 1) & (seg == seg_first), 1.0, 0.0), axis=1, keepdims=True
    )
    joined = jnp.where(tile0[0:1, 0:1] == seg_first + 1.0, 1.0, 0.0)
    flag = joined * jnp.where(lax.axis_index("seq") == 0, 0.0, 1.0)
    flag_ref[...] = jnp.broadcast_to(flag, (8, 128))

    def lower(value):
        return jnp.where(iota(value.shape, 0) >= 8 - (KERNEL - 1), value, 0.0) * flag

    def early(value):
        return jnp.where(iota(value.shape, 0).astype(f32) < drop, value, 0.0)

    zero8 = lambda n: jnp.zeros((8, n), f32)
    halo = [lower(tile0)]
    if nch == 2:
        halo.append(lower(pltpu.roll(tile0, 4, 0)))
    bc8 = early_conv(
        jnp.concatenate([lower(tile1), lower(pltpu.roll(tile1, 4, 0))], 1), bchead[...], taps_bc[...] * 0.5
    )
    b8 = jnp.concatenate([early(bc8[:, 0:STATE]), zero8(STATE)], 0).astype(bf16)
    b8_ref[...] = b8
    old = bcc[0:TAIL, STATE:].astype(f32)
    c8 = jnp.where(iota((8, STATE), 0).astype(f32) < drop, bc8[:, STATE:], old[0:8])
    c8_ref[...] = jnp.concatenate([c8, old[8:16]], 0).astype(bf16)
    for c in range(nch):
        cs = slice(c * wc, (c + 1) * wc)
        x8 = early(early_conv(halo[c], xhead[:, cs], tapx[:, cs] * 0.5)).astype(bf16).astype(f32)
        kr = krows[c][...]
        x8_ref[:, cs] = x8 * kr[11:12]
        xw8 = jnp.concatenate([x8 * kr[8:16], zero8(wc)], 0).astype(bf16)
        xw8_ref[:, cs] = xw8
        if c == 0:
            out[...] = relay_state(kr, recv[0:STATE, :], b8, xw8, flag)


def relay_next(recv, krows, b8, xw8, flag, out):
    wc = out.shape[1]
    out[...] = relay_state(krows[...], recv[...], b8[...], xw8[:, wc:], flag[0:1, 0:1])


def local_kernel(hp, first, z_any, xc, lstate, krows, bcc, bt, rows, seg_ref, order, a_ref, q_ref, sz8, zbuf, sem):
    tokens, wc = zbuf.shape
    nb = tokens // SPAN
    lane0 = first * HEAD_DIM
    copy = pltpu.make_async_copy(z_any.at[:, lane0 : lane0 + wc], zbuf, sem)
    copy.start()
    seg = seg_ref[...].astype(f32)
    ex = expander(hp, 2, wc, first)
    r128 = iota((128, SPAN), 0)
    head_of = r128 & (hp - 1)
    low = iota((SPAN, 128), 1) < HEAD_DIM
    tri = iota((SPAN, SPAN), 0) >= iota((SPAN, SPAN), 1)
    waited = False
    for b in range(nb):
        segcol = to_column(seg[:, blk(b)])
        mask = (segcol == seg[:, blk(b)]) & tri
        c_blk = bcc[blk(b), STATE:]
        scores = jnp.where(mask, mm(c_blk, bt[:, blk(b)]), 0.0)
        cum = split(rows[0:hp, blk(b)], 3)
        neg_q = split(-rows[4 * hp : 5 * hp, blk(b)], 3)
        ones = jnp.ones((3 * hp, SPAN), bf16)
        pad = jnp.zeros((128 - 6 * hp, SPAN), bf16)
        left = jnp.concatenate([cum, ones, pad], 0).T
        right = jnp.concatenate([ones, neg_q, pad], 0).astype(f32)
        f_exp = mm(split(rows[hp : 2 * hp, blk(b)], 2), ex, 0, 0)
        if b > 0:
            e_exp = mm(split(rows[2 * hp : 3 * hp, blk(b)], 2), ex, 0, 0)
            carry = mm(
                jnp.concatenate([c_blk, c_blk], 1), lstate[2 * SPAN * (b - 1) : 2 * SPAN * b, :]
            )
        if not waited:
            copy.wait()
            waited = True
        for j in range(wc // 128):
            js = slice(j * 128, (j + 1) * 128)
            xj = xc[blk(b), js]
            w = []
            for i in range(2):
                h = first + 2 * j + i
                sel = jnp.where(head_of == h, right, 0.0).astype(bf16)
                w.append((scores * jnp.exp2(jnp.minimum(mm(left, sel), 8.0))).astype(bf16))
            zero = jnp.zeros_like(xj)
            pair = jnp.concatenate([jnp.where(low, xj, zero), jnp.where(low, zero, xj)], 0)
            y = mm(jnp.concatenate(w, 1), pair) + xj.astype(f32) * krows[11:12, js]
            if b > 0:
                y = y + e_exp[:, js] * carry[:, js]
            sz = silu_from_half(zbuf[blk(b), js].astype(f32) * 0.5)
            a_ref[blk(b), js] = y * sz
            q_ref[blk(b), js] = f_exp[:, js] * sz
            if b == 0:
                sz8[:, js] = sz[0:8]


def rank_kernel(bcc, b8, c8, cg):
    tokens = bcc.shape[0]
    b_pad = jnp.concatenate([b8[...], jnp.zeros((128 - TAIL, STATE), bf16)], 0)
    cg[:, 0:STATE] = bcc[:, STATE:]
    cg[0:TAIL, 0:STATE] = c8[...]
    c = cg[:, 0:STATE]
    cg[:, STATE : 2 * STATE] = c
    g = mm(c, b_pad, 1, 1)
    cg[:, 2 * STATE :] = jnp.where(
        iota((tokens, 128), 0) >= iota((tokens, 128), 1), g, 0.0
    ).astype(bf16)


def gate_kernel(nrecv, chunk, cg, xw8, x8, flag, a_ref, q_ref, sz8, prev, *refs):
    recvs, (gated, sums) = refs[:nrecv], refs[nrecv:]
    tokens, wc = a_ref.shape
    lanes = slice(chunk * wc, (chunk + 1) * wc)
    total = recvs[0][0:STATE, :].astype(f32)
    for r in recvs[1:]:
        total = total + r[0:STATE, :].astype(f32)
    total = total * flag[0:1, 0:1]
    hi = total.astype(bf16)
    lo = (total - hi.astype(f32)).astype(bf16)
    both = jnp.concatenate([hi, lo], 0)
    small = jnp.concatenate([xw8[:, lanes], jnp.zeros((128 - TAIL, wc), bf16)], 0)
    ones = jnp.ones((16, 128), bf16)
    for b in range(tokens // SPAN):
        p = mm(cg[blk(b), 0 : 2 * STATE], both) + mm(cg[blk(b), 2 * STATE :], small)
        g = a_ref[blk(b), :] + q_ref[blk(b), :] * p
        if b == 0:
            top = g[0:8] + x8[:, lanes] * sz8[...]
            g = jnp.concatenate([top, g[8:]], 0)
        gated[blk(b), :] = g
        sq = g * g
        acc = sq[:, 0:128]
        for j in range(1, wc // 128):
            acc = acc + sq[:, j * 128 : (j + 1) * 128]
        acc3 = split(acc, 3)
        s = mm(ones, acc3, 1, 1)
        s = s[0:1, 0:SPAN] + s[0:1, SPAN : 2 * SPAN] + s[0:1, 2 * SPAN :]
        sums[:, blk(b)] = s + prev[:, blk(b)]


def norm_kernel(nch, sums, gain, *refs):
    gated, out = refs[:nch], refs[nch]
    wc = gated[0].shape[1]
    b = pl.program_id(0)
    row = pl.ds(pl.multiple_of(b * SPAN, SPAN), SPAN)
    total = jnp.sum(sums[...], axis=0, keepdims=True)
    scale = lax.rsqrt(total / (HEADS * HEAD_DIM) + 1e-05)
    wide = jnp.where(iota((16, SPAN), 0) == 0, scale, 0.0)
    col = mm(split(wide, 3), jnp.ones((48, 128), bf16), 0, 0)
    for c in range(nch):
        for j in range(wc // 128):
            js = slice(j * 128, (j + 1) * 128)
            at = slice(c * wc + j * 128, c * wc + (j + 1) * 128)
            out[:, at] = (gated[c][row, js] * col * gain[:, at]).astype(bf16)


VMEM = pl.BlockSpec(memory_space=pltpu.VMEM)
ANY = pl.BlockSpec(memory_space=pl.ANY)


def call(body, ins, outs, scratch=(), name=None, limit=24 << 20):
    return pl.pallas_call(
        body,
        out_shape=[pltpu.VMEM(shape, dtype) for shape, dtype in outs],
        in_specs=ins,
        out_specs=[VMEM] * len(outs),
        scratch_shapes=list(scratch),
        compiler_params=pltpu.CompilerParams(vmem_limit_bytes=limit),
        name=name,
    )


def per_device(x_in, z_in, bc_in, conv_x, conv_bc, dt, a_log, skip_d, norm_gain, seg_ids):
    tokens, width = x_in.shape
    heads = dt.shape[0]
    nb = tokens // SPAN
    hp = max(16, heads)
    peers = lax.axis_size("seq")
    rounds = max(1, peers // 2)
    nch = 2 if width % 512 == 0 else 1
    wc = width // nch
    per_chunk = heads // nch
    ring = [(i, (i + 1) % peers) for i in range(peers)]
    if hp != heads:
        dt = jnp.pad(dt, ((0, hp - heads), (0, 0)))
        a_log = jnp.pad(a_log, (0, hp - heads))
        skip_d = jnp.pad(skip_d, (0, hp - heads))
    seg = seg_ids.reshape(1, tokens)
    alog, skip = a_log.reshape(1, hp), skip_d.reshape(1, hp)
    state_outs = [((tokens, wc), bf16), ((2 * SPAN * (nb - 1), wc), bf16), ((16, wc), f32)]
    dma = pltpu.SemaphoreType.DMA
    first = call(
        functools.partial(first_kernel, heads, hp, nch),
        [ANY, ANY, ANY] + [VMEM] * 5,
        [((STATE + TAIL, wc), bf16)] + state_outs
        + [
            ((tokens, 2 * STATE), bf16),
            ((STATE, tokens), bf16),
            ((5 * hp, tokens), f32),
            ((hp, 128), f32),
            ((3 * tokens, 2 * SPAN), bf16),
            ((TAIL, width), bf16),
            ((TAIL, 2 * STATE), bf16),
            ((KERNEL, 2 * STATE), f32),
        ],
        [
            pltpu.VMEM((tokens, wc), bf16),
            pltpu.VMEM((tokens, 2 * STATE), bf16),
            pltpu.VMEM((TAIL, width), bf16),
            dma((7,)),
        ],
        name="first",
    )
    msg, xc, ls, kr, bcc, bt, rows, kcols, shift, xhead, bchead, taps_bc = first(
        x_in, bc_in, conv_bc, conv_x, dt, alog, skip, seg
    )
    xcs, lss, krs, msgs = [xc], [ls], [kr], [msg]
    recv1 = [lax.ppermute(msg, "seq", ring)]
    if nch == 2:
        msg, xc, ls, kr = call(
            functools.partial(next_kernel, hp, per_chunk),
            [ANY] + [VMEM] * 5,
            [((STATE, wc), bf16)] + state_outs,
            [pltpu.VMEM((tokens, wc), bf16), dma],
            name="next",
        )(x_in, conv_x, shift, bt, rows, kcols)
        xcs.append(xc)
        lss.append(ls)
        krs.append(kr)
        recv1.append(lax.ppermute(msg, "seq", ring))
    relay, xw8, x8, b8, c8, flag = call(
        functools.partial(relay_first, nch),
        [VMEM] * (7 + nch),
        [
            ((STATE, wc), bf16),
            ((TAIL, width), bf16),
            ((8, width), f32),
            ((TAIL, STATE), bf16),
            ((TAIL, STATE), bf16),
            ((8, 128), f32),
        ],
        name="relay_first",
    )(recv1[0], xhead, bchead, conv_x, taps_bc, seg, bcc, *krs)
    recvs = [[recv1[c]] for c in range(nch)]
    relays = [relay]
    if rounds > 1:
        recvs[0].append(lax.ppermute(relay, "seq", ring))
    if nch == 2:
        (relay,) = call(relay_next, [VMEM] * 5, [((STATE, wc), bf16)], name="relay_next")(
            recv1[1], krs[1], b8, xw8, flag
        )
        relays.append(relay)
        if rounds > 1:
            recvs[1].append(lax.ppermute(relay, "seq", ring))
    for _ in range(2, rounds):
        for c in range(nch):
            again = recvs[c][-1].astype(f32) * (krs[c][0:1] * flag[0:1, 0:1])
            recvs[c].append(lax.ppermute(again.astype(bf16), "seq", ring))
    local = []
    for c in range(nch):
        local.append(
            call(
                functools.partial(local_kernel, hp, c * per_chunk),
                [ANY] + [VMEM] * 7 + [ANY],
                [((tokens, wc), f32), ((tokens, wc), f32), ((8, wc), f32)],
                [pltpu.VMEM((tokens, wc), bf16), dma],
                name=f"local{c}",
            )(z_in, xcs[c], lss[c], krs[c], bcc, bt, rows, seg, msgs[0] if c == 0 else relays[-1])
        )
    (cg,) = call(rank_kernel, [VMEM] * 3, [((tokens, 3 * STATE), bf16)], name="rank")(bcc, b8, c8)
    sums = jnp.zeros((1, tokens), f32)
    gated = []
    for c in range(nch):
        n = len(recvs[c])
        g, sums = call(
            functools.partial(gate_kernel, n, c),
            [VMEM] * (8 + n),
            [((tokens, wc), f32), ((1, tokens), f32)],
            name=f"gate{c}",
        )(cg, xw8, x8, flag, *local[c], sums, *recvs[c])
        gated.append(g)
    gathered = lax.all_gather(sums, "head", axis=0, tiled=True)
    out = pl.pallas_call(
        functools.partial(norm_kernel, nch),
        grid=(nb,),
        out_shape=jax.ShapeDtypeStruct((tokens, width), bf16),
        in_specs=[
            pl.BlockSpec((gathered.shape[0], SPAN), lambda i: (0, i)),
            pl.BlockSpec((1, width), lambda i: (0, 0)),
        ]
        + [VMEM] * nch,
        out_specs=pl.BlockSpec((SPAN, width), lambda i: (i, 0)),
        compiler_params=pltpu.CompilerParams(vmem_limit_bytes=24 << 20),
        name="norm",
    )(gathered, norm_gain.reshape(1, width), *gated)
    return out


def solution(mesh):
    in_specs = (
        P("seq", "head"),
        P("seq", "head"),
        P("seq", None),
        P(None, "head"),
        P(),
        P("head", "seq"),
        P("head"),
        P("head"),
        P("head"),
        P("seq"),
    )
    return jax.shard_map(
        per_device, mesh=mesh, in_specs=in_specs, out_specs=P("seq", "head"), check_vma=False
    )
```

time: 97.6 us -> 42.8 us (0.44)
  other arithmetic: 17.8 us -> 0 us
  Pallas kernels: 0 us -> 15 us
  between operations: 15.1 us -> 0.1 us
  matrix products: 9.94 us -> 0 us
  blocking collectives: 18.5 us -> 8.92 us
  local copies, waits for them, and re-layouts: 15.1 us -> 7.06 us
  starting transfers between devices: 12 us -> 5.31 us
  waiting for transfers between devices: 8.49 us -> 5.92 us
    pallas_call x0 -> x10, Pallas kernels: none -> 15 us  [the longest x2 3.82 us: per_device(): call(functools.partial(local_kernel, hp, c * per_chunk), [ANY] + [VMEM] *...]
    dot_general x4 -> x0, matrix products: 9.94 us -> none  [the longest x1 4.94 us: per_device(): jnp.einsum('ctn,chpn->cthp', c_blocks.astype(jnp.float32), starts, precis...]
    unnamed x1 -> x0, blocking collectives: 9.67 us -> none
    all_gather x1 -> x0, waiting for transfers between devices: 8.46 us -> none  [carried_in(): lax.all_gather(part.astype(kind), axis)]
    convert_element_type x11 -> x0, other arithmetic: 6.65 us -> none  [the longest x2 3.28 us: conv_silu(): return jax.nn.silu(total).astype(jnp.bfloat16)]
    ppermute x3 -> x4, starting transfers between devices: 11.9 us -> 5.31 us  [the longest x1 3.1 us: per_device(): recv1 = [lax.ppermute(msg, 'seq', ring)]]
    ppermute x3 -> x4, waiting for transfers between devices: 0.01 us -> 5.92 us  [the longest x1 3.03 us: per_device(): recv1.append(lax.ppermute(msg, 'seq', ring))]
    select_n x4 -> x0, other arithmetic: 4.36 us -> none  [hop(): return jax.tree.map(lambda a, b: jnp.where(reached, a, b), new, before)]
  transfers between devices with their start and end apart: 4 -> 4, of which waited for: 1 -> 3; matrix products, arithmetic and copies ran while one was open for 16% -> 0% of each run, Pallas kernels for 0% -> 19%
where the time goes in v1:
time: 42.8 us; the launch traced here: 42.3 us
  Pallas kernels  15 us (35%)
  blocking collectives  8.92 us (21%)
  local copies, waits for them, and re-layouts  7.06 us (16%)
  waiting for transfers between devices  5.92 us (14%)
  starting transfers between devices  5.31 us (12%)
    all_gather x1, blocking collectives, per_device(): gathered = lax.all_gather(sums, 'head', axis=0, tiled=True)  8.92 us
    unnamed x25, local copies, waits for them, and re-layouts  7.06 us
    pallas_call x2, Pallas kernels, per_device(): call(functools.partial(local_kernel, hp, c * per_chunk), [ANY] + [VMEM] *...  3.82 us
    pallas_call x1, Pallas kernels, per_device(): first(x_in, bc_in, conv_bc, conv_x, dt, alog, skip, seg)  3.57 us
    ppermute x1, starting transfers between devices, per_device(): recv1 = [lax.ppermute(msg, 'seq', ring)]  3.1 us
    ppermute x1, waiting for transfers between devices, per_device(): recv1.append(lax.ppermute(msg, 'seq', ring))  3.03 us
    pallas_call x1, Pallas kernels, per_device(): call(functools.partial(next_kernel, hp, per_chunk), [ANY] + [VMEM] * 5, [...  2.51 us
    pallas_call x1, Pallas kernels, per_device(): pl.pallas_call(functools.partial(norm_kernel, nch), grid=(nb,), out_shape...  2.19 us
  transfers between devices with their start and end apart: 4, of which 3 were waited for; matrix products, arithmetic and copies ran while one was open for 0% of the time, Pallas kernels for 19%

profile of v1, /device:TPU:0, one launch (start us, length us, event | category | flops | bytes accessed | tf_op | source)
XLA Modules:
  0.0 42.3 jit_solution(14546632001230963137)
XLA Ops:
  0.0 1.2 %copy-done = bf16[512,1024]{1,0:T(8,128)(2,1)S(1)} copy-done((bf16[512,1024]{1,0:T(8,128)(2,1)S(1)}, bf16[512,1024]{1,0:T(8,128)(2,1)}, u32[]{:S(2)}) %copy-start) | copy-done | bytes 1048600
  1.2 1.6 %copy-done.2 = bf16[512,2048]{1,0:T(8,128)(2,1)S(1)} copy-done((bf16[512,2048]{1,0:T(8,128)(2,1)S(1)}, bf16[512,2048]{1,0:T(8,128)(2,1)}, u32[]{:S(2)}) %copy-start.2) | copy-done | bytes 2097176
  2.8 0.7 %copy-done.3 = f32[4,1024]{1,0:T(4,128)S(1)} copy-done((f32[4,1024]{1,0:T(4,128)S(1)}, f32[4,1024]{1,0:T(4,128)}, u32[]{:S(2)}) %copy-start.3) | copy-done | bytes 16408
  3.5 0.8 %copy-done.5 = f32[4,2048]{1,0:T(4,128)S(1)} copy-done((f32[4,2048]{1,0:T(4,128)S(1)}, f32[4,2048]{1,0:T(4,128)}, u32[]{:S(2)}) %copy-start.5) | copy-done | bytes 32792
  4.3 0.8 %copy-done.6 = f32[16,512]{1,0:T(8,128)S(1)} copy-done((f32[16,512]{1,0:T(8,128)S(1)}, f32[16,512]{1,0:T(8,128)}, u32[]{:S(2)}) %copy-start.6) | copy-done | bytes 32792
  5.1 0.7 %copy-done.7 = s32[512]{0:T(512)S(1)} copy-done((s32[512]{0:T(512)S(1)}, s32[512]{0:T(512)}, u32[]{:S(2)}) %copy-start.7) | copy-done | bytes 2072
  5.7 0.7 %copy-done.10 = f32[16]{0:T(128)S(1)} copy-done((f32[16]{0:T(128)S(1)}, f32[16]{0:T(128)}, u32[]{:S(2)}) %copy-start.10) | copy-done | bytes 88
  6.4 0.7 %copy-done.11 = f32[16]{0:T(128)S(1)} copy-done((f32[16]{0:T(128)S(1)}, f32[16]{0:T(128)}, u32[]{:S(2)}) %copy-start.11) | copy-done | bytes 88
  7.0 3.6 %first.1 = (bf16[144,512]{1,0:T(8,128)(2,1)S(1)}, bf16[512,512]{1,0:T(8,128)(2,1)S(1)}, bf16[768,512]{1,0:T(8,128)(2,1)S(1)}, f32[16,512]{1,0:T(8,128)S(1)}, bf1...) custom-call(bf16[512,1024]{1,0:T(8,128)(2,1)S(1)} %copy-done, ...), custom_call_target="tpu_custom_call" | custom-call | tf_op jit(solution)/shard_map/first/pallas_call | solution.py:453
  10.6 3.1 %collective-permute-start = (bf16[144,512]{1,0:T(8,128)(2,1)S(1)}, bf16[144,512]{1,0:T(8,128)(2,1)S(1)}, u32[]{:S(2)}, u32[]{:S(2)}) collective-permute-start(bf16[144,512]{1,0:T(8,128)(2,1)S(1)} %get-tuple-element.38.order), channel_id=1, source_target_pairs={{0,8},{8,16},{16,24},{24,0},{1,9},{9,17},{17,25},{25,1},{2,10},{10... | collective-permute-start | bytes 442376 | tf_op jit(solution)/shard_map/ppermute | solution.py:457
  13.7 2.5 %next.1 = (bf16[128,512]{1,0:T(8,128)(2,1)S(1)}, bf16[512,512]{1,0:T(8,128)(2,1)S(1)}, bf16[768,512]{1,0:T(8,128)(2,1)S(1)}, f32[16,512]{1,0:T(8,128)S(1)}) custom-call(bf16[512,1024]{1,0:T(8,128)(2,1)S(1)} %copy-done, f32[4,1024]{1,0:T(4,128)S(1)} %copy-done.4, bf16[1536,256]{1,0:T(8,128)(2,1)S(1)} %get-tuple-element.43.shift, ...), custom_call_target="tpu_custom_call" | custom-call | tf_op jit(solution)/shard_map/next/pallas_call | solution.py:459
  16.3 1.6 %collective-permute-start.1 = (bf16[128,512]{1,0:T(8,128)(2,1)S(1)}, bf16[128,512]{1,0:T(8,128)(2,1)S(1)}, u32[]{:S(2)}, u32[]{:S(2)}) collective-permute-start(bf16[128,512]{1,0:T(8,128)(2,1)S(1)} %get-tuple-element.55), channel_id=1, source_target_pairs={{0,8},{8,16},{16,24},{24,0},{1,9},{9,17},{17,25},{25,1},{2,10},{10... | collective-permute-start | bytes 393224 | tf_op jit(solution)/shard_map/ppermute | solution.py:469
  17.9 1.7 %collective-permute-done.recv.refs_0_ = bf16[144,512]{1,0:T(8,128)(2,1)S(1)} collective-permute-done((bf16[144,512]{1,0:T(8,128)(2,1)S(1)}, bf16[144,512]{1,0:T(8,128)(2,1)S(1)}, u32[]{:S(2)}, u32[]{:S(2)}) %collective-permute-start) | collective-permute-done | bytes 147488 | tf_op jit(solution)/shard_map/ppermute | solution.py:457
  19.6 0.4 relay_first.1
  20.1 3.0 %collective-permute-done.1.recv.refs_0_ = bf16[128,512]{1,0:T(8,128)(2,1)S(1)} collective-permute-done((bf16[128,512]{1,0:T(8,128)(2,1)S(1)}, bf16[128,512]{1,0:T(8,128)(2,1)S(1)}, u32[]{:S(2)}, u32[]{:S(2)}) %collective-permute-start.1) | collective-permute-done | bytes 131104 | tf_op jit(solution)/shard_map/ppermute | solution.py:469
  23.1 0.2 relay_next.1.order
  23.3 0.5 %collective-permute-start.3 = (bf16[128,512]{1,0:T(8,128)(2,1)S(1)}, bf16[128,512]{1,0:T(8,128)(2,1)S(1)}, u32[]{:S(2)}, u32[]{:S(2)}) collective-permute-start(bf16[128,512]{1,0:T(8,128)(2,1)S(1)} %relay_next.1.order), channel_id=1, source_target_pairs={{0,8},{8,16},{16,24},{24,0},{1,9},{9,17},{17,25},{25,1},{2,10},{10... | collective-permute-start | bytes 393224 | tf_op jit(solution)/shard_map/ppermute | solution.py:493
  23.8 1.9 %local0.1 = (f32[512,512]{1,0:T(8,128)S(1)}, f32[512,512]{1,0:T(8,128)S(1)}, f32[8,512]{1,0:T(8,128)S(1)}) custom-call(bf16[512,1024]{1,0:T(8,128)(2,1)S(1)} %copy-done.1, bf16[512,512]{1,0:T(8,128)(2,1)S(1)} %get-tuple-element.59.xc, bf16[768,512]{1,0:T(8,128)(2,1)S(1)} %get-tuple-element.60.lstate, f32[16,512]{1,0:T(8,128)S(1)} %get-tuple-element.42.refs_0_.krows, ...), custom_call_target="tpu_custom_call" | custom-call | tf_op jit(solution)/shard_map/local0/pallas_call | solution.py:501
  25.9 1.9 %local1.1 = (f32[512,512]{1,0:T(8,128)S(1)}, f32[512,512]{1,0:T(8,128)S(1)}, f32[8,512]{1,0:T(8,128)S(1)}) custom-call(bf16[512,1024]{1,0:T(8,128)(2,1)S(1)} %copy-done.1, bf16[512,512]{1,0:T(8,128)(2,1)S(1)} %get-tuple-element.53.xc, bf16[768,512]{1,0:T(8,128)(2,1)S(1)} %get-tuple-element.54.lstate, f32[16,512]{1,0:T(8,128)S(1)} %get-tuple-element.47.refs_1_.krows, ...), custom_call_target="tpu_custom_call" | custom-call | tf_op jit(solution)/shard_map/local1/pallas_call | solution.py:501
  27.9 1.1 %gate0.1 = (f32[512,512]{1,0:T(8,128)S(1)}, f32[1,512]{1,0:T(1,128)S(1)}) custom-call(bf16[512,384]{1,0:T(8,128)(2,1)S(1)} %rank.1.cg, bf16[16,1024]{1,0:T(8,128)(2,1)S(1)} %get-tuple-element.50.xw8, f32[8,1024]{1,0:T(8,128)S(1)} %get-tuple-element.51.x8, f32[8,128]{1,0:T(8,128)S(1)} %get-tuple-element.52.flag, f32[512,512]{1,0:T(8,128)S(1)} %get-tuple-element.61.a_ref, ...), custom_call_target="tpu_custom_call" | custom-call | tf_op jit(solution)/shard_map/gate0/pallas_call | solution.py:514
  29.0 1.2 %collective-permute-done.3.refs_1_ = bf16[128,512]{1,0:T(8,128)(2,1)S(1)} collective-permute-done((bf16[128,512]{1,0:T(8,128)(2,1)S(1)}, bf16[128,512]{1,0:T(8,128)(2,1)S(1)}, u32[]{:S(2)}, u32[]{:S(2)}) %collective-permute-start.3) | collective-permute-done | bytes 131104 | tf_op jit(solution)/shard_map/ppermute | solution.py:493
  30.1 1.1 %gate1.1 = (f32[512,512]{1,0:T(8,128)S(1)}, f32[1,512]{1,0:T(1,128)S(1)}) custom-call(bf16[512,384]{1,0:T(8,128)(2,1)S(1)} %rank.1.cg, bf16[16,1024]{1,0:T(8,128)(2,1)S(1)} %get-tuple-element.50.xw8, f32[8,1024]{1,0:T(8,128)S(1)} %get-tuple-element.51.x8, f32[8,128]{1,0:T(8,128)S(1)} %get-tuple-element.52.flag, f32[512,512]{1,0:T(8,128)S(1)} %get-tuple-element.56.a_ref, ...), custom_call_target="tpu_custom_call" | custom-call | tf_op jit(solution)/shard_map/gate1/pallas_call | solution.py:514
  31.2 8.9 %all-gather = f32[8,1,512]{2,1,0:T(1,128)S(1)} all-gather(f32[1,1,512]{2,1,0:T(1,128)S(1)} %bitcast.14), channel_id=1, replica_groups=mesh['seq'=4,'head'=8] {'head'}, dimensions={0}, use_global_device_ids=true | all-gather | bytes 18432 | tf_op jit(solution)/shard_map/all_gather | solution.py:521
  40.1 2.2 %norm.1 = bf16[512,1024]{1,0:T(8,128)(2,1)} custom-call(f32[8,512]{1,0:T(8,128)S(1)} %bitcast.8, f32[1,1024]{1,0:T(1,128)S(1)} %bitcast.13, f32[512,512]{1,0:T(8,128)S(1)} %get-tuple-element.67.refs_0_, f32[512,512]{1,0:T(8,128)S(1)} %get-tuple-element.68.refs_1_), custom_call_target="tpu_custom_call" | custom-call | tf_op jit(solution)/shard_map/norm/pallas_call | solution.py:522
  (21 shorter events, 0.3 us)
Async XLA Ops:
  0.0 1.2 %copy-start = (bf16[512,1024]{1,0:T(8,128)(2,1)S(1)}, bf16[512,1024]{1,0:T(8,128)(2,1)}, u32[]{:S(2)}) copy-start(bf16[512,1024]{1,0:T(8,128)(2,1)} %x_any.3) | copy-start | bytes 3145732
  1.2 1.6 %copy-start.2 = (bf16[512,2048]{1,0:T(8,128)(2,1)S(1)}, bf16[512,2048]{1,0:T(8,128)(2,1)}, u32[]{:S(2)}) copy-start(bf16[512,2048]{1,0:T(8,128)(2,1)} %bc_any.1) | copy-start | bytes 6291460
  2.8 0.7 %copy-start.3 = (f32[4,1024]{1,0:T(4,128)S(1)}, f32[4,1024]{1,0:T(4,128)}, u32[]{:S(2)}) copy-start(f32[4,1024]{1,0:T(4,128)} %tapx.5) | copy-start | bytes 49156
  3.5 0.8 %copy-start.5 = (f32[4,2048]{1,0:T(4,128)S(1)}, f32[4,2048]{1,0:T(4,128)}, u32[]{:S(2)}) copy-start(f32[4,2048]{1,0:T(4,128)} %tapbc_any.1) | copy-start | bytes 98308
  4.3 0.8 %copy-start.6 = (f32[16,512]{1,0:T(8,128)S(1)}, f32[16,512]{1,0:T(8,128)}, u32[]{:S(2)}) copy-start(f32[16,512]{1,0:T(8,128)} %dt_ref.1) | copy-start | bytes 98308
  5.1 0.7 %copy-start.7 = (s32[512]{0:T(512)S(1)}, s32[512]{0:T(512)}, u32[]{:S(2)}) copy-start(s32[512]{0:T(512)} %param.19) | copy-start | bytes 6148
  5.7 0.7 %copy-start.10 = (f32[16]{0:T(128)S(1)}, f32[16]{0:T(128)}, u32[]{:S(2)}) copy-start(f32[16]{0:T(128)} %param.16) | copy-start | bytes 196
  6.4 0.7 %copy-start.11 = (f32[16]{0:T(128)S(1)}, f32[16]{0:T(128)}, u32[]{:S(2)}) copy-start(f32[16]{0:T(128)} %param.17) | copy-start | bytes 196
  7.0 6.7 %copy-start.4 = (f32[4,1024]{1,0:T(4,128)S(1)}, f32[4,1024]{1,0:T(4,128)}, u32[]{:S(2)}) copy-start(f32[4,1024]{1,0:T(4,128)} %tapx.5) | copy-start | bytes 49156
  7.0 12.6 %copy-start.8 = (s32[512]{0:T(512)S(1)}, s32[512]{0:T(512)}, u32[]{:S(2)}) copy-start(s32[512]{0:T(512)} %param.19) | copy-start | bytes 6148
  10.6 13.2 %copy-start.1 = (bf16[512,1024]{1,0:T(8,128)(2,1)S(1)}, bf16[512,1024]{1,0:T(8,128)(2,1)}, u32[]{:S(2)}) copy-start(bf16[512,1024]{1,0:T(8,128)(2,1)} %z_any.3) | copy-start | bytes 3145732
  10.6 9.0 %collective-permute-start = (bf16[144,512]{1,0:T(8,128)(2,1)S(1)}, bf16[144,512]{1,0:T(8,128)(2,1)S(1)}, u32[]{:S(2)}, u32[]{:S(2)}) collective-permute-start(bf16[144,512]{1,0:T(8,128)(2,1)S(1)} %get-tuple-element.38.order), channel_id=1, source_target_pairs={{0,8},{8,16},{16,24},{24,0},{1,9},{9,17},{17,25},{25,1},{2,10},{10... | collective-permute-start | bytes 442376 | tf_op jit(solution)/shard_map/ppermute | solution.py:457
  16.3 6.8 %collective-permute-start.1 = (bf16[128,512]{1,0:T(8,128)(2,1)S(1)}, bf16[128,512]{1,0:T(8,128)(2,1)S(1)}, u32[]{:S(2)}, u32[]{:S(2)}) collective-permute-start(bf16[128,512]{1,0:T(8,128)(2,1)S(1)} %get-tuple-element.55), channel_id=1, source_target_pairs={{0,8},{8,16},{16,24},{24,0},{1,9},{9,17},{17,25},{25,1},{2,10},{10... | collective-permute-start | bytes 393224 | tf_op jit(solution)/shard_map/ppermute | solution.py:469
  20.0 7.9 %collective-permute-start.2 = (bf16[128,512]{1,0:T(8,128)(2,1)S(1)}, bf16[128,512]{1,0:T(8,128)(2,1)S(1)}, u32[]{:S(2)}, u32[]{:S(2)}) collective-permute-start(bf16[128,512]{1,0:T(8,128)(2,1)S(1)} %get-tuple-element.64), channel_id=1, source_target_pairs={{0,8},{8,16},{16,24},{24,0},{1,9},{9,17},{17,25},{25,1},{2,10},{10... | collective-permute-start | bytes 393224 | tf_op jit(solution)/shard_map/ppermute | solution.py:486
  23.3 6.8 %collective-permute-start.3 = (bf16[128,512]{1,0:T(8,128)(2,1)S(1)}, bf16[128,512]{1,0:T(8,128)(2,1)S(1)}, u32[]{:S(2)}, u32[]{:S(2)}) collective-permute-start(bf16[128,512]{1,0:T(8,128)(2,1)S(1)} %relay_next.1.order), channel_id=1, source_target_pairs={{0,8},{8,16},{16,24},{24,0},{1,9},{9,17},{17,25},{25,1},{2,10},{10... | collective-permute-start | bytes 393224 | tf_op jit(solution)/shard_map/ppermute | solution.py:493
  28.9 11.2 %copy-start.9 = (f32[1024]{0:T(1024)S(1)}, f32[1024]{0:T(1024)}, u32[]{:S(2)}) copy-start(f32[1024]{0:T(1024)} %param.18) | copy-start | bytes 12292

commit v2 on v1

--- a/solution.py
+++ b/solution.py
@@ -15,6 +15,7 @@
 LOG2E = 1.4426950408889634
 TINY = 1e-37
 TAIL = 16
+TILE = 512
 f32 = jnp.float32
 bf16 = jnp.bfloat16
 
@@ -61,7 +62,7 @@
     nb = tokens // SPAN
     kr = mm(split(kcols, 3), expander(hp, 3, wc, first), 0, 0)[:16]
     krows[...] = kr
-    tile = 256 if wc % 256 == 0 else wc
+    tile = min(TILE, wc)
     ex = expander(hp, 2, wc, first)
     for j in range(wc // tile):
         js = slice(j * tile, (j + 1) * tile)
@@ -79,7 +80,9 @@
             half = half + x[blk(b), js].astype(f32) * taps[3:4, js]
             act = silu_from_half(half)
             if b == 0:
-                act = jnp.where(iota(act.shape, 0).astype(f32) < drop, 0.0, act)
+                top = act[0:TAIL]
+                top = jnp.where(iota(top.shape, 0).astype(f32) < drop, 0.0, top)
+                act = jnp.concatenate([top, act[TAIL:]], 0)
             act = act.astype(bf16)
             xc[blk(b), js] = act
             to_end = mm(split(rows[3 * hp : 4 * hp, blk(b)], 2), ex[:, js], 0, 0)
@@ -87,26 +90,26 @@
             fresh = mm(bt[:, blk(b)], weighted)
             state = fresh if b == 0 else state * kr[b : b + 1, js] + fresh
             if b < nb - 1:
-                hi = state.astype(bf16)
-                lstate[2 * SPAN * b : 2 * SPAN * b + SPAN, js] = hi
-                lstate[2 * SPAN * b + SPAN : 2 * SPAN * (b + 1), js] = (
-                    state - hi.astype(f32)
-                ).astype(bf16)
+                lstate[blk(b), js] = state.astype(bf16)
         msg[0:STATE, js] = state.astype(bf16)
 
 
 def first_kernel(
     heads, hp, nch,
-    x_any, bc_any, tapbc_any, tapx, dt_ref, alog_ref, skip_ref, seg_ref,
-    msg, xc, lstate, krows, bcc, bt, rows, kcols, shift, xhead, bchead, taps_bc,
-    xbuf, bcbuf, xtail, sems,
+    x_any, bc_any, tapbc_any, tapx_any, dt_any, alog_any, skip_any, seg_any,
+    msg, xc, lstate, krows, bcc, bt, rows, kcols, shift, xhead, bchead, taps_bc, tapx, seg_ref,
+    *refs,
 ):
+    xnext = refs[: nch - 1]
+    xbuf, bcbuf, xtail, dt_ref, alog_ref, skip_ref, sems = refs[nch - 1 :]
     tokens, wc = xbuf.shape
     nb = tokens // SPAN
     group = lax.axis_index("head") * heads // (HEADS // GROUPS)
     col_b = pl.multiple_of(group * STATE, STATE)
     col_c = pl.multiple_of((group + GROUPS) * STATE, STATE)
     width = nch * wc
+    small = [(dt_any, dt_ref), (alog_any, alog_ref), (skip_any, skip_ref), (seg_any, seg_ref), (tapx_any, tapx)]
+    small = [pltpu.make_async_copy(a, b, sems.at[7 + i]) for i, (a, b) in enumerate(small)]
     copies = [
         pltpu.make_async_copy(bc_any.at[:, pl.ds(col_b, STATE)], bcbuf.at[:, 0:STATE], sems.at[0]),
         pltpu.make_async_copy(bc_any.at[:, pl.ds(col_c, STATE)], bcbuf.at[:, STATE:], sems.at[1]),
@@ -116,8 +119,12 @@
         pltpu.make_async_copy(x_any.at[tokens - TAIL :, :], xtail, sems.at[5]),
         pltpu.make_async_copy(x_any.at[0:TAIL, :], xhead, sems.at[6]),
     ]
-    for copy in copies:
+    if nch == 2:
+        copies.append(pltpu.make_async_copy(x_any.at[:, wc:], xnext[0], sems.at[12]))
+    for copy in small + copies:
         copy.start()
+    for copy in small:
+        copy.wait()
     seg = seg_ref[...].astype(f32)
     seg_first = seg[:, 0:1]
     seg_last = [seg[:, (b + 1) * SPAN - 1 : (b + 1) * SPAN] for b in range(nb)]
@@ -183,11 +190,12 @@
         act = silu_from_half(half).astype(bf16)
         bcc[blk(b), :] = act
         bt[:, blk(b)] = act[:, 0:STATE].T
-    for copy in copies[4:]:
-        copy.wait()
+    copies[4].wait()
     chunk_state(
         hp, 0, xbuf, tapx[:, 0:wc] * 0.5, shift, bt, rows, kc, drop, xc, lstate, krows, msg
     )
+    for copy in copies[5:]:
+        copy.wait()
     lane_last = iota((1, SPAN), 1)
     is_tail = jnp.where((lane_last >= SPAN - (KERNEL - 1)) & (seg[:, blk(nb - 1)] == seg_last[-1]), 1.0, 0.0)
     first_valid = 8.0 - jnp.sum(is_tail, axis=1, keepdims=True)
@@ -207,11 +215,8 @@
     msg[STATE:, :] = jnp.concatenate([tile0, tile1], 0).astype(bf16)
 
 
-def next_kernel(hp, first, x_any, tapx, shift, bt, rows, kcols, msg, xc, lstate, krows, xbuf, sem):
+def next_kernel(hp, first, xbuf, tapx, shift, bt, rows, kcols, msg, xc, lstate, krows):
     wc = xbuf.shape[1]
-    copy = pltpu.make_async_copy(x_any.at[:, wc : 2 * wc], xbuf, sem)
-    copy.start()
-    copy.wait()
     chunk_state(
         hp, first, xbuf, tapx[:, wc : 2 * wc] * 0.5, shift, bt, rows, kcols[...],
         kcols[0:1, 16:17], xc, lstate, krows, msg,
@@ -276,29 +281,40 @@
             out[...] = relay_state(kr, recv[0:STATE, :], b8, xw8, flag)
 
 
-def relay_next(recv, krows, b8, xw8, flag, out):
+def relay_next(recv, krows, b8, xw8, flag, order, out):
     wc = out.shape[1]
     out[...] = relay_state(krows[...], recv[...], b8[...], xw8[:, wc:], flag[0:1, 0:1])
 
 
-def local_kernel(hp, first, z_any, xc, lstate, krows, bcc, bt, rows, seg_ref, order, a_ref, q_ref, sz8, zbuf, sem):
+def local_kernel(
+    hp, first, z_any, xc, lstate, krows, bcc, bt, rows, seg_ref, cg, recv, xw8, x8, flag, order,
+    a_ref, q_ref, zbuf, sem,
+):
     tokens, wc = zbuf.shape
     nb = tokens // SPAN
     lane0 = first * HEAD_DIM
-    copy = pltpu.make_async_copy(z_any.at[:, lane0 : lane0 + wc], zbuf, sem)
+    lanes = slice(lane0, lane0 + wc)
+    copy = pltpu.make_async_copy(z_any.at[:, lanes], zbuf, sem)
     copy.start()
     seg = seg_ref[...].astype(f32)
     ex = expander(hp, 2, wc, first)
-    r128 = iota((128, SPAN), 0)
-    head_of = r128 & (hp - 1)
+    head_of = iota((128, SPAN), 0) & (hp - 1)
     low = iota((SPAN, 128), 1) < HEAD_DIM
     tri = iota((SPAN, SPAN), 0) >= iota((SPAN, SPAN), 1)
-    waited = False
+    entering = jnp.concatenate(
+        [
+            (recv[0:STATE, :].astype(f32) * flag[0:1, 0:1]).astype(bf16),
+            xw8[:, lanes],
+            jnp.zeros((128 - TAIL, wc), bf16),
+        ],
+        0,
+    )
     for b in range(nb):
         segcol = to_column(seg[:, blk(b)])
         mask = (segcol == seg[:, blk(b)]) & tri
         c_blk = bcc[blk(b), STATE:]
         scores = jnp.where(mask, mm(c_blk, bt[:, blk(b)]), 0.0)
+        scores = jnp.concatenate([scores, scores], 1)
         cum = split(rows[0:hp, blk(b)], 3)
         neg_q = split(-rows[4 * hp : 5 * hp, blk(b)], 3)
         ones = jnp.ones((3 * hp, SPAN), bf16)
@@ -306,32 +322,30 @@
         left = jnp.concatenate([cum, ones, pad], 0).T
         right = jnp.concatenate([ones, neg_q, pad], 0).astype(f32)
         f_exp = mm(split(rows[hp : 2 * hp, blk(b)], 2), ex, 0, 0)
+        inflow = mm(cg[blk(b), :], entering)
         if b > 0:
             e_exp = mm(split(rows[2 * hp : 3 * hp, blk(b)], 2), ex, 0, 0)
-            carry = mm(
-                jnp.concatenate([c_blk, c_blk], 1), lstate[2 * SPAN * (b - 1) : 2 * SPAN * b, :]
-            )
-        if not waited:
+            carry = mm(c_blk, lstate[blk(b - 1), :])
+        if b == 0:
             copy.wait()
-            waited = True
         for j in range(wc // 128):
             js = slice(j * 128, (j + 1) * 128)
             xj = xc[blk(b), js]
-            w = []
-            for i in range(2):
-                h = first + 2 * j + i
-                sel = jnp.where(head_of == h, right, 0.0).astype(bf16)
-                w.append((scores * jnp.exp2(jnp.minimum(mm(left, sel), 8.0))).astype(bf16))
+            h = first + 2 * j
+            sel = [jnp.where(head_of == h + i, right, 0.0).astype(bf16) for i in range(2)]
+            decay = jnp.exp2(jnp.minimum(mm(left, jnp.concatenate(sel, 1)), 8.0))
             zero = jnp.zeros_like(xj)
             pair = jnp.concatenate([jnp.where(low, xj, zero), jnp.where(low, zero, xj)], 0)
-            y = mm(jnp.concatenate(w, 1), pair) + xj.astype(f32) * krows[11:12, js]
+            y = mm((scores * decay).astype(bf16), pair) + xj.astype(f32) * krows[11:12, js]
             if b > 0:
                 y = y + e_exp[:, js] * carry[:, js]
+            else:
+                top = y[0:8] + x8[:, lane0 + j * 128 : lane0 + (j + 1) * 128]
+                y = jnp.concatenate([top, y[8:]], 0)
+            f = f_exp[:, js]
             sz = silu_from_half(zbuf[blk(b), js].astype(f32) * 0.5)
-            a_ref[blk(b), js] = y * sz
-            q_ref[blk(b), js] = f_exp[:, js] * sz
-            if b == 0:
-                sz8[:, js] = sz[0:8]
+            a_ref[blk(b), js] = (y + f * inflow[:, js]) * sz
+            q_ref[blk(b), js] = f * sz
 
 
 def rank_kernel(bcc, b8, c8, cg):
@@ -339,58 +353,56 @@
     b_pad = jnp.concatenate([b8[...], jnp.zeros((128 - TAIL, STATE), bf16)], 0)
     cg[:, 0:STATE] = bcc[:, STATE:]
     cg[0:TAIL, 0:STATE] = c8[...]
-    c = cg[:, 0:STATE]
-    cg[:, STATE : 2 * STATE] = c
-    g = mm(c, b_pad, 1, 1)
-    cg[:, 2 * STATE :] = jnp.where(
-        iota((tokens, 128), 0) >= iota((tokens, 128), 1), g, 0.0
-    ).astype(bf16)
-
-
-def gate_kernel(nrecv, chunk, cg, xw8, x8, flag, a_ref, q_ref, sz8, prev, *refs):
+    g = mm(cg[:, 0:STATE], b_pad, 1, 1)
+    causal = iota((tokens, 128), 0) >= iota((tokens, 128), 1)
+    cg[:, STATE:] = jnp.where(causal, g, 0.0).astype(bf16)
+
+
+def gate_kernel(nrecv, cg, flag, a_ref, q_ref, prev, *refs):
     recvs, (gated, sums) = refs[:nrecv], refs[nrecv:]
     tokens, wc = a_ref.shape
-    lanes = slice(chunk * wc, (chunk + 1) * wc)
-    total = recvs[0][0:STATE, :].astype(f32)
-    for r in recvs[1:]:
-        total = total + r[0:STATE, :].astype(f32)
-    total = total * flag[0:1, 0:1]
-    hi = total.astype(bf16)
-    lo = (total - hi.astype(f32)).astype(bf16)
-    both = jnp.concatenate([hi, lo], 0)
-    small = jnp.concatenate([xw8[:, lanes], jnp.zeros((128 - TAIL, wc), bf16)], 0)
-    ones = jnp.ones((16, 128), bf16)
+    if nrecv == 1:
+        total = recvs[0][...]
+    elif nrecv > 1:
+        total = recvs[0][...].astype(f32)
+        for r in recvs[1:]:
+            total = total + r[...].astype(f32)
+        total = total.astype(bf16)
+    tile = min(256, wc)
     for b in range(tokens // SPAN):
-        p = mm(cg[blk(b), 0 : 2 * STATE], both) + mm(cg[blk(b), 2 * STATE :], small)
-        g = a_ref[blk(b), :] + q_ref[blk(b), :] * p
-        if b == 0:
-            top = g[0:8] + x8[:, lanes] * sz8[...]
-            g = jnp.concatenate([top, g[8:]], 0)
-        gated[blk(b), :] = g
-        sq = g * g
-        acc = sq[:, 0:128]
-        for j in range(1, wc // 128):
-            acc = acc + sq[:, j * 128 : (j + 1) * 128]
-        acc3 = split(acc, 3)
-        s = mm(ones, acc3, 1, 1)
-        s = s[0:1, 0:SPAN] + s[0:1, SPAN : 2 * SPAN] + s[0:1, 2 * SPAN :]
-        sums[:, blk(b)] = s + prev[:, blk(b)]
+        acc = None
+        for j in range(wc // tile):
+            js = slice(j * tile, (j + 1) * tile)
+            g = a_ref[blk(b), js]
+            if nrecv:
+                g = g + (q_ref[blk(b), js] * flag[0:1, 0:1]) * mm(cg[blk(b), 0:STATE], total[:, js])
+            gated[blk(b), js] = g
+            sq = g * g
+            for i in range(tile // 128):
+                part = sq[:, i * 128 : (i + 1) * 128]
+                acc = part if acc is None else acc + part
+        sums[:, blk(b)] = prev[:, blk(b)] + jnp.sum(acc.T, axis=0, keepdims=True)
 
 
 def norm_kernel(nch, sums, gain, *refs):
-    gated, out = refs[:nch], refs[nch]
-    wc = gated[0].shape[1]
-    b = pl.program_id(0)
-    row = pl.ds(pl.multiple_of(b * SPAN, SPAN), SPAN)
-    total = jnp.sum(sums[...], axis=0, keepdims=True)
-    scale = lax.rsqrt(total / (HEADS * HEAD_DIM) + 1e-05)
-    wide = jnp.where(iota((16, SPAN), 0) == 0, scale, 0.0)
-    col = mm(split(wide, 3), jnp.ones((48, 128), bf16), 0, 0)
-    for c in range(nch):
-        for j in range(wc // 128):
-            js = slice(j * 128, (j + 1) * 128)
-            at = slice(c * wc + j * 128, c * wc + (j + 1) * 128)
-            out[:, at] = (gated[c][row, js] * col * gain[:, at]).astype(bf16)
+    gated, (out, buf, sems) = refs[:nch], refs[nch:]
+    tokens, wc = gated[0].shape
+    scale = lax.rsqrt(sums[...] / (HEADS * HEAD_DIM) + 1e-05)
+    ones = jnp.ones((48, 128), bf16)
+    copies = []
+    for b in range(tokens // SPAN):
+        wide = jnp.where(iota((16, SPAN), 0) == 0, scale[:, blk(b)], 0.0)
+        col = mm(split(wide, 3), ones, 0, 0)
+        for c in range(nch):
+            for j in range(wc // 128):
+                js = slice(j * 128, (j + 1) * 128)
+                at = slice(c * wc + j * 128, c * wc + (j + 1) * 128)
+                buf[blk(b), at] = (gated[c][blk(b), js] * col * gain[:, at]).astype(bf16)
+        copy = pltpu.make_async_copy(buf.at[blk(b), :], out.at[blk(b), :], sems.at[b])
+        copy.start()
+        copies.append(copy)
+    for copy in copies:
+        copy.wait()
 
 
 VMEM = pl.BlockSpec(memory_space=pltpu.VMEM)
@@ -426,11 +438,12 @@
         skip_d = jnp.pad(skip_d, (0, hp - heads))
     seg = seg_ids.reshape(1, tokens)
     alog, skip = a_log.reshape(1, hp), skip_d.reshape(1, hp)
-    state_outs = [((tokens, wc), bf16), ((2 * SPAN * (nb - 1), wc), bf16), ((16, wc), f32)]
+    state_outs = [((tokens, wc), bf16), ((SPAN * (nb - 1), wc), bf16), ((16, wc), f32)]
     dma = pltpu.SemaphoreType.DMA
+    hbm = lambda value: pltpu.with_memory_space_constraint(value, pltpu.HBM)
     first = call(
         functools.partial(first_kernel, heads, hp, nch),
-        [ANY, ANY, ANY] + [VMEM] * 5,
+        [ANY] * 8,
         [((STATE + TAIL, wc), bf16)] + state_outs
         + [
             ((tokens, 2 * STATE), bf16),
@@ -441,28 +454,33 @@
             ((TAIL, width), bf16),
             ((TAIL, 2 * STATE), bf16),
             ((KERNEL, 2 * STATE), f32),
-        ],
+            ((KERNEL, width), f32),
+            ((1, tokens), jnp.int32),
+        ]
+        + [((tokens, wc), bf16)] * (nch - 1),
         [
             pltpu.VMEM((tokens, wc), bf16),
             pltpu.VMEM((tokens, 2 * STATE), bf16),
             pltpu.VMEM((TAIL, width), bf16),
-            dma((7,)),
+            pltpu.VMEM((hp, tokens), f32),
+            pltpu.VMEM((1, hp), f32),
+            pltpu.VMEM((1, hp), f32),
+            dma((13,)),
         ],
         name="first",
     )
-    msg, xc, ls, kr, bcc, bt, rows, kcols, shift, xhead, bchead, taps_bc = first(
-        x_in, bc_in, conv_bc, conv_x, dt, alog, skip, seg
-    )
-    xcs, lss, krs, msgs = [xc], [ls], [kr], [msg]
+    (
+        msg, xc, ls, kr, bcc, bt, rows, kcols, shift, xhead, bchead, taps_bc, tapx, seg, *xnext
+    ) = first(*[hbm(v) for v in (x_in, bc_in, conv_bc, conv_x, dt, alog, skip, seg)])
+    xcs, lss, krs = [xc], [ls], [kr]
     recv1 = [lax.ppermute(msg, "seq", ring)]
     if nch == 2:
         msg, xc, ls, kr = call(
             functools.partial(next_kernel, hp, per_chunk),
-            [ANY] + [VMEM] * 5,
+            [VMEM] * 6,
             [((STATE, wc), bf16)] + state_outs,
-            [pltpu.VMEM((tokens, wc), bf16), dma],
             name="next",
-        )(x_in, conv_x, shift, bt, rows, kcols)
+        )(xnext[0], tapx, shift, bt, rows, kcols)
         xcs.append(xc)
         lss.append(ls)
         krs.append(kr)
@@ -479,60 +497,57 @@
             ((8, 128), f32),
         ],
         name="relay_first",
-    )(recv1[0], xhead, bchead, conv_x, taps_bc, seg, bcc, *krs)
-    recvs = [[recv1[c]] for c in range(nch)]
-    relays = [relay]
+    )(recv1[0], xhead, bchead, tapx, taps_bc, seg, bcc, *krs)
+    later = [[] for c in range(nch)]
     if rounds > 1:
-        recvs[0].append(lax.ppermute(relay, "seq", ring))
-    if nch == 2:
-        (relay,) = call(relay_next, [VMEM] * 5, [((STATE, wc), bf16)], name="relay_next")(
-            recv1[1], krs[1], b8, xw8, flag
-        )
-        relays.append(relay)
-        if rounds > 1:
-            recvs[1].append(lax.ppermute(relay, "seq", ring))
-    for _ in range(2, rounds):
-        for c in range(nch):
-            again = recvs[c][-1].astype(f32) * (krs[c][0:1] * flag[0:1, 0:1])
-            recvs[c].append(lax.ppermute(again.astype(bf16), "seq", ring))
+        later[0].append(lax.ppermute(relay, "seq", ring))
+    (cg,) = call(rank_kernel, [VMEM] * 3, [((tokens, 2 * STATE), bf16)], name="rank")(bcc, b8, c8)
     local = []
     for c in range(nch):
+        if c == 1:
+            (relay,) = call(relay_next, [VMEM] * 5 + [ANY], [((STATE, wc), bf16)], name="relay_next")(
+                recv1[1], krs[1], b8, xw8, flag, local[0][1]
+            )
+            if rounds > 1:
+                later[1].append(lax.ppermute(relay, "seq", ring))
         local.append(
             call(
                 functools.partial(local_kernel, hp, c * per_chunk),
-                [ANY] + [VMEM] * 7 + [ANY],
-                [((tokens, wc), f32), ((tokens, wc), f32), ((8, wc), f32)],
+                [ANY] + [VMEM] * 12 + [ANY],
+                [((tokens, wc), f32), ((tokens, wc), f32)],
                 [pltpu.VMEM((tokens, wc), bf16), dma],
                 name=f"local{c}",
-            )(z_in, xcs[c], lss[c], krs[c], bcc, bt, rows, seg, msgs[0] if c == 0 else relays[-1])
+            )(z_in, xcs[c], lss[c], krs[c], bcc, bt, rows, seg, cg, recv1[c], xw8, x8, flag, relay)
         )
-    (cg,) = call(rank_kernel, [VMEM] * 3, [((tokens, 3 * STATE), bf16)], name="rank")(bcc, b8, c8)
+    for _ in range(2, rounds):
+        for c in range(nch):
+            again = later[c][-1].astype(f32) * (krs[c][0:1] * flag[0:1, 0:1])
+            later[c].append(lax.ppermute(again.astype(bf16), "seq", ring))
     sums = jnp.zeros((1, tokens), f32)
     gated = []
     for c in range(nch):
-        n = len(recvs[c])
+        n = len(later[c])
         g, sums = call(
-            functools.partial(gate_kernel, n, c),
-            [VMEM] * (8 + n),
+            functools.partial(gate_kernel, n),
+            [VMEM] * (5 + n),
             [((tokens, wc), f32), ((1, tokens), f32)],
             name=f"gate{c}",
-        )(cg, xw8, x8, flag, *local[c], sums, *recvs[c])
+        )(cg, flag, *local[c], sums, *later[c])
         gated.append(g)
-    gathered = lax.all_gather(sums, "head", axis=0, tiled=True)
-    out = pl.pallas_call(
+    members = lax.axis_size("head")
+    step = 1
+    while step < members:
+        sums = sums + lax.ppermute(sums, "head", [(i, i ^ step) for i in range(members)])
+        step *= 2
+    return pl.pallas_call(
         functools.partial(norm_kernel, nch),
-        grid=(nb,),
         out_shape=jax.ShapeDtypeStruct((tokens, width), bf16),
-        in_specs=[
-            pl.BlockSpec((gathered.shape[0], SPAN), lambda i: (0, i)),
-            pl.BlockSpec((1, width), lambda i: (0, 0)),
-        ]
-        + [VMEM] * nch,
-        out_specs=pl.BlockSpec((SPAN, width), lambda i: (i, 0)),
+        in_specs=[VMEM] * (2 + nch),
+        out_specs=ANY,
+        scratch_shapes=[pltpu.VMEM((tokens, width), bf16), dma((nb,))],
         compiler_params=pltpu.CompilerParams(vmem_limit_bytes=24 << 20),
         name="norm",
-    )(gathered, norm_gain.reshape(1, width), *gated)
-    return out
+    )(sums, norm_gain.reshape(1, width), *gated)
 
 
 def solution(mesh):

time: 42.8 us -> 32.9 us (0.77)
  blocking collectives: 8.92 us -> 0 us
  local copies, waits for them, and re-layouts: 7.06 us -> 0.01 us
  waiting for transfers between devices: 5.92 us -> 12.5 us
  Pallas kernels: 15 us -> 11.1 us
  starting transfers between devices: 5.31 us -> 8.99 us
    all_gather x1 -> x0, blocking collectives: 8.92 us -> none  [per_device(): gathered = lax.all_gather(sums, 'head', axis=0, tiled=True)]
    ppermute x2 -> x5, waiting for transfers between devices: 1.17 us -> 9.38 us  [the longest x3 5.35 us: per_device(): lax.ppermute(sums, 'head', [(i, i ^ step) for i in range(members)])]
    unnamed x25 -> x4, local copies, waits for them, and re-layouts: 7.06 us -> 0.01 us
    ppermute x2 -> x5, starting transfers between devices: 0.57 us -> 4.25 us  [the longest x3 3.04 us: per_device(): lax.ppermute(sums, 'head', [(i, i ^ step) for i in range(members)])]
    pallas_call x7, Pallas kernels: 10.8 us -> 7.37 us  [the longest x1 3.33 us: per_device(): first(*[hbm(v) for v in (x_in, bc_in, conv_bc, conv_x, dt, alog, skip, se...]
    ppermute x1, waiting for transfers between devices: 3.03 us -> 0.12 us  [per_device(): recv1.append(lax.ppermute(msg, 'seq', ring))]
    ppermute x1, waiting for transfers between devices: 1.72 us -> 3.04 us  [per_device(): recv1 = [lax.ppermute(msg, 'seq', ring)]]
  transfers between devices with their start and end apart: 4 -> 7, of which waited for: 3 -> 7; matrix products, arithmetic and copies ran while one was open for 0% -> 0% of each run, Pallas kernels for 19% -> 19%
where the time goes in v2:
time: 32.9 us; the launch traced here: 32.8 us
  waiting for transfers between devices  12.5 us (38%)
  Pallas kernels  11.1 us (34%)
  starting transfers between devices  8.99 us (27%)
    ppermute x3, waiting for transfers between devices, per_device(): lax.ppermute(sums, 'head', [(i, i ^ step) for i in range(members)])  5.35 us
    pallas_call x2, Pallas kernels, per_device(): call(functools.partial(local_kernel, hp, c * per_chunk), [ANY] + [VMEM] *...  3.42 us
    pallas_call x1, Pallas kernels, per_device(): first(*[hbm(v) for v in (x_in, bc_in, conv_bc, conv_x, dt, alog, skip, se...  3.33 us
    ppermute x1, starting transfers between devices, per_device(): recv1 = [lax.ppermute(msg, 'seq', ring)]  3.1 us
    ppermute x1, waiting for transfers between devices, per_device(): recv1 = [lax.ppermute(msg, 'seq', ring)]  3.04 us
    ppermute x3, starting transfers between devices, per_device(): lax.ppermute(sums, 'head', [(i, i ^ step) for i in range(members)])  3.04 us
    ppermute x1, waiting for transfers between devices, per_device(): later[0].append(lax.ppermute(relay, 'seq', ring))  2.67 us
    ppermute x1, starting transfers between devices, per_device(): recv1.append(lax.ppermute(msg, 'seq', ring))  1.63 us
  transfers between devices with their start and end apart: 7, of which 7 were waited for; matrix products, arithmetic and copies ran while one was open for 0% of the time, Pallas kernels for 19%

profile of v2, /device:TPU:0, one launch (start us, length us, event | category | flops | bytes accessed | tf_op | source)
XLA Modules:
  0.0 32.8 jit_solution(3396628217645840054)
XLA Ops:
  0.0 3.3 %first.1 = (bf16[144,512]{1,0:T(8,128)(2,1)S(1)}, bf16[512,512]{1,0:T(8,128)(2,1)S(1)}, bf16[384,512]{1,0:T(8,128)(2,1)S(1)}, f32[16,512]{1,0:T(8,128)S(1)}, bf1...) custom-call(bf16[512,1024]{1,0:T(8,128)(2,1)} %x_any.1, ...), custom_call_target="tpu_custom_call" | custom-call | tf_op jit(solution)/shard_map/first/pallas_call | solution.py:474
  3.4 3.1 %collective-permute-start = (bf16[144,512]{1,0:T(8,128)(2,1)S(1)}, bf16[144,512]{1,0:T(8,128)(2,1)S(1)}, u32[]{:S(2)}, u32[]{:S(2)}) collective-permute-start(bf16[144,512]{1,0:T(8,128)(2,1)S(1)} %get-tuple-element.39), channel_id=1, source_target_pairs={{0,8},{8,16},{16,24},{24,0},{1,9},{9,17},{17,25},{25,1},{2,10},{10... | collective-permute-start | bytes 442376 | tf_op jit(solution)/shard_map/ppermute | solution.py:476
  6.5 1.5 %next.1 = (bf16[128,512]{1,0:T(8,128)(2,1)S(1)}, bf16[512,512]{1,0:T(8,128)(2,1)S(1)}, bf16[384,512]{1,0:T(8,128)(2,1)S(1)}, f32[16,512]{1,0:T(8,128)S(1)}) custom-call(bf16[512,512]{1,0:T(8,128)(2,1)S(1)} %get-tuple-element.46.xbuf, f32[4,1024]{1,0:T(4,128)S(1)} %get-tuple-element.42.tapx, bf16[1536,256]{1,0:T(8,128)(2,1)S(1)} %get-tuple-element.47.shift, ...), custom_call_target="tpu_custom_call" | custom-call | tf_op jit(solution)/shard_map/next/pallas_call | solution.py:478
  8.0 1.6 %collective-permute-start.1 = (bf16[128,512]{1,0:T(8,128)(2,1)S(1)}, bf16[128,512]{1,0:T(8,128)(2,1)S(1)}, u32[]{:S(2)}, u32[]{:S(2)}) collective-permute-start(bf16[128,512]{1,0:T(8,128)(2,1)S(1)} %get-tuple-element.57), channel_id=1, source_target_pairs={{0,8},{8,16},{16,24},{24,0},{1,9},{9,17},{17,25},{25,1},{2,10},{10... | collective-permute-start | bytes 393224 | tf_op jit(solution)/shard_map/ppermute | solution.py:487
  9.6 3.0 %collective-permute-done.recv = bf16[144,512]{1,0:T(8,128)(2,1)S(1)} collective-permute-done((bf16[144,512]{1,0:T(8,128)(2,1)S(1)}, bf16[144,512]{1,0:T(8,128)(2,1)S(1)}, u32[]{:S(2)}, u32[]{:S(2)}) %collective-permute-start) | collective-permute-done | bytes 147488 | tf_op jit(solution)/shard_map/ppermute | solution.py:476
  12.7 0.4 %relay_first.1 = (bf16[128,512]{1,0:T(8,128)(2,1)S(1)}, bf16[16,1024]{1,0:T(8,128)(2,1)S(1)}, f32[8,1024]{1,0:T(8,128)S(1)}, bf16[16,128]{1,0:T(8,128)(2,1)S(1)}...) custom-call(bf16[144,512]{1,0:T(8,128)(2,1)S(1)} %collective-permute-done.recv, ...), custom_call_target="tpu_custom_call" | custom-call | tf_op jit(solution)/shard_map/relay_first/pallas_call | solution.py:488
  13.0 0.1 collective-permute-start.2
  13.1 0.2 rank.1.cg
  13.3 1.7 %local0.1 = (f32[512,512]{1,0:T(8,128)S(1)}, f32[512,512]{1,0:T(8,128)S(1)}) custom-call(bf16[512,1024]{1,0:T(8,128)(2,1)S(1)} %copy-done, bf16[512,512]{1,0:T(8,128)(2,1)S(1)} %get-tuple-element.60.xc, bf16[384,512]{1,0:T(8,128)(2,1)S(1)} %get-tuple-element.61.lstate, f32[16,512]{1,0:T(8,128)S(1)} %get-tuple-element.45.refs_0_.krows, ...), custom_call_target="tpu_custom_call" | custom-call | tf_op jit(solution)/shard_map/local0/pallas_call | solution.py:514
  15.0 0.1 collective-permute-done.1.recv
  15.1 0.2 relay_next.1.order
  15.3 1.2 %collective-permute-start.3 = (bf16[128,512]{1,0:T(8,128)(2,1)S(1)}, bf16[128,512]{1,0:T(8,128)(2,1)S(1)}, u32[]{:S(2)}, u32[]{:S(2)}) collective-permute-start(bf16[128,512]{1,0:T(8,128)(2,1)S(1)} %relay_next.1.order), channel_id=1, source_target_pairs={{0,8},{8,16},{16,24},{24,0},{1,9},{9,17},{17,25},{25,1},{2,10},{10... | collective-permute-start | bytes 393224 | tf_op jit(solution)/shard_map/ppermute | solution.py:512
  16.5 1.7 %local1.1 = (f32[512,512]{1,0:T(8,128)S(1)}, f32[512,512]{1,0:T(8,128)S(1)}) custom-call(bf16[512,1024]{1,0:T(8,128)(2,1)S(1)} %copy-done, bf16[512,512]{1,0:T(8,128)(2,1)S(1)} %get-tuple-element.55.xc, bf16[384,512]{1,0:T(8,128)(2,1)S(1)} %get-tuple-element.56.lstate, f32[16,512]{1,0:T(8,128)S(1)} %get-tuple-element.51.refs_1_.krows, ...), custom_call_target="tpu_custom_call" | custom-call | tf_op jit(solution)/shard_map/local1/pallas_call | solution.py:514
  18.2 2.7 %collective-permute-done.2.refs_0_ = bf16[128,512]{1,0:T(8,128)(2,1)S(1)} collective-permute-done((bf16[128,512]{1,0:T(8,128)(2,1)S(1)}, bf16[128,512]{1,0:T(8,128)(2,1)S(1)}, u32[]{:S(2)}, u32[]{:S(2)}) %collective-permute-start.2) | collective-permute-done | bytes 131104 | tf_op jit(solution)/shard_map/ppermute | solution.py:503
  20.9 0.4 %gate0.1 = (f32[512,512]{1,0:T(8,128)S(1)}, f32[1,512]{1,0:T(1,128)S(1)}) custom-call(bf16[512,256]{1,0:T(8,128)(2,1)S(1)} %rank.1.cg, f32[8,128]{1,0:T(8,128)S(1)} %get-tuple-element.54.flag, f32[512,512]{1,0:T(8,128)S(1)} %get-tuple-element.66.a_ref, f32[512,512]{1,0:T(8,128)S(1)} %get-tuple-element.63.order.q_ref, f32[1,512]{1,0:T(1,128)S(1)} %broadcast_in_dim.3.prev, ...), custom_call_target="tpu_custom_call" | custom-call | tf_op jit(solution)/shard_map/gate0/pallas_call | solution.py:530
  21.3 1.4 %collective-permute-done.3.refs_0_ = bf16[128,512]{1,0:T(8,128)(2,1)S(1)} collective-permute-done((bf16[128,512]{1,0:T(8,128)(2,1)S(1)}, bf16[128,512]{1,0:T(8,128)(2,1)S(1)}, u32[]{:S(2)}, u32[]{:S(2)}) %collective-permute-start.3) | collective-permute-done | bytes 131104 | tf_op jit(solution)/shard_map/ppermute | solution.py:512
  22.7 0.4 %gate1.1 = (f32[512,512]{1,0:T(8,128)S(1)}, f32[1,512]{1,0:T(1,128)S(1)}) custom-call(bf16[512,256]{1,0:T(8,128)(2,1)S(1)} %rank.1.cg, f32[8,128]{1,0:T(8,128)S(1)} %get-tuple-element.54.flag, f32[512,512]{1,0:T(8,128)S(1)} %get-tuple-element.64.a_ref, f32[512,512]{1,0:T(8,128)S(1)} %get-tuple-element.65.q_ref, f32[1,512]{1,0:T(1,128)S(1)} %get-tuple-element.67.prev, ...), custom_call_target="tpu_custom_call" | custom-call | tf_op jit(solution)/shard_map/gate1/pallas_call | solution.py:530
  23.1 0.1 collective-permute-start.4
  23.2 1.1 %collective-permute-done.4 = f32[1,512]{1,0:T(1,128)S(1)} collective-permute-done((f32[1,512]{1,0:T(1,128)S(1)}, f32[1,512]{1,0:T(1,128)S(1)}, u32[]{:S(2)}, u32[]{:S(2)}) %collective-permute-start.4) | collective-permute-done | bytes 2080 | tf_op jit(solution)/shard_map/ppermute | solution.py:540
  24.3 1.5 %collective-permute-start.5 = (f32[1,512]{1,0:T(1,128)S(1)}, f32[1,512]{1,0:T(1,128)S(1)}, u32[]{:S(2)}, u32[]{:S(2)}) collective-permute-start(f32[1,512]{1,0:T(1,128)S(1)} %add.9), channel_id=1, source_target_pairs={{0,2},{1,3},{2,0},{3,1},{4,6},{5,7},{6,4},{7,5},{8,10},{9,11},{10,... | collective-permute-start | bytes 6152 | tf_op jit(solution)/shard_map/ppermute | solution.py:540
  25.8 2.1 %collective-permute-done.5 = f32[1,512]{1,0:T(1,128)S(1)} collective-permute-done((f32[1,512]{1,0:T(1,128)S(1)}, f32[1,512]{1,0:T(1,128)S(1)}, u32[]{:S(2)}, u32[]{:S(2)}) %collective-permute-start.5) | collective-permute-done | bytes 2080 | tf_op jit(solution)/shard_map/ppermute | solution.py:540
  27.9 1.5 %collective-permute-start.6 = (f32[1,512]{1,0:T(1,128)S(1)}, f32[1,512]{1,0:T(1,128)S(1)}, u32[]{:S(2)}, u32[]{:S(2)}) collective-permute-start(f32[1,512]{1,0:T(1,128)S(1)} %add.10), channel_id=1, source_target_pairs={{0,4},{1,5},{2,6},{3,7},{4,0},{5,1},{6,2},{7,3},{8,12},{9,13},{10,... | collective-permute-start | bytes 6152 | tf_op jit(solution)/shard_map/ppermute | solution.py:540
  29.4 2.1 %collective-permute-done.6 = f32[1,512]{1,0:T(1,128)S(1)} collective-permute-done((f32[1,512]{1,0:T(1,128)S(1)}, f32[1,512]{1,0:T(1,128)S(1)}, u32[]{:S(2)}, u32[]{:S(2)}) %collective-permute-start.6) | collective-permute-done | bytes 2080 | tf_op jit(solution)/shard_map/ppermute | solution.py:540
  31.5 1.3 %norm.1 = bf16[512,1024]{1,0:T(8,128)(2,1)} custom-call(f32[1,512]{1,0:T(1,128)S(1)} %add.11.sums, f32[1,1024]{1,0:T(1,128)S(1)} %bitcast.4, f32[512,512]{1,0:T(8,128)S(1)} %get-tuple-element.69.refs_0_, f32[512,512]{1,0:T(8,128)S(1)} %get-tuple-element.70.refs_1_), custom_call_target="tpu_custom_call" | custom-call | tf_op jit(solution)/shard_map/norm/pallas_call | solution.py:542
  (8 shorter events, 0.0 us)
Async XLA Ops:
  3.3 9.9 %copy-start = (bf16[512,1024]{1,0:T(8,128)(2,1)S(1)}, bf16[512,1024]{1,0:T(8,128)(2,1)}, u32[]{:S(2)}) copy-start(bf16[512,1024]{1,0:T(8,128)(2,1)} %z_any.3) | copy-start | bytes 3145732
  3.4 9.3 %collective-permute-start = (bf16[144,512]{1,0:T(8,128)(2,1)S(1)}, bf16[144,512]{1,0:T(8,128)(2,1)S(1)}, u32[]{:S(2)}, u32[]{:S(2)}) collective-permute-start(bf16[144,512]{1,0:T(8,128)(2,1)S(1)} %get-tuple-element.39), channel_id=1, source_target_pairs={{0,8},{8,16},{16,24},{24,0},{1,9},{9,17},{17,25},{25,1},{2,10},{10... | collective-permute-start | bytes 442376 | tf_op jit(solution)/shard_map/ppermute | solution.py:476
  8.0 7.1 %collective-permute-start.1 = (bf16[128,512]{1,0:T(8,128)(2,1)S(1)}, bf16[128,512]{1,0:T(8,128)(2,1)S(1)}, u32[]{:S(2)}, u32[]{:S(2)}) collective-permute-start(bf16[128,512]{1,0:T(8,128)(2,1)S(1)} %get-tuple-element.57), channel_id=1, source_target_pairs={{0,8},{8,16},{16,24},{24,0},{1,9},{9,17},{17,25},{25,1},{2,10},{10... | collective-permute-start | bytes 393224 | tf_op jit(solution)/shard_map/ppermute | solution.py:487
  13.0 7.8 %collective-permute-start.2 = (bf16[128,512]{1,0:T(8,128)(2,1)S(1)}, bf16[128,512]{1,0:T(8,128)(2,1)S(1)}, u32[]{:S(2)}, u32[]{:S(2)}) collective-permute-start(bf16[128,512]{1,0:T(8,128)(2,1)S(1)} %get-tuple-element.62.order), channel_id=1, source_target_pairs={{0,8},{8,16},{16,24},{24,0},{1,9},{9,17},{17,25},{25,1},{2,10},{10... | collective-permute-start | bytes 393224 | tf_op jit(solution)/shard_map/ppermute | solution.py:503
  15.3 7.3 %collective-permute-start.3 = (bf16[128,512]{1,0:T(8,128)(2,1)S(1)}, bf16[128,512]{1,0:T(8,128)(2,1)S(1)}, u32[]{:S(2)}, u32[]{:S(2)}) collective-permute-start(bf16[128,512]{1,0:T(8,128)(2,1)S(1)} %relay_next.1.order), channel_id=1, source_target_pairs={{0,8},{8,16},{16,24},{24,0},{1,9},{9,17},{17,25},{25,1},{2,10},{10... | collective-permute-start | bytes 393224 | tf_op jit(solution)/shard_map/ppermute | solution.py:512
  20.9 10.6 %copy-start.1 = (f32[1024]{0:T(1024)S(1)}, f32[1024]{0:T(1024)}, u32[]{:S(2)}) copy-start(f32[1024]{0:T(1024)} %param.18) | copy-start | bytes 12292
  23.1 1.2 %collective-permute-start.4 = (f32[1,512]{1,0:T(1,128)S(1)}, f32[1,512]{1,0:T(1,128)S(1)}, u32[]{:S(2)}, u32[]{:S(2)}) collective-permute-start(f32[1,512]{1,0:T(1,128)S(1)} %get-tuple-element.68), channel_id=1, source_target_pairs={{0,1},{1,0},{2,3},{3,2},{4,5},{5,4},{6,7},{7,6},{8,9},{9,8},{10,11... | collective-permute-start | bytes 6152 | tf_op jit(solution)/shard_map/ppermute | solution.py:540
  24.3 3.6 %collective-permute-start.5 = (f32[1,512]{1,0:T(1,128)S(1)}, f32[1,512]{1,0:T(1,128)S(1)}, u32[]{:S(2)}, u32[]{:S(2)}) collective-permute-start(f32[1,512]{1,0:T(1,128)S(1)} %add.9), channel_id=1, source_target_pairs={{0,2},{1,3},{2,0},{3,1},{4,6},{5,7},{6,4},{7,5},{8,10},{9,11},{10,... | collective-permute-start | bytes 6152 | tf_op jit(solution)/shard_map/ppermute | solution.py:540
  27.9 3.6 %collective-permute-start.6 = (f32[1,512]{1,0:T(1,128)S(1)}, f32[1,512]{1,0:T(1,128)S(1)}, u32[]{:S(2)}, u32[]{:S(2)}) collective-permute-start(f32[1,512]{1,0:T(1,128)S(1)} %add.10), channel_id=1, source_target_pairs={{0,4},{1,5},{2,6},{3,7},{4,0},{5,1},{6,2},{7,3},{8,12},{9,13},{10,... | collective-permute-start | bytes 6152 | tf_op jit(solution)/shard_map/ppermute | solution.py:540

commit v3 on v2

--- a/solution.py
+++ b/solution.py
@@ -43,6 +43,19 @@
     return jnp.where(row == col, 1.0, 0.0).astype(bf16)
 
 
+def reached(hops):
+    return jnp.where(lax.axis_index("seq") >= hops, 1.0, 0.0)
+
+
+def onward(peers, members, start):
+    moves = []
+    for i in range(peers):
+        for h in range(members):
+            ahead = (i + 1 if i + 1 < peers else start) * members + h
+            moves.append((i * members + h, ahead if i >= start else i * members + (h ^ 1)))
+    return moves
+
+
 def silu_from_half(half):
     return half + half * jnp.tanh(half)
 
@@ -64,34 +77,39 @@
     krows[...] = kr
     tile = min(TILE, wc)
     ex = expander(hp, 2, wc, first)
-    for j in range(wc // tile):
+    steps = [(j, b) for j in range(wc // tile) for b in range(nb)]
+
+    def gather(j, b):
         js = slice(j * tile, (j + 1) * tile)
-        state = None
-        for b in range(nb):
-            if b == 0:
-                sh = mm(shift[0 : 3 * SPAN, SPAN:], x[blk(0), js])
-            else:
-                sh = mm(
-                    shift[3 * SPAN * b : 3 * SPAN * (b + 1), :],
-                    x[(b - 1) * SPAN : (b + 1) * SPAN, js],
-                )
-            half = sh[0:SPAN] * taps[0:1, js] + sh[SPAN : 2 * SPAN] * taps[1:2, js]
-            half = half + sh[2 * SPAN :] * taps[2:3, js]
-            half = half + x[blk(b), js].astype(f32) * taps[3:4, js]
-            act = silu_from_half(half)
-            if b == 0:
-                top = act[0:TAIL]
-                top = jnp.where(iota(top.shape, 0).astype(f32) < drop, 0.0, top)
-                act = jnp.concatenate([top, act[TAIL:]], 0)
-            act = act.astype(bf16)
-            xc[blk(b), js] = act
-            to_end = mm(split(rows[3 * hp : 4 * hp, blk(b)], 2), ex[:, js], 0, 0)
-            weighted = (act.astype(f32) * to_end).astype(bf16)
-            fresh = mm(bt[:, blk(b)], weighted)
-            state = fresh if b == 0 else state * kr[b : b + 1, js] + fresh
-            if b < nb - 1:
-                lstate[blk(b), js] = state.astype(bf16)
-        msg[0:STATE, js] = state.astype(bf16)
+        if b == 0:
+            return mm(shift[0 : 3 * SPAN, SPAN:], x[blk(0), js])
+        return mm(shift[3 * SPAN * b : 3 * SPAN * (b + 1), :], x[(b - 1) * SPAN : (b + 1) * SPAN, js])
+
+    to_end = [mm(split(rows[3 * hp : 4 * hp, blk(b)], 2), ex, 0, 0) for b in range(nb)]
+    ready = gather(*steps[0])
+    state = None
+    for i, (j, b) in enumerate(steps):
+        js = slice(j * tile, (j + 1) * tile)
+        sh = ready
+        if i + 1 < len(steps):
+            ready = gather(*steps[i + 1])
+        half = sh[0:SPAN] * taps[0:1, js] + sh[SPAN : 2 * SPAN] * taps[1:2, js]
+        half = half + sh[2 * SPAN :] * taps[2:3, js]
+        half = half + x[blk(b), js].astype(f32) * taps[3:4, js]
+        act = silu_from_half(half)
+        if b == 0:
+            top = act[0:TAIL]
+            top = jnp.where(iota(top.shape, 0).astype(f32) < drop, 0.0, top)
+            act = jnp.concatenate([top, act[TAIL:]], 0)
+        act = act.astype(bf16)
+        xc[blk(b), js] = act
+        weighted = (act.astype(f32) * to_end[b][:, js]).astype(bf16)
+        fresh = mm(bt[:, blk(b)], weighted)
+        state = fresh if b == 0 else state * kr[b : b + 1, js] + fresh
+        if b < nb - 1:
+            lstate[blk(b), js] = state.astype(bf16)
+        else:
+            msg[0:STATE, js] = state.astype(bf16)
 
 
 def first_kernel(
@@ -153,7 +171,7 @@
             kc = kc + jnp.where(lane == b, keep, 0.0)
         else:
             rows[2 * hp : 3 * hp, blk(b)] = jnp.zeros((hp, SPAN), f32)
-            is_drop = jnp.where((lane1 < KERNEL - 1) & (segb == seg_first), 1.0, 0.0)
+            is_drop = jnp.where((lane1 < KERNEL - 1) & (segb == seg_first), reached(1), 0.0)
             drop = jnp.sum(is_drop, axis=1, keepdims=True)
             early = jnp.exp2(jnp.where(lane < KERNEL - 1, -cum, 0.0)) * dtb * is_drop
             kc = kc + pltpu.roll(early, 8, 1)
@@ -238,7 +256,7 @@
 
 def relay_first(nch, recv, xhead, bchead, tapx, taps_bc, seg_ref, bcc, *refs):
     krows = refs[:nch]
-    out, xw8_ref, x8_ref, b8_ref, c8_ref, flag_ref = refs[nch:]
+    out, xw8_ref, x8_ref, b8_ref, c8_ref, flag_ref = refs[nch + 1 :]
     wc = out.shape[1]
     tile = recv[STATE:, :].astype(f32)
     tile0, tile1 = tile[0:8], tile[8:16, 0:STATE]
@@ -246,10 +264,9 @@
     seg_first = seg[:, 0:1]
     lane = iota((1, SPAN), 1)
     drop = jnp.sum(
-        jnp.where((lane < KERNEL - 1) & (seg == seg_first), 1.0, 0.0), axis=1, keepdims=True
-    )
-    joined = jnp.where(tile0[0:1, 0:1] == seg_first + 1.0, 1.0, 0.0)
-    flag = joined * jnp.where(lax.axis_index("seq") == 0, 0.0, 1.0)
+        jnp.where((lane < KERNEL - 1) & (seg == seg_first), reached(1), 0.0), axis=1, keepdims=True
+    )
+    flag = jnp.where(tile0[0:1, 0:1] == seg_first + 1.0, reached(1), 0.0)
     flag_ref[...] = jnp.broadcast_to(flag, (8, 128))
 
     def lower(value):
@@ -281,15 +298,22 @@
             out[...] = relay_state(kr, recv[0:STATE, :], b8, xw8, flag)
 
 
-def relay_next(recv, krows, b8, xw8, flag, order, out):
+def relay_next(recv, krows, b8, xw8, flag, out):
     wc = out.shape[1]
     out[...] = relay_state(krows[...], recv[...], b8[...], xw8[:, wc:], flag[0:1, 0:1])
 
 
-def local_kernel(
-    hp, first, z_any, xc, lstate, krows, bcc, bt, rows, seg_ref, cg, recv, xw8, x8, flag, order,
-    a_ref, q_ref, zbuf, sem,
-):
+def inflow_rhs(recv, xw8, flag):
+    state = (recv[0:STATE, :].astype(f32) * flag[0:1, 0:1]).astype(bf16)
+    return jnp.concatenate([state, xw8, jnp.zeros((128 - TAIL, state.shape[1]), bf16)], 0)
+
+
+def local_kernel(hp, first, late, *refs):
+    z_any, xc, lstate, krows, bcc, bt, rows, seg_ref = refs[:8]
+    if late:
+        cg, recv, xw8, x8, flag, order = refs[8:14]
+    a_ref, q_ref = refs[-5:-3] if not late else refs[-4:-2]
+    zbuf, sem = refs[-2:]
     tokens, wc = zbuf.shape
     nb = tokens // SPAN
     lane0 = first * HEAD_DIM
@@ -301,14 +325,8 @@
     head_of = iota((128, SPAN), 0) & (hp - 1)
     low = iota((SPAN, 128), 1) < HEAD_DIM
     tri = iota((SPAN, SPAN), 0) >= iota((SPAN, SPAN), 1)
-    entering = jnp.concatenate(
-        [
-            (recv[0:STATE, :].astype(f32) * flag[0:1, 0:1]).astype(bf16),
-            xw8[:, lanes],
-            jnp.zeros((128 - TAIL, wc), bf16),
-        ],
-        0,
-    )
+    if late:
+        entering = inflow_rhs(recv, xw8[:, lanes], flag)
     for b in range(nb):
         segcol = to_column(seg[:, blk(b)])
         mask = (segcol == seg[:, blk(b)]) & tri
@@ -322,7 +340,8 @@
         left = jnp.concatenate([cum, ones, pad], 0).T
         right = jnp.concatenate([ones, neg_q, pad], 0).astype(f32)
         f_exp = mm(split(rows[hp : 2 * hp, blk(b)], 2), ex, 0, 0)
-        inflow = mm(cg[blk(b), :], entering)
+        if late:
+            inflow = mm(cg[blk(b), :], entering)
         if b > 0:
             e_exp = mm(split(rows[2 * hp : 3 * hp, blk(b)], 2), ex, 0, 0)
             carry = mm(c_blk, lstate[blk(b - 1), :])
@@ -339,16 +358,20 @@
             y = mm((scores * decay).astype(bf16), pair) + xj.astype(f32) * krows[11:12, js]
             if b > 0:
                 y = y + e_exp[:, js] * carry[:, js]
-            else:
+            elif late:
                 top = y[0:8] + x8[:, lane0 + j * 128 : lane0 + (j + 1) * 128]
                 y = jnp.concatenate([top, y[8:]], 0)
             f = f_exp[:, js]
+            if late:
+                y = y + f * inflow[:, js]
             sz = silu_from_half(zbuf[blk(b), js].astype(f32) * 0.5)
-            a_ref[blk(b), js] = (y + f * inflow[:, js]) * sz
+            if b == 0 and not late:
+                refs[-3][:, js] = sz[0:8]
+            a_ref[blk(b), js] = y * sz
             q_ref[blk(b), js] = f * sz
 
 
-def rank_kernel(bcc, b8, c8, cg):
+def rank_kernel(bcc, b8, c8, order, cg):
     tokens = bcc.shape[0]
     b_pad = jnp.concatenate([b8[...], jnp.zeros((128 - TAIL, STATE), bf16)], 0)
     cg[:, 0:STATE] = bcc[:, STATE:]
@@ -358,16 +381,23 @@
     cg[:, STATE:] = jnp.where(causal, g, 0.0).astype(bf16)
 
 
-def gate_kernel(nrecv, cg, flag, a_ref, q_ref, prev, *refs):
-    recvs, (gated, sums) = refs[:nrecv], refs[nrecv:]
+def gate_kernel(nrecv, early, *refs):
+    cg, flag, a_ref, q_ref, prev = refs[:5]
+    recvs, refs = refs[5 : 5 + nrecv], refs[5 + nrecv :]
+    gated, sums = refs[-2:]
     tokens, wc = a_ref.shape
+    total = None
     if nrecv == 1:
         total = recvs[0][...]
     elif nrecv > 1:
-        total = recvs[0][...].astype(f32)
-        for r in recvs[1:]:
-            total = total + r[...].astype(f32)
+        total = 0.0
+        for i, r in enumerate(recvs):
+            total = total + r[...].astype(f32) * reached(i + 2)
         total = total.astype(bf16)
+    valid = flag[0:1, 0:1] * reached(2)
+    if early:
+        recv, xw8, x8, sz8 = refs[:4]
+        entering = inflow_rhs(recv, xw8[:, 0:wc], flag)
     tile = min(256, wc)
     for b in range(tokens // SPAN):
         acc = None
@@ -375,7 +405,11 @@
             js = slice(j * tile, (j + 1) * tile)
             g = a_ref[blk(b), js]
             if nrecv:
-                g = g + (q_ref[blk(b), js] * flag[0:1, 0:1]) * mm(cg[blk(b), 0:STATE], total[:, js])
+                g = g + (q_ref[blk(b), js] * valid) * mm(cg[blk(b), 0:STATE], total[:, js])
+            if early:
+                g = g + q_ref[blk(b), js] * mm(cg[blk(b), :], entering[:, js])
+                if b == 0:
+                    g = jnp.concatenate([g[0:8] + x8[:, js] * sz8[:, js], g[8:]], 0)
             gated[blk(b), js] = g
             sq = g * g
             for i in range(tile // 128):
@@ -431,7 +465,11 @@
     nch = 2 if width % 512 == 0 else 1
     wc = width // nch
     per_chunk = heads // nch
-    ring = [(i, (i + 1) % peers) for i in range(peers)]
+    members = lax.axis_size("head")
+
+    def shift(value, hops):
+        return lax.ppermute(value, ("seq", "head"), onward(peers, members, hops - 1))
+
     if hp != heads:
         dt = jnp.pad(dt, ((0, hp - heads), (0, 0)))
         a_log = jnp.pad(a_log, (0, hp - heads))
@@ -470,24 +508,36 @@
         name="first",
     )
     (
-        msg, xc, ls, kr, bcc, bt, rows, kcols, shift, xhead, bchead, taps_bc, tapx, seg, *xnext
+        msg, xc, ls, kr, bcc, bt, rows, kcols, shifts, xhead, bchead, taps_bc, tapx, seg, *xnext
     ) = first(*[hbm(v) for v in (x_in, bc_in, conv_bc, conv_x, dt, alog, skip, seg)])
     xcs, lss, krs = [xc], [ls], [kr]
-    recv1 = [lax.ppermute(msg, "seq", ring)]
+    recv1 = [shift(msg, 1)]
     if nch == 2:
         msg, xc, ls, kr = call(
             functools.partial(next_kernel, hp, per_chunk),
             [VMEM] * 6,
             [((STATE, wc), bf16)] + state_outs,
             name="next",
-        )(xnext[0], tapx, shift, bt, rows, kcols)
+        )(xnext[0], tapx, shifts, bt, rows, kcols)
         xcs.append(xc)
         lss.append(ls)
         krs.append(kr)
-        recv1.append(lax.ppermute(msg, "seq", ring))
+        recv1.append(shift(msg, 1))
+    def run_local(c, extra):
+        late = len(extra) > 0
+        outs = [((tokens, wc), f32)] * 2 + ([] if late else [((8, wc), f32)])
+        return call(
+            functools.partial(local_kernel, hp, c * per_chunk, late),
+            [ANY] + [VMEM] * (7 + max(0, len(extra) - 1)) + [ANY] * late,
+            outs,
+            [pltpu.VMEM((tokens, wc), bf16), dma],
+            name=f"local{c}",
+        )(z_in, xcs[c], lss[c], krs[c], bcc, bt, rows, seg, *extra)
+
+    local = [run_local(0, ())]
     relay, xw8, x8, b8, c8, flag = call(
         functools.partial(relay_first, nch),
-        [VMEM] * (7 + nch),
+        [VMEM] * (7 + nch) + [ANY],
         [
             ((STATE, wc), bf16),
             ((TAIL, width), bf16),
@@ -497,47 +547,42 @@
             ((8, 128), f32),
         ],
         name="relay_first",
-    )(recv1[0], xhead, bchead, tapx, taps_bc, seg, bcc, *krs)
+    )(recv1[0], xhead, bchead, tapx, taps_bc, seg, bcc, *krs, local[0][2])
     later = [[] for c in range(nch)]
     if rounds > 1:
-        later[0].append(lax.ppermute(relay, "seq", ring))
-    (cg,) = call(rank_kernel, [VMEM] * 3, [((tokens, 2 * STATE), bf16)], name="rank")(bcc, b8, c8)
-    local = []
-    for c in range(nch):
-        if c == 1:
-            (relay,) = call(relay_next, [VMEM] * 5 + [ANY], [((STATE, wc), bf16)], name="relay_next")(
-                recv1[1], krs[1], b8, xw8, flag, local[0][1]
-            )
-            if rounds > 1:
-                later[1].append(lax.ppermute(relay, "seq", ring))
-        local.append(
-            call(
-                functools.partial(local_kernel, hp, c * per_chunk),
-                [ANY] + [VMEM] * 12 + [ANY],
-                [((tokens, wc), f32), ((tokens, wc), f32)],
-                [pltpu.VMEM((tokens, wc), bf16), dma],
-                name=f"local{c}",
-            )(z_in, xcs[c], lss[c], krs[c], bcc, bt, rows, seg, cg, recv1[c], xw8, x8, flag, relay)
+        later[0].append(shift(relay, 2))
+    if nch == 2:
+        (relay,) = call(relay_next, [VMEM] * 5, [((STATE, wc), bf16)], name="relay_next")(
+            recv1[1], krs[1], b8, xw8, flag
         )
-    for _ in range(2, rounds):
+        if rounds > 1:
+            later[1].append(shift(relay, 2))
+    (cg,) = call(rank_kernel, [VMEM] * 3 + [ANY], [((tokens, 2 * STATE), bf16)], name="rank")(
+        bcc, b8, c8, relay
+    )
+    if nch == 2:
+        local.append(run_local(1, (cg, recv1[1], xw8, x8, flag, relay)))
+    for hops in range(3, rounds + 1):
         for c in range(nch):
-            again = later[c][-1].astype(f32) * (krs[c][0:1] * flag[0:1, 0:1])
-            later[c].append(lax.ppermute(again.astype(bf16), "seq", ring))
+            again = later[c][-1].astype(f32) * (krs[c][0:1] * flag[0:1, 0:1] * reached(hops - 1))
+            later[c].append(shift(again.astype(bf16), hops))
     sums = jnp.zeros((1, tokens), f32)
     gated = []
     for c in range(nch):
         n = len(later[c])
+        a, q, *rest = local[c]
+        extra = [recv1[c], xw8, x8, *rest] if rest else []
         g, sums = call(
-            functools.partial(gate_kernel, n),
-            [VMEM] * (5 + n),
+            functools.partial(gate_kernel, n, len(rest) > 0),
+            [VMEM] * (5 + n + len(extra)),
             [((tokens, wc), f32), ((1, tokens), f32)],
             name=f"gate{c}",
-        )(cg, flag, *local[c], sums, *later[c])
+        )(cg, flag, a, q, sums, *later[c], *extra)
         gated.append(g)
-    members = lax.axis_size("head")
+    swap = lambda step: lax.ppermute(sums, "head", [(i, i ^ step) for i in range(members)])
     step = 1
     while step < members:
-        sums = sums + lax.ppermute(sums, "head", [(i, i ^ step) for i in range(members)])
+        sums = sums + swap(step)
         step *= 2
     return pl.pallas_call(
         functools.partial(norm_kernel, nch),

time: 32.9 us -> 28.9 us (0.88)
  the two profiles are of different devices: /device:TPU:0 before, /device:TPU:14 now
where the time goes in v3:
time: 28.9 us; the launch traced here: 28.8 us
  Pallas kernels  10.6 us (37%)
  waiting for transfers between devices  9.64 us (33%)
  starting transfers between devices  8.43 us (29%)
    ppermute x4, starting transfers between devices, shift(): lax.ppermute(value, ('seq', 'head'), onward(peers, members, hops - 1))  7.32 us
    ppermute x3, waiting for transfers between devices, per_device(): lax.ppermute(sums, 'head', [(i, i ^ step) for i in range(members)])  7.28 us
    pallas_call x2, Pallas kernels, run_local(): call(functools.partial(local_kernel, hp, c * per_chunk, late), [ANY] + [V...  3.26 us
    pallas_call x1, Pallas kernels, per_device(): first(*[hbm(v) for v in (x_in, bc_in, conv_bc, conv_x, dt, alog, skip, se...  3.13 us
    ppermute x4, waiting for transfers between devices, shift(): lax.ppermute(value, ('seq', 'head'), onward(peers, members, hops - 1))  2.36 us
    pallas_call x1, Pallas kernels, per_device(): pl.pallas_call(functools.partial(norm_kernel, nch), out_shape=jax.ShapeDt...  1.29 us
    pallas_call x1, Pallas kernels, per_device(): call(functools.partial(next_kernel, hp, per_chunk), [VMEM] * 6, [((STATE,...  1.24 us
    ppermute x3, starting transfers between devices, per_device(): lax.ppermute(sums, 'head', [(i, i ^ step) for i in range(members)])  1.11 us
  transfers between devices with their start and end apart: 7, of which 7 were waited for; matrix products, arithmetic and copies ran while one was open for 0% of the time, Pallas kernels for 20%

profile of v3, /device:TPU:14, one launch (start us, length us, event | category | flops | bytes accessed | tf_op | source)
XLA Modules:
  0.0 28.8 jit_solution(7505499557234131608)
XLA Ops:
  0.0 3.1 %first.1 = (bf16[144,512]{1,0:T(8,128)(2,1)S(1)}, bf16[512,512]{1,0:T(8,128)(2,1)S(1)}, bf16[384,512]{1,0:T(8,128)(2,1)S(1)}, f32[16,512]{1,0:T(8,128)S(1)}, bf1...) custom-call(bf16[512,1024]{1,0:T(8,128)(2,1)} %x_any.1, ...), custom_call_target="tpu_custom_call" | custom-call | tf_op jit(solution)/shard_map/first/pallas_call | solution.py:512
  3.1 1.6 %collective-permute-start = (bf16[144,512]{1,0:T(8,128)(2,1)S(1)}, bf16[144,512]{1,0:T(8,128)(2,1)S(1)}, u32[]{:S(2)}, u32[]{:S(2)}) collective-permute-start(bf16[144,512]{1,0:T(8,128)(2,1)S(1)} %get-tuple-element.40), channel_id=1, source_target_pairs={{0,8},{1,9},{2,10},{3,11},{4,12},{5,13},{6,14},{7,15},{8,16},{9,17... | collective-permute-start | bytes 442376 | tf_op jit(solution)/shard_map/ppermute | solution.py:471
  4.8 1.2 %next.1 = (bf16[128,512]{1,0:T(8,128)(2,1)S(1)}, bf16[512,512]{1,0:T(8,128)(2,1)S(1)}, bf16[384,512]{1,0:T(8,128)(2,1)S(1)}, f32[16,512]{1,0:T(8,128)S(1)}) custom-call(bf16[512,512]{1,0:T(8,128)(2,1)S(1)} %get-tuple-element.47.xbuf, f32[4,1024]{1,0:T(4,128)S(1)} %get-tuple-element.43.tapx, bf16[1536,256]{1,0:T(8,128)(2,1)S(1)} %get-tuple-element.48.shift, ...), custom_call_target="tpu_custom_call" | custom-call | tf_op jit(solution)/shard_map/next/pallas_call | solution.py:516
  6.0 1.6 %collective-permute-start.1 = (bf16[128,512]{1,0:T(8,128)(2,1)S(1)}, bf16[128,512]{1,0:T(8,128)(2,1)S(1)}, u32[]{:S(2)}, u32[]{:S(2)}) collective-permute-start(bf16[128,512]{1,0:T(8,128)(2,1)S(1)} %get-tuple-element.58), channel_id=1, source_target_pairs={{0,8},{1,9},{2,10},{3,11},{4,12},{5,13},{6,14},{7,15},{8,16},{9,17... | collective-permute-start | bytes 393224 | tf_op jit(solution)/shard_map/ppermute | solution.py:471
  7.6 1.5 %local0.1 = (f32[512,512]{1,0:T(8,128)S(1)}, f32[512,512]{1,0:T(8,128)S(1)}, f32[8,512]{1,0:T(8,128)S(1)}) custom-call(bf16[512,1024]{1,0:T(8,128)(2,1)S(1)} %copy-done, bf16[512,512]{1,0:T(8,128)(2,1)S(1)} %get-tuple-element.53.refs_1_, bf16[384,512]{1,0:T(8,128)(2,1)S(1)} %get-tuple-element.54.refs_2_, f32[16,512]{1,0:T(8,128)S(1)} %get-tuple-element.46.refs_3_.refs_0_, ...), custom_call_target="tpu_custom_call" | custom-call | tf_op jit(solution)/shard_map/local0/pallas_call | solution.py:529
  9.2 0.2 collective-permute-done.recv.refs_6_
  9.4 0.4 %relay_first.1 = (bf16[128,512]{1,0:T(8,128)(2,1)S(1)}, bf16[16,1024]{1,0:T(8,128)(2,1)S(1)}, f32[8,1024]{1,0:T(8,128)S(1)}, bf16[16,128]{1,0:T(8,128)(2,1)S(1)}...) custom-call(bf16[144,512]{1,0:T(8,128)(2,1)S(1)} %collective-permute-done.recv.refs_6_, ...), custom_call_target="tpu_custom_call" | custom-call | tf_op jit(solution)/shard_map/relay_first/pallas_call | solution.py:538
  9.7 1.6 %collective-permute-start.2 = (bf16[128,512]{1,0:T(8,128)(2,1)S(1)}, bf16[128,512]{1,0:T(8,128)(2,1)S(1)}, u32[]{:S(2)}, u32[]{:S(2)}) collective-permute-start(bf16[128,512]{1,0:T(8,128)(2,1)S(1)} %get-tuple-element.68), channel_id=1, source_target_pairs={{0,1},{1,0},{2,3},{3,2},{4,5},{5,4},{6,7},{7,6},{8,16},{9,17},{10,... | collective-permute-start | bytes 393224 | tf_op jit(solution)/shard_map/ppermute | solution.py:471
  11.4 0.2 collective-permute-done.1.recv.refs_9_
  11.6 0.2 relay_next.1.order.refs_13_
  11.8 2.4 %collective-permute-start.3 = (bf16[128,512]{1,0:T(8,128)(2,1)S(1)}, bf16[128,512]{1,0:T(8,128)(2,1)S(1)}, u32[]{:S(2)}, u32[]{:S(2)}) collective-permute-start(bf16[128,512]{1,0:T(8,128)(2,1)S(1)} %relay_next.1.order.refs_13_), channel_id=1, source_target_pairs={{0,1},{1,0},{2,3},{3,2},{4,5},{5,4},{6,7},{7,6},{8,16},{9,17},{10,... | collective-permute-start | bytes 393224 | tf_op jit(solution)/shard_map/ppermute | solution.py:471
  14.3 0.2 rank.1.refs_8_.refs_0_
  14.4 1.7 %local1.1 = (f32[512,512]{1,0:T(8,128)S(1)}, f32[512,512]{1,0:T(8,128)S(1)}) custom-call(bf16[512,1024]{1,0:T(8,128)(2,1)S(1)} %copy-done, bf16[512,512]{1,0:T(8,128)(2,1)S(1)} %get-tuple-element.61.refs_1_, bf16[384,512]{1,0:T(8,128)(2,1)S(1)} %get-tuple-element.62.refs_2_, f32[16,512]{1,0:T(8,128)S(1)} %get-tuple-element.52.refs_1_.krows.refs_3_, ...), custom_call_target="tpu_custom_call" | custom-call | tf_op jit(solution)/shard_map/local1/pallas_call | solution.py:529
  16.2 1.0 %collective-permute-done.2.refs_5_ = bf16[128,512]{1,0:T(8,128)(2,1)S(1)} collective-permute-done((bf16[128,512]{1,0:T(8,128)(2,1)S(1)}, bf16[128,512]{1,0:T(8,128)(2,1)S(1)}, u32[]{:S(2)}, u32[]{:S(2)}) %collective-permute-start.2) | collective-permute-done | bytes 131104 | tf_op jit(solution)/shard_map/ppermute | solution.py:471
  17.1 0.6 %gate0.1 = (f32[512,512]{1,0:T(8,128)S(1)}, f32[1,512]{1,0:T(1,128)S(1)}) custom-call(bf16[512,256]{1,0:T(8,128)(2,1)S(1)} %rank.1.refs_8_.refs_0_, f32[8,128]{1,0:T(8,128)S(1)} %get-tuple-element.60.flag.refs_12_.refs_1_, f32[512,512]{1,0:T(8,128)S(1)} %get-tuple-element.66.refs_2_, f32[512,512]{1,0:T(8,128)S(1)} %get-tuple-element.67.refs_3_, ...), custom_call_target="tpu_custom_call" | custom-call | tf_op jit(solution)/shard_map/gate0/pallas_call | solution.py:575
  17.7 1.0 %collective-permute-done.3.refs_5_ = bf16[128,512]{1,0:T(8,128)(2,1)S(1)} collective-permute-done((bf16[128,512]{1,0:T(8,128)(2,1)S(1)}, bf16[128,512]{1,0:T(8,128)(2,1)S(1)}, u32[]{:S(2)}, u32[]{:S(2)}) %collective-permute-start.3) | collective-permute-done | bytes 131104 | tf_op jit(solution)/shard_map/ppermute | solution.py:471
  18.7 0.4 %gate1.1 = (f32[512,512]{1,0:T(8,128)S(1)}, f32[1,512]{1,0:T(1,128)S(1)}) custom-call(bf16[512,256]{1,0:T(8,128)(2,1)S(1)} %rank.1.refs_8_.refs_0_, f32[8,128]{1,0:T(8,128)S(1)} %get-tuple-element.60.flag.refs_12_.refs_1_, f32[512,512]{1,0:T(8,128)S(1)} %get-tuple-element.64.refs_2_, f32[512,512]{1,0:T(8,128)S(1)} %get-tuple-element.65.refs_3_, ...), custom_call_target="tpu_custom_call" | custom-call | tf_op jit(solution)/shard_map/gate1/pallas_call | solution.py:575
  19.1 0.1 collective-permute-start.4
  19.2 1.1 %collective-permute-done.4 = f32[1,512]{1,0:T(1,128)S(1)} collective-permute-done((f32[1,512]{1,0:T(1,128)S(1)}, f32[1,512]{1,0:T(1,128)S(1)}, u32[]{:S(2)}, u32[]{:S(2)}) %collective-permute-start.4) | collective-permute-done | bytes 2080 | tf_op jit(solution)/shard_map/ppermute | solution.py:582
  20.3 0.5 %collective-permute-start.5 = (f32[1,512]{1,0:T(1,128)S(1)}, f32[1,512]{1,0:T(1,128)S(1)}, u32[]{:S(2)}, u32[]{:S(2)}) collective-permute-start(f32[1,512]{1,0:T(1,128)S(1)} %add.9), channel_id=1, source_target_pairs={{0,2},{1,3},{2,0},{3,1},{4,6},{5,7},{6,4},{7,5},{8,10},{9,11},{10,... | collective-permute-start | bytes 6152 | tf_op jit(solution)/shard_map/ppermute | solution.py:582
  20.9 3.0 %collective-permute-done.5 = f32[1,512]{1,0:T(1,128)S(1)} collective-permute-done((f32[1,512]{1,0:T(1,128)S(1)}, f32[1,512]{1,0:T(1,128)S(1)}, u32[]{:S(2)}, u32[]{:S(2)}) %collective-permute-start.5) | collective-permute-done | bytes 2080 | tf_op jit(solution)/shard_map/ppermute | solution.py:582
  23.9 0.5 %collective-permute-start.6 = (f32[1,512]{1,0:T(1,128)S(1)}, f32[1,512]{1,0:T(1,128)S(1)}, u32[]{:S(2)}, u32[]{:S(2)}) collective-permute-start(f32[1,512]{1,0:T(1,128)S(1)} %add.10), channel_id=1, source_target_pairs={{0,4},{1,5},{2,6},{3,7},{4,0},{5,1},{6,2},{7,3},{8,12},{9,13},{10,... | collective-permute-start | bytes 6152 | tf_op jit(solution)/shard_map/ppermute | solution.py:582
  24.4 3.1 %collective-permute-done.6 = f32[1,512]{1,0:T(1,128)S(1)} collective-permute-done((f32[1,512]{1,0:T(1,128)S(1)}, f32[1,512]{1,0:T(1,128)S(1)}, u32[]{:S(2)}, u32[]{:S(2)}) %collective-permute-start.6) | collective-permute-done | bytes 2080 | tf_op jit(solution)/shard_map/ppermute | solution.py:582
  27.5 1.3 %norm.1 = bf16[512,1024]{1,0:T(8,128)(2,1)} custom-call(f32[1,512]{1,0:T(1,128)S(1)} %add.11.sums, f32[1,1024]{1,0:T(1,128)S(1)} %bitcast.4, f32[512,512]{1,0:T(8,128)S(1)} %get-tuple-element.71.refs_0_, f32[512,512]{1,0:T(8,128)S(1)} %get-tuple-element.72.refs_1_), custom_call_target="tpu_custom_call" | custom-call | tf_op jit(solution)/shard_map/norm/pallas_call | solution.py:587
  (8 shorter events, 0.0 us)
Async XLA Ops:
  0.0 7.6 %copy-start = (bf16[512,1024]{1,0:T(8,128)(2,1)S(1)}, bf16[512,1024]{1,0:T(8,128)(2,1)}, u32[]{:S(2)}) copy-start(bf16[512,1024]{1,0:T(8,128)(2,1)} %refs_0_.3) | copy-start | bytes 3145732
  3.1 6.2 %collective-permute-start = (bf16[144,512]{1,0:T(8,128)(2,1)S(1)}, bf16[144,512]{1,0:T(8,128)(2,1)S(1)}, u32[]{:S(2)}, u32[]{:S(2)}) collective-permute-start(bf16[144,512]{1,0:T(8,128)(2,1)S(1)} %get-tuple-element.40), channel_id=1, source_target_pairs={{0,8},{1,9},{2,10},{3,11},{4,12},{5,13},{6,14},{7,15},{8,16},{9,17... | collective-permute-start | bytes 442376 | tf_op jit(solution)/shard_map/ppermute | solution.py:471
  6.0 5.6 %collective-permute-start.1 = (bf16[128,512]{1,0:T(8,128)(2,1)S(1)}, bf16[128,512]{1,0:T(8,128)(2,1)S(1)}, u32[]{:S(2)}, u32[]{:S(2)}) collective-permute-start(bf16[128,512]{1,0:T(8,128)(2,1)S(1)} %get-tuple-element.58), channel_id=1, source_target_pairs={{0,8},{1,9},{2,10},{3,11},{4,12},{5,13},{6,14},{7,15},{8,16},{9,17... | collective-permute-start | bytes 393224 | tf_op jit(solution)/shard_map/ppermute | solution.py:471
  9.7 7.4 %collective-permute-start.2 = (bf16[128,512]{1,0:T(8,128)(2,1)S(1)}, bf16[128,512]{1,0:T(8,128)(2,1)S(1)}, u32[]{:S(2)}, u32[]{:S(2)}) collective-permute-start(bf16[128,512]{1,0:T(8,128)(2,1)S(1)} %get-tuple-element.68), channel_id=1, source_target_pairs={{0,1},{1,0},{2,3},{3,2},{4,5},{5,4},{6,7},{7,6},{8,16},{9,17},{10,... | collective-permute-start | bytes 393224 | tf_op jit(solution)/shard_map/ppermute | solution.py:471
  11.8 6.9 %collective-permute-start.3 = (bf16[128,512]{1,0:T(8,128)(2,1)S(1)}, bf16[128,512]{1,0:T(8,128)(2,1)S(1)}, u32[]{:S(2)}, u32[]{:S(2)}) collective-permute-start(bf16[128,512]{1,0:T(8,128)(2,1)S(1)} %relay_next.1.order.refs_13_), channel_id=1, source_target_pairs={{0,1},{1,0},{2,3},{3,2},{4,5},{5,4},{6,7},{7,6},{8,16},{9,17},{10,... | collective-permute-start | bytes 393224 | tf_op jit(solution)/shard_map/ppermute | solution.py:471
  17.1 10.4 %copy-start.1 = (f32[1024]{0:T(1024)S(1)}, f32[1024]{0:T(1024)}, u32[]{:S(2)}) copy-start(f32[1024]{0:T(1024)} %param.18) | copy-start | bytes 12292
  19.1 1.2 %collective-permute-start.4 = (f32[1,512]{1,0:T(1,128)S(1)}, f32[1,512]{1,0:T(1,128)S(1)}, u32[]{:S(2)}, u32[]{:S(2)}) collective-permute-start(f32[1,512]{1,0:T(1,128)S(1)} %get-tuple-element.70), channel_id=1, source_target_pairs={{0,1},{1,0},{2,3},{3,2},{4,5},{5,4},{6,7},{7,6},{8,9},{9,8},{10,11... | collective-permute-start | bytes 6152 | tf_op jit(solution)/shard_map/ppermute | solution.py:582
  20.3 3.6 %collective-permute-start.5 = (f32[1,512]{1,0:T(1,128)S(1)}, f32[1,512]{1,0:T(1,128)S(1)}, u32[]{:S(2)}, u32[]{:S(2)}) collective-permute-start(f32[1,512]{1,0:T(1,128)S(1)} %add.9), channel_id=1, source_target_pairs={{0,2},{1,3},{2,0},{3,1},{4,6},{5,7},{6,4},{7,5},{8,10},{9,11},{10,... | collective-permute-start | bytes 6152 | tf_op jit(solution)/shard_map/ppermute | solution.py:582
  23.9 3.6 %collective-permute-start.6 = (f32[1,512]{1,0:T(1,128)S(1)}, f32[1,512]{1,0:T(1,128)S(1)}, u32[]{:S(2)}, u32[]{:S(2)}) collective-permute-start(f32[1,512]{1,0:T(1,128)S(1)} %add.10), channel_id=1, source_target_pairs={{0,4},{1,5},{2,6},{3,7},{4,0},{5,1},{6,2},{7,3},{8,12},{9,13},{10,... | collective-permute-start | bytes 6152 | tf_op jit(solution)/shard_map/ppermute | solution.py:582

commit v4 on v3

--- a/solution.py
+++ b/solution.py
@@ -70,33 +70,49 @@
     return mm(rows, jnp.ones((16, 128), bf16), 0, 0)
 
 
-def chunk_state(hp, first, x, taps, shift, bt, rows, kcols, drop, xc, lstate, krows, msg):
+def windows(shift, data, b, js):
+    inner = mm(shift[3 * SPAN * b : 3 * SPAN * (b + 1), :], data[blk(b), js])
+    if b == 0:
+        return inner, None
+    at = 3 * data.shape[0] + 3 * TAIL * b
+    return inner, mm(shift[at : at + 3 * TAIL, 0:TAIL], data[b * SPAN - TAIL : b * SPAN, js])
+
+
+def conv_of(sh, data, taps):
+    inner, edge = sh
+    half = inner[0:SPAN] * taps[0:1] + inner[SPAN : 2 * SPAN] * taps[1:2]
+    half = half + inner[2 * SPAN :] * taps[2:3] + data.astype(f32) * taps[3:4]
+    if edge is not None:
+        top = edge[0:TAIL] * taps[0:1] + edge[TAIL : 2 * TAIL] * taps[1:2]
+        half = jnp.concatenate([half[0:TAIL] + (top + edge[2 * TAIL :] * taps[2:3]), half[TAIL:]], 0)
+    return silu_from_half(half)
+
+
+def chunk_state(
+    hp, first, x, taps, shift, bt, rows, kcols, drop, xc, lstate, krows, msg, prepare=None
+):
     tokens, wc = x.shape
     nb = tokens // SPAN
-    kr = mm(split(kcols, 3), expander(hp, 3, wc, first), 0, 0)[:16]
+    kr = mm(split(kcols[:, 0:16], 3), expander(hp, 3, wc, first), 0, 0)
     krows[...] = kr
     tile = min(TILE, wc)
     ex = expander(hp, 2, wc, first)
     steps = [(j, b) for j in range(wc // tile) for b in range(nb)]
 
     def gather(j, b):
-        js = slice(j * tile, (j + 1) * tile)
-        if b == 0:
-            return mm(shift[0 : 3 * SPAN, SPAN:], x[blk(0), js])
-        return mm(shift[3 * SPAN * b : 3 * SPAN * (b + 1), :], x[(b - 1) * SPAN : (b + 1) * SPAN, js])
-
+        return windows(shift, x, b, slice(j * tile, (j + 1) * tile))
+
+    ready = gather(*steps[0])
+    if prepare is not None:
+        prepare()
     to_end = [mm(split(rows[3 * hp : 4 * hp, blk(b)], 2), ex, 0, 0) for b in range(nb)]
-    ready = gather(*steps[0])
     state = None
     for i, (j, b) in enumerate(steps):
         js = slice(j * tile, (j + 1) * tile)
         sh = ready
         if i + 1 < len(steps):
             ready = gather(*steps[i + 1])
-        half = sh[0:SPAN] * taps[0:1, js] + sh[SPAN : 2 * SPAN] * taps[1:2, js]
-        half = half + sh[2 * SPAN :] * taps[2:3, js]
-        half = half + x[blk(b), js].astype(f32) * taps[3:4, js]
-        act = silu_from_half(half)
+        act = conv_of(sh, x[blk(b), js], taps[:, js])
         if b == 0:
             top = act[0:TAIL]
             top = jnp.where(iota(top.shape, 0).astype(f32) < drop, 0.0, top)
@@ -115,11 +131,10 @@
 def first_kernel(
     heads, hp, nch,
     x_any, bc_any, tapbc_any, tapx_any, dt_any, alog_any, skip_any, seg_any,
-    msg, xc, lstate, krows, bcc, bt, rows, kcols, shift, xhead, bchead, taps_bc, tapx, seg_ref,
-    *refs,
+    msg, xc, lstate, krows, bt, rows, kcols, shift, xhead, bchead, taps_bc, tapx, seg_ref, craw,
+    last_ref, *refs,
 ):
-    xnext = refs[: nch - 1]
-    xbuf, bcbuf, xtail, dt_ref, alog_ref, skip_ref, sems = refs[nch - 1 :]
+    bbuf, xbuf, xtail, dt_ref, alog_ref, skip_ref, sems = refs
     tokens, wc = xbuf.shape
     nb = tokens // SPAN
     group = lax.axis_index("head") * heads // (HEADS // GROUPS)
@@ -129,8 +144,8 @@
     small = [(dt_any, dt_ref), (alog_any, alog_ref), (skip_any, skip_ref), (seg_any, seg_ref), (tapx_any, tapx)]
     small = [pltpu.make_async_copy(a, b, sems.at[7 + i]) for i, (a, b) in enumerate(small)]
     copies = [
-        pltpu.make_async_copy(bc_any.at[:, pl.ds(col_b, STATE)], bcbuf.at[:, 0:STATE], sems.at[0]),
-        pltpu.make_async_copy(bc_any.at[:, pl.ds(col_c, STATE)], bcbuf.at[:, STATE:], sems.at[1]),
+        pltpu.make_async_copy(bc_any.at[:, pl.ds(col_b, STATE)], bbuf, sems.at[0]),
+        pltpu.make_async_copy(bc_any.at[:, pl.ds(col_c, STATE)], craw, sems.at[1]),
         pltpu.make_async_copy(tapbc_any.at[:, pl.ds(col_b, STATE)], taps_bc.at[:, 0:STATE], sems.at[2]),
         pltpu.make_async_copy(tapbc_any.at[:, pl.ds(col_c, STATE)], taps_bc.at[:, STATE:], sems.at[3]),
         pltpu.make_async_copy(x_any.at[:, 0:wc], xbuf, sems.at[4]),
@@ -138,7 +153,7 @@
         pltpu.make_async_copy(x_any.at[0:TAIL, :], xhead, sems.at[6]),
     ]
     if nch == 2:
-        copies.append(pltpu.make_async_copy(x_any.at[:, wc:], xnext[0], sems.at[12]))
+        copies.append(pltpu.make_async_copy(x_any.at[:, wc:], last_ref, sems.at[12]))
     for copy in small + copies:
         copy.start()
     for copy in small:
@@ -182,35 +197,35 @@
     kc = kc + jnp.where(lane == 0, fend, 0.0) + jnp.where(lane == 16, drop, 0.0)
     kcols[...] = kc
     delta = iota((SPAN, SPAN), 1) - iota((SPAN, SPAN), 0)
+    edge = iota((TAIL, SPAN), 1) - iota((TAIL, SPAN), 0)
     for b in range(nb):
         segcol = to_column(seg[:, blk(b)])
-        same = segcol == seg[:, blk(b)]
+        same = jnp.where(segcol == seg[:, blk(b)], 1.0, 0.0)
+        if b > 0:
+            past = jnp.concatenate([seg[:, b * SPAN - TAIL : b * SPAN], jnp.zeros((1, SPAN - TAIL), f32)], 1)
+            same_past = jnp.where(segcol[0:TAIL] == past, 1.0, 0.0)
         for k in range(KERNEL - 1):
             back = KERNEL - 1 - k
-            r = slice(3 * SPAN * b + SPAN * k, 3 * SPAN * b + SPAN * (k + 1))
-            shift[r, SPAN:] = jnp.where((delta == -back) & same, 1.0, 0.0).astype(bf16)
+            r = 3 * SPAN * b + SPAN * k
+            shift[r : r + SPAN, :] = jnp.where(delta == -back, same, 0.0).astype(bf16)
             if b > 0:
-                same_prev = segcol == seg[:, blk(b - 1)]
-                shift[r, 0:SPAN] = jnp.where((delta == SPAN - back) & same_prev, 1.0, 0.0).astype(bf16)
-            else:
-                shift[r, 0:SPAN] = jnp.zeros((SPAN, SPAN), bf16)
-    for copy in copies[:4]:
+                r = 3 * tokens + TAIL * (3 * b + k)
+                shift[r : r + TAIL, :] = jnp.where(edge == TAIL - back, same_past, 0.0).astype(bf16)
+    for copy in copies[:5]:
         copy.wait()
-    bchead[...] = bcbuf[0:TAIL, :]
-    tb = taps_bc[...] * 0.5
-    for b in range(nb):
-        if b == 0:
-            sh = mm(shift[0 : 3 * SPAN, SPAN:], bcbuf[blk(0), :])
-        else:
-            sh = mm(shift[3 * SPAN * b : 3 * SPAN * (b + 1), :], bcbuf[(b - 1) * SPAN : (b + 1) * SPAN, :])
-        half = sh[0:SPAN] * tb[0:1] + sh[SPAN : 2 * SPAN] * tb[1:2]
-        half = half + sh[2 * SPAN :] * tb[2:3] + bcbuf[blk(b), :].astype(f32) * tb[3:4]
-        act = silu_from_half(half).astype(bf16)
-        bcc[blk(b), :] = act
-        bt[:, blk(b)] = act[:, 0:STATE].T
-    copies[4].wait()
+    bchead[:, 0:STATE] = bbuf[0:TAIL, :]
+    bchead[:, STATE:] = craw[0:TAIL, :]
+    every = slice(0, STATE)
+
+    def keys():
+        taps = taps_bc[:, 0:STATE] * 0.5
+        for b in range(nb):
+            bt[:, blk(b)] = conv_of(windows(shift, bbuf, b, every), bbuf[blk(b), :], taps).astype(bf16).T
+            if nch == 1:
+                queries(shift, craw, taps_bc, last_ref, b)
+
     chunk_state(
-        hp, 0, xbuf, tapx[:, 0:wc] * 0.5, shift, bt, rows, kc, drop, xc, lstate, krows, msg
+        hp, 0, xbuf, tapx[:, 0:wc] * 0.5, shift, bt, rows, kc, drop, xc, lstate, krows, msg, keys
     )
     for copy in copies[5:]:
         copy.wait()
@@ -226,18 +241,30 @@
     if nch == 2:
         tile0 = tile0 + pltpu.roll(tail_of(xtail[:, wc:]), 4, 0)
     tile0 = jnp.where(iota(tile0.shape, 0) == 0, seg_last[-1] + 1.0, tile0)
-    tail_bc = tail_of(bcbuf[tokens - TAIL :, :])
-    tile1 = tail_bc[:, 0:STATE] + pltpu.roll(tail_bc[:, STATE:], 4, 0)
+    tile1 = tail_of(bbuf[tokens - TAIL :, :]) + pltpu.roll(tail_of(craw[tokens - TAIL :, :]), 4, 0)
     if wc > STATE:
         tile1 = jnp.concatenate([tile1, jnp.zeros((8, wc - STATE), f32)], 1)
     msg[STATE:, :] = jnp.concatenate([tile0, tile1], 0).astype(bf16)
 
 
-def next_kernel(hp, first, xbuf, tapx, shift, bt, rows, kcols, msg, xc, lstate, krows):
+def queries(shift, craw, taps_bc, cc, b):
+    taps = taps_bc[:, STATE:] * 0.5
+    sh = windows(shift, craw, b, slice(0, STATE))
+    cc[blk(b), :] = conv_of(sh, craw[blk(b), :], taps).astype(bf16)
+
+
+def next_kernel(
+    hp, first, xbuf, tapx, shift, bt, rows, kcols, craw, taps_bc, msg, xc, lstate, krows, cc
+):
     wc = xbuf.shape[1]
+
+    def prepare():
+        for b in range(xbuf.shape[0] // SPAN):
+            queries(shift, craw, taps_bc, cc, b)
+
     chunk_state(
         hp, first, xbuf, tapx[:, wc : 2 * wc] * 0.5, shift, bt, rows, kcols[...],
-        kcols[0:1, 16:17], xc, lstate, krows, msg,
+        kcols[0:1, 16:17], xc, lstate, krows, msg, prepare,
     )
 
 
@@ -254,7 +281,7 @@
     return (base * krows[0:1]).astype(bf16)
 
 
-def relay_first(nch, recv, xhead, bchead, tapx, taps_bc, seg_ref, bcc, *refs):
+def relay_first(nch, recv, xhead, bchead, tapx, taps_bc, seg_ref, cc, *refs):
     krows = refs[:nch]
     out, xw8_ref, x8_ref, b8_ref, c8_ref, flag_ref = refs[nch + 1 :]
     wc = out.shape[1]
@@ -284,7 +311,7 @@
     )
     b8 = jnp.concatenate([early(bc8[:, 0:STATE]), zero8(STATE)], 0).astype(bf16)
     b8_ref[...] = b8
-    old = bcc[0:TAIL, STATE:].astype(f32)
+    old = cc[0:TAIL, :].astype(f32)
     c8 = jnp.where(iota((8, STATE), 0).astype(f32) < drop, bc8[:, STATE:], old[0:8])
     c8_ref[...] = jnp.concatenate([c8, old[8:16]], 0).astype(bf16)
     for c in range(nch):
@@ -309,17 +336,14 @@
 
 
 def local_kernel(hp, first, late, *refs):
-    z_any, xc, lstate, krows, bcc, bt, rows, seg_ref = refs[:8]
+    z_ref, xc, lstate, krows, cc, bt, rows, seg_ref = refs[:8]
     if late:
         cg, recv, xw8, x8, flag, order = refs[8:14]
-    a_ref, q_ref = refs[-5:-3] if not late else refs[-4:-2]
-    zbuf, sem = refs[-2:]
-    tokens, wc = zbuf.shape
+    a_ref, q_ref = refs[-2:] if late else refs[-3:-1]
+    tokens, wc = a_ref.shape
     nb = tokens // SPAN
     lane0 = first * HEAD_DIM
     lanes = slice(lane0, lane0 + wc)
-    copy = pltpu.make_async_copy(z_any.at[:, lanes], zbuf, sem)
-    copy.start()
     seg = seg_ref[...].astype(f32)
     ex = expander(hp, 2, wc, first)
     head_of = iota((128, SPAN), 0) & (hp - 1)
@@ -330,7 +354,7 @@
     for b in range(nb):
         segcol = to_column(seg[:, blk(b)])
         mask = (segcol == seg[:, blk(b)]) & tri
-        c_blk = bcc[blk(b), STATE:]
+        c_blk = cc[blk(b), :]
         scores = jnp.where(mask, mm(c_blk, bt[:, blk(b)]), 0.0)
         scores = jnp.concatenate([scores, scores], 1)
         cum = split(rows[0:hp, blk(b)], 3)
@@ -345,8 +369,6 @@
         if b > 0:
             e_exp = mm(split(rows[2 * hp : 3 * hp, blk(b)], 2), ex, 0, 0)
             carry = mm(c_blk, lstate[blk(b - 1), :])
-        if b == 0:
-            copy.wait()
         for j in range(wc // 128):
             js = slice(j * 128, (j + 1) * 128)
             xj = xc[blk(b), js]
@@ -364,17 +386,17 @@
             f = f_exp[:, js]
             if late:
                 y = y + f * inflow[:, js]
-            sz = silu_from_half(zbuf[blk(b), js].astype(f32) * 0.5)
+            sz = silu_from_half(z_ref[blk(b), lane0 + j * 128 : lane0 + (j + 1) * 128].astype(f32) * 0.5)
             if b == 0 and not late:
-                refs[-3][:, js] = sz[0:8]
+                refs[-1][:, js] = sz[0:8]
             a_ref[blk(b), js] = y * sz
             q_ref[blk(b), js] = f * sz
 
 
-def rank_kernel(bcc, b8, c8, order, cg):
-    tokens = bcc.shape[0]
+def rank_kernel(cc, b8, c8, order, cg):
+    tokens = cc.shape[0]
     b_pad = jnp.concatenate([b8[...], jnp.zeros((128 - TAIL, STATE), bf16)], 0)
-    cg[:, 0:STATE] = bcc[:, STATE:]
+    cg[:, 0:STATE] = cc[...]
     cg[0:TAIL, 0:STATE] = c8[...]
     g = mm(cg[:, 0:STATE], b_pad, 1, 1)
     causal = iota((tokens, 128), 0) >= iota((tokens, 128), 1)
@@ -484,21 +506,21 @@
         [ANY] * 8,
         [((STATE + TAIL, wc), bf16)] + state_outs
         + [
-            ((tokens, 2 * STATE), bf16),
             ((STATE, tokens), bf16),
             ((5 * hp, tokens), f32),
             ((hp, 128), f32),
-            ((3 * tokens, 2 * SPAN), bf16),
+            ((3 * (tokens + TAIL * nb), SPAN), bf16),
             ((TAIL, width), bf16),
             ((TAIL, 2 * STATE), bf16),
             ((KERNEL, 2 * STATE), f32),
             ((KERNEL, width), f32),
             ((1, tokens), jnp.int32),
-        ]
-        + [((tokens, wc), bf16)] * (nch - 1),
+            ((tokens, STATE), bf16),
+            ((tokens, wc if nch == 2 else STATE), bf16),
+        ],
         [
+            pltpu.VMEM((tokens, STATE), bf16),
             pltpu.VMEM((tokens, wc), bf16),
-            pltpu.VMEM((tokens, 2 * STATE), bf16),
             pltpu.VMEM((TAIL, width), bf16),
             pltpu.VMEM((hp, tokens), f32),
             pltpu.VMEM((1, hp), f32),
@@ -508,17 +530,17 @@
         name="first",
     )
     (
-        msg, xc, ls, kr, bcc, bt, rows, kcols, shifts, xhead, bchead, taps_bc, tapx, seg, *xnext
+        msg, xc, ls, kr, bt, rows, kcols, shifts, xhead, bchead, taps_bc, tapx, seg, craw, cc
     ) = first(*[hbm(v) for v in (x_in, bc_in, conv_bc, conv_x, dt, alog, skip, seg)])
     xcs, lss, krs = [xc], [ls], [kr]
     recv1 = [shift(msg, 1)]
     if nch == 2:
-        msg, xc, ls, kr = call(
+        msg, xc, ls, kr, cc = call(
             functools.partial(next_kernel, hp, per_chunk),
-            [VMEM] * 6,
-            [((STATE, wc), bf16)] + state_outs,
+            [VMEM] * 8,
+            [((STATE, wc), bf16)] + state_outs + [((tokens, STATE), bf16)],
             name="next",
-        )(xnext[0], tapx, shifts, bt, rows, kcols)
+        )(cc, tapx, shifts, bt, rows, kcols, craw, taps_bc)
         xcs.append(xc)
         lss.append(ls)
         krs.append(kr)
@@ -528,11 +550,10 @@
         outs = [((tokens, wc), f32)] * 2 + ([] if late else [((8, wc), f32)])
         return call(
             functools.partial(local_kernel, hp, c * per_chunk, late),
-            [ANY] + [VMEM] * (7 + max(0, len(extra) - 1)) + [ANY] * late,
+            [VMEM] * (8 + max(0, len(extra) - 1)) + [ANY] * late,
             outs,
-            [pltpu.VMEM((tokens, wc), bf16), dma],
             name=f"local{c}",
-        )(z_in, xcs[c], lss[c], krs[c], bcc, bt, rows, seg, *extra)
+        )(z_in, xcs[c], lss[c], krs[c], cc, bt, rows, seg, *extra)
 
     local = [run_local(0, ())]
     relay, xw8, x8, b8, c8, flag = call(
@@ -547,7 +568,7 @@
             ((8, 128), f32),
         ],
         name="relay_first",
-    )(recv1[0], xhead, bchead, tapx, taps_bc, seg, bcc, *krs, local[0][2])
+    )(recv1[0], xhead, bchead, tapx, taps_bc, seg, cc, *krs, local[0][2])
     later = [[] for c in range(nch)]
     if rounds > 1:
         later[0].append(shift(relay, 2))
@@ -558,7 +579,7 @@
         if rounds > 1:
             later[1].append(shift(relay, 2))
     (cg,) = call(rank_kernel, [VMEM] * 3 + [ANY], [((tokens, 2 * STATE), bf16)], name="rank")(
-        bcc, b8, c8, relay
+        cc, b8, c8, relay
     )
     if nch == 2:
         local.append(run_local(1, (cg, recv1[1], xw8, x8, flag, relay)))

time: 28.9 us -> 28.7 us (level)
  Pallas kernels: 10.6 us -> 9.89 us
  waiting for transfers between devices: 9.64 us -> 10.1 us
    ppermute x4, waiting for transfers between devices: 2.36 us -> 2.82 us  [shift(): lax.ppermute(value, ('seq', 'head'), onward(peers, members, hops - 1))]
    pallas_call x3, Pallas kernels: 4.5 us -> 4.04 us  [the longest x2 2.84 us: run_local(): call(functools.partial(local_kernel, hp, c * per_chunk, late), [VMEM] * (...]
  transfers between devices with their start and end apart: 7 -> 7, of which waited for: 7 -> 7; matrix products, arithmetic and copies ran while one was open for 0% -> 0% of each run, Pallas kernels for 20% -> 19%
where the time goes in v4:
time: 28.7 us; the launch traced here: 28.5 us
  waiting for transfers between devices  10.1 us (35%)
  Pallas kernels  9.89 us (34%)
  starting transfers between devices  8.42 us (29%)
    ppermute x4, starting transfers between devices, shift(): lax.ppermute(value, ('seq', 'head'), onward(peers, members, hops - 1))  7.33 us
    ppermute x3, waiting for transfers between devices, per_device(): lax.ppermute(sums, 'head', [(i, i ^ step) for i in range(members)])  7.29 us
    pallas_call x1, Pallas kernels, per_device(): first(*[hbm(v) for v in (x_in, bc_in, conv_bc, conv_x, dt, alog, skip, se...  2.85 us
    pallas_call x2, Pallas kernels, run_local(): call(functools.partial(local_kernel, hp, c * per_chunk, late), [VMEM] * (...  2.84 us
    ppermute x4, waiting for transfers between devices, shift(): lax.ppermute(value, ('seq', 'head'), onward(peers, members, hops - 1))  2.82 us
    pallas_call x1, Pallas kernels, per_device(): pl.pallas_call(functools.partial(norm_kernel, nch), out_shape=jax.ShapeDt...  1.29 us
    pallas_call x1, Pallas kernels, per_device(): call(functools.partial(next_kernel, hp, per_chunk), [VMEM] * 8, [((STATE,...  1.2 us
    ppermute x3, starting transfers between devices, per_device(): lax.ppermute(sums, 'head', [(i, i ^ step) for i in range(members)])  1.09 us
  transfers between devices with their start and end apart: 7, of which 7 were waited for; matrix products, arithmetic and copies ran while one was open for 0% of the time, Pallas kernels for 19%

profile of v4, /device:TPU:14, one launch (start us, length us, event | category | flops | bytes accessed | tf_op | source)
XLA Modules:
  0.0 28.5 jit_solution(7594269989779293940)
XLA Ops:
  0.0 2.9 %first.1 = (bf16[144,512]{1,0:T(8,128)(2,1)S(1)}, bf16[512,512]{1,0:T(8,128)(2,1)S(1)}, bf16[384,512]{1,0:T(8,128)(2,1)S(1)}, f32[16,512]{1,0:T(8,128)S(1)}, bf1...) custom-call(bf16[512,1024]{1,0:T(8,128)(2,1)} %x_any.1, ...), custom_call_target="tpu_custom_call" | custom-call | tf_op jit(solution)/shard_map/first/pallas_call | solution.py:534
  2.9 1.6 %collective-permute-start = (bf16[144,512]{1,0:T(8,128)(2,1)S(1)}, bf16[144,512]{1,0:T(8,128)(2,1)S(1)}, u32[]{:S(2)}, u32[]{:S(2)}) collective-permute-start(bf16[144,512]{1,0:T(8,128)(2,1)S(1)} %get-tuple-element.49), channel_id=1, source_target_pairs={{0,8},{1,9},{2,10},{3,11},{4,12},{5,13},{6,14},{7,15},{8,16},{9,17... | collective-permute-start | bytes 442376 | tf_op jit(solution)/shard_map/ppermute | solution.py:493
  4.5 1.2 %next.1 = (bf16[128,512]{1,0:T(8,128)(2,1)S(1)}, bf16[512,512]{1,0:T(8,128)(2,1)S(1)}, bf16[384,512]{1,0:T(8,128)(2,1)S(1)}, f32[16,512]{1,0:T(8,128)S(1)}, bf16[512,128]{1,0:T(8,128)(2,1)S(1)}) custom-call(bf16[512,512]{1,0:T(8,128)(2,1)S(1)} %get-tuple-element.40.xbuf, f32[4,1024]{1,0:T(4,128)S(1)} %get-tuple-element.41.tapx, ...), custom_call_target="tpu_custom_call" | custom-call | tf_op jit(solution)/shard_map/next/pallas_call | solution.py:538
  5.7 1.6 %collective-permute-start.1 = (bf16[128,512]{1,0:T(8,128)(2,1)S(1)}, bf16[128,512]{1,0:T(8,128)(2,1)S(1)}, u32[]{:S(2)}, u32[]{:S(2)}) collective-permute-start(bf16[128,512]{1,0:T(8,128)(2,1)S(1)} %get-tuple-element.60), channel_id=1, source_target_pairs={{0,8},{1,9},{2,10},{3,11},{4,12},{5,13},{6,14},{7,15},{8,16},{9,17... | collective-permute-start | bytes 393224 | tf_op jit(solution)/shard_map/ppermute | solution.py:493
  7.3 1.3 %local0.1 = (f32[512,512]{1,0:T(8,128)S(1)}, f32[512,512]{1,0:T(8,128)S(1)}, f32[8,512]{1,0:T(8,128)S(1)}) custom-call(bf16[512,1024]{1,0:T(8,128)(2,1)S(1)} %copy-done, bf16[512,512]{1,0:T(8,128)(2,1)S(1)} %get-tuple-element.55.refs_1_, bf16[384,512]{1,0:T(8,128)(2,1)S(1)} %get-tuple-element.56.refs_2_, f32[16,512]{1,0:T(8,128)S(1)} %get-tuple-element.53.refs_3_.refs_0_, ...), custom_call_target="tpu_custom_call" | custom-call | tf_op jit(solution)/shard_map/local0/pallas_call | solution.py:551
  8.7 0.4 %collective-permute-done.recv.refs_6_ = bf16[144,512]{1,0:T(8,128)(2,1)S(1)} collective-permute-done((bf16[144,512]{1,0:T(8,128)(2,1)S(1)}, bf16[144,512]{1,0:T(8,128)(2,1)S(1)}, u32[]{:S(2)}, u32[]{:S(2)}) %collective-permute-start) | collective-permute-done | bytes 147488 | tf_op jit(solution)/shard_map/ppermute | solution.py:493
  9.1 0.4 %relay_first.1 = (bf16[128,512]{1,0:T(8,128)(2,1)S(1)}, bf16[16,1024]{1,0:T(8,128)(2,1)S(1)}, f32[8,1024]{1,0:T(8,128)S(1)}, bf16[16,128]{1,0:T(8,128)(2,1)S(1)}...) custom-call(bf16[144,512]{1,0:T(8,128)(2,1)S(1)} %collective-permute-done.recv.refs_6_, ...), custom_call_target="tpu_custom_call" | custom-call | tf_op jit(solution)/shard_map/relay_first/pallas_call | solution.py:559
  9.5 1.6 %collective-permute-start.2 = (bf16[128,512]{1,0:T(8,128)(2,1)S(1)}, bf16[128,512]{1,0:T(8,128)(2,1)S(1)}, u32[]{:S(2)}, u32[]{:S(2)}) collective-permute-start(bf16[128,512]{1,0:T(8,128)(2,1)S(1)} %get-tuple-element.70), channel_id=1, source_target_pairs={{0,1},{1,0},{2,3},{3,2},{4,5},{5,4},{6,7},{7,6},{8,16},{9,17},{10,... | collective-permute-start | bytes 393224 | tf_op jit(solution)/shard_map/ppermute | solution.py:493
  11.1 0.2 collective-permute-done.1.recv.refs_9_
  11.3 0.2 relay_next.1.order.refs_13_
  11.5 2.4 %collective-permute-start.3 = (bf16[128,512]{1,0:T(8,128)(2,1)S(1)}, bf16[128,512]{1,0:T(8,128)(2,1)S(1)}, u32[]{:S(2)}, u32[]{:S(2)}) collective-permute-start(bf16[128,512]{1,0:T(8,128)(2,1)S(1)} %relay_next.1.order.refs_13_), channel_id=1, source_target_pairs={{0,1},{1,0},{2,3},{3,2},{4,5},{5,4},{6,7},{7,6},{8,16},{9,17},{10,... | collective-permute-start | bytes 393224 | tf_op jit(solution)/shard_map/ppermute | solution.py:493
  14.0 0.2 rank.1.refs_8_.refs_0_
  14.1 1.5 %local1.1 = (f32[512,512]{1,0:T(8,128)S(1)}, f32[512,512]{1,0:T(8,128)S(1)}) custom-call(bf16[512,1024]{1,0:T(8,128)(2,1)S(1)} %copy-done, bf16[512,512]{1,0:T(8,128)(2,1)S(1)} %get-tuple-element.63.refs_1_, bf16[384,512]{1,0:T(8,128)(2,1)S(1)} %get-tuple-element.64.refs_2_, f32[16,512]{1,0:T(8,128)S(1)} %get-tuple-element.54.refs_1_.krows.refs_3_, ...), custom_call_target="tpu_custom_call" | custom-call | tf_op jit(solution)/shard_map/local1/pallas_call | solution.py:551
  15.7 1.2 %collective-permute-done.2.refs_5_ = bf16[128,512]{1,0:T(8,128)(2,1)S(1)} collective-permute-done((bf16[128,512]{1,0:T(8,128)(2,1)S(1)}, bf16[128,512]{1,0:T(8,128)(2,1)S(1)}, u32[]{:S(2)}, u32[]{:S(2)}) %collective-permute-start.2) | collective-permute-done | bytes 131104 | tf_op jit(solution)/shard_map/ppermute | solution.py:493
  16.8 0.6 %gate0.1 = (f32[512,512]{1,0:T(8,128)S(1)}, f32[1,512]{1,0:T(1,128)S(1)}) custom-call(bf16[512,256]{1,0:T(8,128)(2,1)S(1)} %rank.1.refs_8_.refs_0_, f32[8,128]{1,0:T(8,128)S(1)} %get-tuple-element.62.flag.refs_12_.refs_1_, f32[512,512]{1,0:T(8,128)S(1)} %get-tuple-element.68.refs_2_, f32[512,512]{1,0:T(8,128)S(1)} %get-tuple-element.69.refs_3_, ...), custom_call_target="tpu_custom_call" | custom-call | tf_op jit(solution)/shard_map/gate0/pallas_call | solution.py:596
  17.4 1.0 %collective-permute-done.3.refs_5_ = bf16[128,512]{1,0:T(8,128)(2,1)S(1)} collective-permute-done((bf16[128,512]{1,0:T(8,128)(2,1)S(1)}, bf16[128,512]{1,0:T(8,128)(2,1)S(1)}, u32[]{:S(2)}, u32[]{:S(2)}) %collective-permute-start.3) | collective-permute-done | bytes 131104 | tf_op jit(solution)/shard_map/ppermute | solution.py:493
  18.4 0.4 %gate1.1 = (f32[512,512]{1,0:T(8,128)S(1)}, f32[1,512]{1,0:T(1,128)S(1)}) custom-call(bf16[512,256]{1,0:T(8,128)(2,1)S(1)} %rank.1.refs_8_.refs_0_, f32[8,128]{1,0:T(8,128)S(1)} %get-tuple-element.62.flag.refs_12_.refs_1_, f32[512,512]{1,0:T(8,128)S(1)} %get-tuple-element.66.refs_2_, f32[512,512]{1,0:T(8,128)S(1)} %get-tuple-element.67.refs_3_, ...), custom_call_target="tpu_custom_call" | custom-call | tf_op jit(solution)/shard_map/gate1/pallas_call | solution.py:596
  18.8 0.1 collective-permute-start.4
  18.9 1.1 %collective-permute-done.4 = f32[1,512]{1,0:T(1,128)S(1)} collective-permute-done((f32[1,512]{1,0:T(1,128)S(1)}, f32[1,512]{1,0:T(1,128)S(1)}, u32[]{:S(2)}, u32[]{:S(2)}) %collective-permute-start.4) | collective-permute-done | bytes 2080 | tf_op jit(solution)/shard_map/ppermute | solution.py:603
  20.0 0.5 %collective-permute-start.5 = (f32[1,512]{1,0:T(1,128)S(1)}, f32[1,512]{1,0:T(1,128)S(1)}, u32[]{:S(2)}, u32[]{:S(2)}) collective-permute-start(f32[1,512]{1,0:T(1,128)S(1)} %add.9), channel_id=1, source_target_pairs={{0,2},{1,3},{2,0},{3,1},{4,6},{5,7},{6,4},{7,5},{8,10},{9,11},{10,... | collective-permute-start | bytes 6152 | tf_op jit(solution)/shard_map/ppermute | solution.py:603
  20.6 3.1 %collective-permute-done.5 = f32[1,512]{1,0:T(1,128)S(1)} collective-permute-done((f32[1,512]{1,0:T(1,128)S(1)}, f32[1,512]{1,0:T(1,128)S(1)}, u32[]{:S(2)}, u32[]{:S(2)}) %collective-permute-start.5) | collective-permute-done | bytes 2080 | tf_op jit(solution)/shard_map/ppermute | solution.py:603
  23.6 0.5 %collective-permute-start.6 = (f32[1,512]{1,0:T(1,128)S(1)}, f32[1,512]{1,0:T(1,128)S(1)}, u32[]{:S(2)}, u32[]{:S(2)}) collective-permute-start(f32[1,512]{1,0:T(1,128)S(1)} %add.10), channel_id=1, source_target_pairs={{0,4},{1,5},{2,6},{3,7},{4,0},{5,1},{6,2},{7,3},{8,12},{9,13},{10,... | collective-permute-start | bytes 6152 | tf_op jit(solution)/shard_map/ppermute | solution.py:603
  24.1 3.1 %collective-permute-done.6 = f32[1,512]{1,0:T(1,128)S(1)} collective-permute-done((f32[1,512]{1,0:T(1,128)S(1)}, f32[1,512]{1,0:T(1,128)S(1)}, u32[]{:S(2)}, u32[]{:S(2)}) %collective-permute-start.6) | collective-permute-done | bytes 2080 | tf_op jit(solution)/shard_map/ppermute | solution.py:603
  27.2 1.3 %norm.1 = bf16[512,1024]{1,0:T(8,128)(2,1)} custom-call(f32[1,512]{1,0:T(1,128)S(1)} %add.11.sums, f32[1,1024]{1,0:T(1,128)S(1)} %bitcast.4, f32[512,512]{1,0:T(8,128)S(1)} %get-tuple-element.73.refs_0_, f32[512,512]{1,0:T(8,128)S(1)} %get-tuple-element.74.refs_1_), custom_call_target="tpu_custom_call" | custom-call | tf_op jit(solution)/shard_map/norm/pallas_call | solution.py:608
  (8 shorter events, 0.0 us)
Async XLA Ops:
  0.0 7.3 %copy-start = (bf16[512,1024]{1,0:T(8,128)(2,1)S(1)}, bf16[512,1024]{1,0:T(8,128)(2,1)}, u32[]{:S(2)}) copy-start(bf16[512,1024]{1,0:T(8,128)(2,1)} %refs_0_.3) | copy-start | bytes 3145732
  2.9 6.2 %collective-permute-start = (bf16[144,512]{1,0:T(8,128)(2,1)S(1)}, bf16[144,512]{1,0:T(8,128)(2,1)S(1)}, u32[]{:S(2)}, u32[]{:S(2)}) collective-permute-start(bf16[144,512]{1,0:T(8,128)(2,1)S(1)} %get-tuple-element.49), channel_id=1, source_target_pairs={{0,8},{1,9},{2,10},{3,11},{4,12},{5,13},{6,14},{7,15},{8,16},{9,17... | collective-permute-start | bytes 442376 | tf_op jit(solution)/shard_map/ppermute | solution.py:493
  5.7 5.6 %collective-permute-start.1 = (bf16[128,512]{1,0:T(8,128)(2,1)S(1)}, bf16[128,512]{1,0:T(8,128)(2,1)S(1)}, u32[]{:S(2)}, u32[]{:S(2)}) collective-permute-start(bf16[128,512]{1,0:T(8,128)(2,1)S(1)} %get-tuple-element.60), channel_id=1, source_target_pairs={{0,8},{1,9},{2,10},{3,11},{4,12},{5,13},{6,14},{7,15},{8,16},{9,17... | collective-permute-start | bytes 393224 | tf_op jit(solution)/shard_map/ppermute | solution.py:493
  9.5 7.3 %collective-permute-start.2 = (bf16[128,512]{1,0:T(8,128)(2,1)S(1)}, bf16[128,512]{1,0:T(8,128)(2,1)S(1)}, u32[]{:S(2)}, u32[]{:S(2)}) collective-permute-start(bf16[128,512]{1,0:T(8,128)(2,1)S(1)} %get-tuple-element.70), channel_id=1, source_target_pairs={{0,1},{1,0},{2,3},{3,2},{4,5},{5,4},{6,7},{7,6},{8,16},{9,17},{10,... | collective-permute-start | bytes 393224 | tf_op jit(solution)/shard_map/ppermute | solution.py:493
  11.5 6.9 %collective-permute-start.3 = (bf16[128,512]{1,0:T(8,128)(2,1)S(1)}, bf16[128,512]{1,0:T(8,128)(2,1)S(1)}, u32[]{:S(2)}, u32[]{:S(2)}) collective-permute-start(bf16[128,512]{1,0:T(8,128)(2,1)S(1)} %relay_next.1.order.refs_13_), channel_id=1, source_target_pairs={{0,1},{1,0},{2,3},{3,2},{4,5},{5,4},{6,7},{7,6},{8,16},{9,17},{10,... | collective-permute-start | bytes 393224 | tf_op jit(solution)/shard_map/ppermute | solution.py:493
  16.8 10.4 %copy-start.1 = (f32[1024]{0:T(1024)S(1)}, f32[1024]{0:T(1024)}, u32[]{:S(2)}) copy-start(f32[1024]{0:T(1024)} %param.18) | copy-start | bytes 12292
  18.8 1.2 %collective-permute-start.4 = (f32[1,512]{1,0:T(1,128)S(1)}, f32[1,512]{1,0:T(1,128)S(1)}, u32[]{:S(2)}, u32[]{:S(2)}) collective-permute-start(f32[1,512]{1,0:T(1,128)S(1)} %get-tuple-element.72), channel_id=1, source_target_pairs={{0,1},{1,0},{2,3},{3,2},{4,5},{5,4},{6,7},{7,6},{8,9},{9,8},{10,11... | collective-permute-start | bytes 6152 | tf_op jit(solution)/shard_map/ppermute | solution.py:603
  20.0 3.6 %collective-permute-start.5 = (f32[1,512]{1,0:T(1,128)S(1)}, f32[1,512]{1,0:T(1,128)S(1)}, u32[]{:S(2)}, u32[]{:S(2)}) collective-permute-start(f32[1,512]{1,0:T(1,128)S(1)} %add.9), channel_id=1, source_target_pairs={{0,2},{1,3},{2,0},{3,1},{4,6},{5,7},{6,4},{7,5},{8,10},{9,11},{10,... | collective-permute-start | bytes 6152 | tf_op jit(solution)/shard_map/ppermute | solution.py:603
  23.6 3.6 %collective-permute-start.6 = (f32[1,512]{1,0:T(1,128)S(1)}, f32[1,512]{1,0:T(1,128)S(1)}, u32[]{:S(2)}, u32[]{:S(2)}) collective-permute-start(f32[1,512]{1,0:T(1,128)S(1)} %add.10), channel_id=1, source_target_pairs={{0,4},{1,5},{2,6},{3,7},{4,0},{5,1},{6,2},{7,3},{8,12},{9,13},{10,... | collective-permute-start | bytes 6152 | tf_op jit(solution)/shard_map/ppermute | solution.py:603

commit v5 on v4

--- a/solution.py
+++ b/solution.py
@@ -41,6 +41,10 @@
     row = iota((parts * heads, width), 0) & (heads - 1)
     col = (iota((parts * heads, width), 1) >> 6) + first
     return jnp.where(row == col, 1.0, 0.0).astype(bf16)
+
+
+def message_rows(wc):
+    return STATE + (8 if wc >= 4 * STATE else TAIL)
 
 
 def reached(hops):
@@ -240,8 +244,20 @@
     tile0 = tail_of(xtail[:, 0:wc])
     if nch == 2:
         tile0 = tile0 + pltpu.roll(tail_of(xtail[:, wc:]), 4, 0)
+    tail_b, tail_c = tail_of(bbuf[tokens - TAIL :, :]), tail_of(craw[tokens - TAIL :, :])
+    if message_rows(wc) == STATE + 8:
+        row0 = jnp.concatenate([tail_b[5:6], tail_c[5:6], tail_b[6:7], tail_c[6:7]], 1)
+        mark = jnp.broadcast_to(seg_last[-1] + 1.0, (1, STATE))
+        row4 = jnp.concatenate([tail_b[7:8], tail_c[7:8], mark, mark], 1)
+        if wc > 4 * STATE:
+            rest = jnp.zeros((1, wc - 4 * STATE), f32)
+            row0, row4 = (jnp.concatenate([r, rest], 1) for r in (row0, row4))
+        row = iota(tile0.shape, 0)
+        tile0 = jnp.where(row == 0, row0, jnp.where(row == 4, row4, tile0))
+        msg[STATE:, :] = tile0.astype(bf16)
+        return
     tile0 = jnp.where(iota(tile0.shape, 0) == 0, seg_last[-1] + 1.0, tile0)
-    tile1 = tail_of(bbuf[tokens - TAIL :, :]) + pltpu.roll(tail_of(craw[tokens - TAIL :, :]), 4, 0)
+    tile1 = tail_b + pltpu.roll(tail_c, 4, 0)
     if wc > STATE:
         tile1 = jnp.concatenate([tile1, jnp.zeros((8, wc - STATE), f32)], 1)
     msg[STATE:, :] = jnp.concatenate([tile0, tile1], 0).astype(bf16)
@@ -286,14 +302,27 @@
     out, xw8_ref, x8_ref, b8_ref, c8_ref, flag_ref = refs[nch + 1 :]
     wc = out.shape[1]
     tile = recv[STATE:, :].astype(f32)
-    tile0, tile1 = tile[0:8], tile[8:16, 0:STATE]
+    tile0 = tile[0:8]
+    mark = tile0[0:1, 0:1]
+    if message_rows(wc) == STATE + 8:
+        row = iota((8, STATE), 0)
+
+        def three(at):
+            first, second = tile0[0:1, at : at + STATE], tile0[0:1, at + 2 * STATE : at + 3 * STATE]
+            third = jnp.where(row == 7, tile0[4:5, at : at + STATE], 0.0)
+            return jnp.where(row == 5, first, jnp.where(row == 6, second, third))
+
+        mark = tile0[4:5, 2 * STATE : 2 * STATE + 1]
+        tail_b, tail_c = three(0), three(STATE)
+    else:
+        tail_b, tail_c = tile[8:16, 0:STATE], pltpu.roll(tile[8:16, 0:STATE], 4, 0)
     seg = seg_ref[:, 0:SPAN].astype(f32)
     seg_first = seg[:, 0:1]
     lane = iota((1, SPAN), 1)
     drop = jnp.sum(
         jnp.where((lane < KERNEL - 1) & (seg == seg_first), reached(1), 0.0), axis=1, keepdims=True
     )
-    flag = jnp.where(tile0[0:1, 0:1] == seg_first + 1.0, reached(1), 0.0)
+    flag = jnp.where(mark == seg_first + 1.0, reached(1), 0.0)
     flag_ref[...] = jnp.broadcast_to(flag, (8, 128))
 
     def lower(value):
@@ -307,7 +336,7 @@
     if nch == 2:
         halo.append(lower(pltpu.roll(tile0, 4, 0)))
     bc8 = early_conv(
-        jnp.concatenate([lower(tile1), lower(pltpu.roll(tile1, 4, 0))], 1), bchead[...], taps_bc[...] * 0.5
+        jnp.concatenate([lower(tail_b), lower(tail_c)], 1), bchead[...], taps_bc[...] * 0.5
     )
     b8 = jnp.concatenate([early(bc8[:, 0:STATE]), zero8(STATE)], 0).astype(bf16)
     b8_ref[...] = b8
@@ -504,7 +533,7 @@
     first = call(
         functools.partial(first_kernel, heads, hp, nch),
         [ANY] * 8,
-        [((STATE + TAIL, wc), bf16)] + state_outs
+        [((message_rows(wc), wc), bf16)] + state_outs
         + [
             ((STATE, tokens), bf16),
             ((5 * hp, tokens), f32),

time: 28.7 us -> 28.5 us (level)
  no operation moved by 1% of the time
where the time goes in v5:
time: 28.5 us; the launch traced here: 28.3 us
  waiting for transfers between devices  9.97 us (35%)
  Pallas kernels  9.82 us (34%)
  starting transfers between devices  8.43 us (30%)
    ppermute x4, starting transfers between devices, shift(): lax.ppermute(value, ('seq', 'head'), onward(peers, members, hops - 1))  7.34 us
    ppermute x3, waiting for transfers between devices, per_device(): lax.ppermute(sums, 'head', [(i, i ^ step) for i in range(members)])  7.29 us
    pallas_call x2, Pallas kernels, run_local(): call(functools.partial(local_kernel, hp, c * per_chunk, late), [VMEM] * (...  2.83 us
    pallas_call x1, Pallas kernels, per_device(): first(*[hbm(v) for v in (x_in, bc_in, conv_bc, conv_x, dt, alog, skip, se...  2.83 us
    ppermute x4, waiting for transfers between devices, shift(): lax.ppermute(value, ('seq', 'head'), onward(peers, members, hops - 1))  2.68 us
    pallas_call x1, Pallas kernels, per_device(): pl.pallas_call(functools.partial(norm_kernel, nch), out_shape=jax.ShapeDt...  1.29 us
    pallas_call x1, Pallas kernels, per_device(): call(functools.partial(next_kernel, hp, per_chunk), [VMEM] * 8, [((STATE,...  1.17 us
    ppermute x3, starting transfers between devices, per_device(): lax.ppermute(sums, 'head', [(i, i ^ step) for i in range(members)])  1.1 us
  transfers between devices with their start and end apart: 7, of which 7 were waited for; matrix products, arithmetic and copies ran while one was open for 0% of the time, Pallas kernels for 19%

profile of v5, /device:TPU:14, one launch (start us, length us, event | category | flops | bytes accessed | tf_op | source)
XLA Modules:
  0.0 28.3 jit_solution(6330534508924803034)
XLA Ops:
  0.0 2.8 %first.1 = (bf16[136,512]{1,0:T(8,128)(2,1)S(1)}, bf16[512,512]{1,0:T(8,128)(2,1)S(1)}, bf16[384,512]{1,0:T(8,128)(2,1)S(1)}, f32[16,512]{1,0:T(8,128)S(1)}, bf1...) custom-call(bf16[512,1024]{1,0:T(8,128)(2,1)} %x_any.1, ...), custom_call_target="tpu_custom_call" | custom-call | tf_op jit(solution)/shard_map/first/pallas_call | solution.py:563
  2.8 1.6 %collective-permute-start = (bf16[136,512]{1,0:T(8,128)(2,1)S(1)}, bf16[136,512]{1,0:T(8,128)(2,1)S(1)}, u32[]{:S(2)}, u32[]{:S(2)}) collective-permute-start(bf16[136,512]{1,0:T(8,128)(2,1)S(1)} %get-tuple-element.49), channel_id=1, source_target_pairs={{0,8},{1,9},{2,10},{3,11},{4,12},{5,13},{6,14},{7,15},{8,16},{9,17... | collective-permute-start | bytes 417800 | tf_op jit(solution)/shard_map/ppermute | solution.py:522
  4.5 1.2 %next.1 = (bf16[128,512]{1,0:T(8,128)(2,1)S(1)}, bf16[512,512]{1,0:T(8,128)(2,1)S(1)}, bf16[384,512]{1,0:T(8,128)(2,1)S(1)}, f32[16,512]{1,0:T(8,128)S(1)}, bf16[512,128]{1,0:T(8,128)(2,1)S(1)}) custom-call(bf16[512,512]{1,0:T(8,128)(2,1)S(1)} %get-tuple-element.40.xbuf, f32[4,1024]{1,0:T(4,128)S(1)} %get-tuple-element.41.tapx, ...), custom_call_target="tpu_custom_call" | custom-call | tf_op jit(solution)/shard_map/next/pallas_call | solution.py:567
  5.6 1.6 %collective-permute-start.1 = (bf16[128,512]{1,0:T(8,128)(2,1)S(1)}, bf16[128,512]{1,0:T(8,128)(2,1)S(1)}, u32[]{:S(2)}, u32[]{:S(2)}) collective-permute-start(bf16[128,512]{1,0:T(8,128)(2,1)S(1)} %get-tuple-element.60), channel_id=1, source_target_pairs={{0,8},{1,9},{2,10},{3,11},{4,12},{5,13},{6,14},{7,15},{8,16},{9,17... | collective-permute-start | bytes 393224 | tf_op jit(solution)/shard_map/ppermute | solution.py:522
  7.3 1.3 %local0.1 = (f32[512,512]{1,0:T(8,128)S(1)}, f32[512,512]{1,0:T(8,128)S(1)}, f32[8,512]{1,0:T(8,128)S(1)}) custom-call(bf16[512,1024]{1,0:T(8,128)(2,1)S(1)} %copy-done, bf16[512,512]{1,0:T(8,128)(2,1)S(1)} %get-tuple-element.55.refs_1_, bf16[384,512]{1,0:T(8,128)(2,1)S(1)} %get-tuple-element.56.refs_2_, f32[16,512]{1,0:T(8,128)S(1)} %get-tuple-element.53.refs_3_.refs_0_, ...), custom_call_target="tpu_custom_call" | custom-call | tf_op jit(solution)/shard_map/local0/pallas_call | solution.py:580
  8.6 0.2 collective-permute-done.recv.refs_6_
  8.8 0.4 %relay_first.1 = (bf16[128,512]{1,0:T(8,128)(2,1)S(1)}, bf16[16,1024]{1,0:T(8,128)(2,1)S(1)}, f32[8,1024]{1,0:T(8,128)S(1)}, bf16[16,128]{1,0:T(8,128)(2,1)S(1)}...) custom-call(bf16[136,512]{1,0:T(8,128)(2,1)S(1)} %collective-permute-done.recv.refs_6_, ...), custom_call_target="tpu_custom_call" | custom-call | tf_op jit(solution)/shard_map/relay_first/pallas_call | solution.py:588
  9.1 1.6 %collective-permute-start.2 = (bf16[128,512]{1,0:T(8,128)(2,1)S(1)}, bf16[128,512]{1,0:T(8,128)(2,1)S(1)}, u32[]{:S(2)}, u32[]{:S(2)}) collective-permute-start(bf16[128,512]{1,0:T(8,128)(2,1)S(1)} %get-tuple-element.70), channel_id=1, source_target_pairs={{0,1},{1,0},{2,3},{3,2},{4,5},{5,4},{6,7},{7,6},{8,16},{9,17},{10,... | collective-permute-start | bytes 393224 | tf_op jit(solution)/shard_map/ppermute | solution.py:522
  10.8 0.3 %collective-permute-done.1.recv.refs_9_ = bf16[128,512]{1,0:T(8,128)(2,1)S(1)} collective-permute-done((bf16[128,512]{1,0:T(8,128)(2,1)S(1)}, bf16[128,512]{1,0:T(8,128)(2,1)S(1)}, u32[]{:S(2)}, u32[]{:S(2)}) %collective-permute-start.1) | collective-permute-done | bytes 131104 | tf_op jit(solution)/shard_map/ppermute | solution.py:522
  11.1 0.2 relay_next.1.order.refs_13_
  11.3 2.4 %collective-permute-start.3 = (bf16[128,512]{1,0:T(8,128)(2,1)S(1)}, bf16[128,512]{1,0:T(8,128)(2,1)S(1)}, u32[]{:S(2)}, u32[]{:S(2)}) collective-permute-start(bf16[128,512]{1,0:T(8,128)(2,1)S(1)} %relay_next.1.order.refs_13_), channel_id=1, source_target_pairs={{0,1},{1,0},{2,3},{3,2},{4,5},{5,4},{6,7},{7,6},{8,16},{9,17},{10,... | collective-permute-start | bytes 393224 | tf_op jit(solution)/shard_map/ppermute | solution.py:522
  13.8 0.2 rank.1.refs_8_.refs_0_
  13.9 1.5 %local1.1 = (f32[512,512]{1,0:T(8,128)S(1)}, f32[512,512]{1,0:T(8,128)S(1)}) custom-call(bf16[512,1024]{1,0:T(8,128)(2,1)S(1)} %copy-done, bf16[512,512]{1,0:T(8,128)(2,1)S(1)} %get-tuple-element.63.refs_1_, bf16[384,512]{1,0:T(8,128)(2,1)S(1)} %get-tuple-element.64.refs_2_, f32[16,512]{1,0:T(8,128)S(1)} %get-tuple-element.54.refs_1_.krows.refs_3_, ...), custom_call_target="tpu_custom_call" | custom-call | tf_op jit(solution)/shard_map/local1/pallas_call | solution.py:580
  15.5 1.3 %collective-permute-done.2.refs_5_ = bf16[128,512]{1,0:T(8,128)(2,1)S(1)} collective-permute-done((bf16[128,512]{1,0:T(8,128)(2,1)S(1)}, bf16[128,512]{1,0:T(8,128)(2,1)S(1)}, u32[]{:S(2)}, u32[]{:S(2)}) %collective-permute-start.2) | collective-permute-done | bytes 131104 | tf_op jit(solution)/shard_map/ppermute | solution.py:522
  16.8 0.6 %gate0.1 = (f32[512,512]{1,0:T(8,128)S(1)}, f32[1,512]{1,0:T(1,128)S(1)}) custom-call(bf16[512,256]{1,0:T(8,128)(2,1)S(1)} %rank.1.refs_8_.refs_0_, f32[8,128]{1,0:T(8,128)S(1)} %get-tuple-element.62.flag.refs_12_.refs_1_, f32[512,512]{1,0:T(8,128)S(1)} %get-tuple-element.68.refs_2_, f32[512,512]{1,0:T(8,128)S(1)} %get-tuple-element.69.refs_3_, ...), custom_call_target="tpu_custom_call" | custom-call | tf_op jit(solution)/shard_map/gate0/pallas_call | solution.py:625
  17.3 0.9 %collective-permute-done.3.refs_5_ = bf16[128,512]{1,0:T(8,128)(2,1)S(1)} collective-permute-done((bf16[128,512]{1,0:T(8,128)(2,1)S(1)}, bf16[128,512]{1,0:T(8,128)(2,1)S(1)}, u32[]{:S(2)}, u32[]{:S(2)}) %collective-permute-start.3) | collective-permute-done | bytes 131104 | tf_op jit(solution)/shard_map/ppermute | solution.py:522
  18.2 0.4 %gate1.1 = (f32[512,512]{1,0:T(8,128)S(1)}, f32[1,512]{1,0:T(1,128)S(1)}) custom-call(bf16[512,256]{1,0:T(8,128)(2,1)S(1)} %rank.1.refs_8_.refs_0_, f32[8,128]{1,0:T(8,128)S(1)} %get-tuple-element.62.flag.refs_12_.refs_1_, f32[512,512]{1,0:T(8,128)S(1)} %get-tuple-element.66.refs_2_, f32[512,512]{1,0:T(8,128)S(1)} %get-tuple-element.67.refs_3_, ...), custom_call_target="tpu_custom_call" | custom-call | tf_op jit(solution)/shard_map/gate1/pallas_call | solution.py:625
  18.6 0.1 collective-permute-start.4
  18.7 1.1 %collective-permute-done.4 = f32[1,512]{1,0:T(1,128)S(1)} collective-permute-done((f32[1,512]{1,0:T(1,128)S(1)}, f32[1,512]{1,0:T(1,128)S(1)}, u32[]{:S(2)}, u32[]{:S(2)}) %collective-permute-start.4) | collective-permute-done | bytes 2080 | tf_op jit(solution)/shard_map/ppermute | solution.py:632
  19.8 0.5 %collective-permute-start.5 = (f32[1,512]{1,0:T(1,128)S(1)}, f32[1,512]{1,0:T(1,128)S(1)}, u32[]{:S(2)}, u32[]{:S(2)}) collective-permute-start(f32[1,512]{1,0:T(1,128)S(1)} %add.9), channel_id=1, source_target_pairs={{0,2},{1,3},{2,0},{3,1},{4,6},{5,7},{6,4},{7,5},{8,10},{9,11},{10,... | collective-permute-start | bytes 6152 | tf_op jit(solution)/shard_map/ppermute | solution.py:632
  20.4 3.1 %collective-permute-done.5 = f32[1,512]{1,0:T(1,128)S(1)} collective-permute-done((f32[1,512]{1,0:T(1,128)S(1)}, f32[1,512]{1,0:T(1,128)S(1)}, u32[]{:S(2)}, u32[]{:S(2)}) %collective-permute-start.5) | collective-permute-done | bytes 2080 | tf_op jit(solution)/shard_map/ppermute | solution.py:632
  23.4 0.5 %collective-permute-start.6 = (f32[1,512]{1,0:T(1,128)S(1)}, f32[1,512]{1,0:T(1,128)S(1)}, u32[]{:S(2)}, u32[]{:S(2)}) collective-permute-start(f32[1,512]{1,0:T(1,128)S(1)} %add.10), channel_id=1, source_target_pairs={{0,4},{1,5},{2,6},{3,7},{4,0},{5,1},{6,2},{7,3},{8,12},{9,13},{10,... | collective-permute-start | bytes 6152 | tf_op jit(solution)/shard_map/ppermute | solution.py:632
  23.9 3.1 %collective-permute-done.6 = f32[1,512]{1,0:T(1,128)S(1)} collective-permute-done((f32[1,512]{1,0:T(1,128)S(1)}, f32[1,512]{1,0:T(1,128)S(1)}, u32[]{:S(2)}, u32[]{:S(2)}) %collective-permute-start.6) | collective-permute-done | bytes 2080 | tf_op jit(solution)/shard_map/ppermute | solution.py:632
  27.0 1.3 %norm.1 = bf16[512,1024]{1,0:T(8,128)(2,1)} custom-call(f32[1,512]{1,0:T(1,128)S(1)} %add.11.sums, f32[1,1024]{1,0:T(1,128)S(1)} %bitcast.4, f32[512,512]{1,0:T(8,128)S(1)} %get-tuple-element.73.refs_0_, f32[512,512]{1,0:T(8,128)S(1)} %get-tuple-element.74.refs_1_), custom_call_target="tpu_custom_call" | custom-call | tf_op jit(solution)/shard_map/norm/pallas_call | solution.py:637
  (8 shorter events, 0.0 us)
Async XLA Ops:
  0.0 7.3 %copy-start = (bf16[512,1024]{1,0:T(8,128)(2,1)S(1)}, bf16[512,1024]{1,0:T(8,128)(2,1)}, u32[]{:S(2)}) copy-start(bf16[512,1024]{1,0:T(8,128)(2,1)} %refs_0_.3) | copy-start | bytes 3145732
  2.8 5.9 %collective-permute-start = (bf16[136,512]{1,0:T(8,128)(2,1)S(1)}, bf16[136,512]{1,0:T(8,128)(2,1)S(1)}, u32[]{:S(2)}, u32[]{:S(2)}) collective-permute-start(bf16[136,512]{1,0:T(8,128)(2,1)S(1)} %get-tuple-element.49), channel_id=1, source_target_pairs={{0,8},{1,9},{2,10},{3,11},{4,12},{5,13},{6,14},{7,15},{8,16},{9,17... | collective-permute-start | bytes 417800 | tf_op jit(solution)/shard_map/ppermute | solution.py:522
  5.6 5.5 %collective-permute-start.1 = (bf16[128,512]{1,0:T(8,128)(2,1)S(1)}, bf16[128,512]{1,0:T(8,128)(2,1)S(1)}, u32[]{:S(2)}, u32[]{:S(2)}) collective-permute-start(bf16[128,512]{1,0:T(8,128)(2,1)S(1)} %get-tuple-element.60), channel_id=1, source_target_pairs={{0,8},{1,9},{2,10},{3,11},{4,12},{5,13},{6,14},{7,15},{8,16},{9,17... | collective-permute-start | bytes 393224 | tf_op jit(solution)/shard_map/ppermute | solution.py:522
  9.1 7.6 %collective-permute-start.2 = (bf16[128,512]{1,0:T(8,128)(2,1)S(1)}, bf16[128,512]{1,0:T(8,128)(2,1)S(1)}, u32[]{:S(2)}, u32[]{:S(2)}) collective-permute-start(bf16[128,512]{1,0:T(8,128)(2,1)S(1)} %get-tuple-element.70), channel_id=1, source_target_pairs={{0,1},{1,0},{2,3},{3,2},{4,5},{5,4},{6,7},{7,6},{8,16},{9,17},{10,... | collective-permute-start | bytes 393224 | tf_op jit(solution)/shard_map/ppermute | solution.py:522
  11.3 6.9 %collective-permute-start.3 = (bf16[128,512]{1,0:T(8,128)(2,1)S(1)}, bf16[128,512]{1,0:T(8,128)(2,1)S(1)}, u32[]{:S(2)}, u32[]{:S(2)}) collective-permute-start(bf16[128,512]{1,0:T(8,128)(2,1)S(1)} %relay_next.1.order.refs_13_), channel_id=1, source_target_pairs={{0,1},{1,0},{2,3},{3,2},{4,5},{5,4},{6,7},{7,6},{8,16},{9,17},{10,... | collective-permute-start | bytes 393224 | tf_op jit(solution)/shard_map/ppermute | solution.py:522
  16.8 10.2 %copy-start.1 = (f32[1024]{0:T(1024)S(1)}, f32[1024]{0:T(1024)}, u32[]{:S(2)}) copy-start(f32[1024]{0:T(1024)} %param.18) | copy-start | bytes 12292
  18.6 1.2 %collective-permute-start.4 = (f32[1,512]{1,0:T(1,128)S(1)}, f32[1,512]{1,0:T(1,128)S(1)}, u32[]{:S(2)}, u32[]{:S(2)}) collective-permute-start(f32[1,512]{1,0:T(1,128)S(1)} %get-tuple-element.72), channel_id=1, source_target_pairs={{0,1},{1,0},{2,3},{3,2},{4,5},{5,4},{6,7},{7,6},{8,9},{9,8},{10,11... | collective-permute-start | bytes 6152 | tf_op jit(solution)/shard_map/ppermute | solution.py:632
  19.8 3.6 %collective-permute-start.5 = (f32[1,512]{1,0:T(1,128)S(1)}, f32[1,512]{1,0:T(1,128)S(1)}, u32[]{:S(2)}, u32[]{:S(2)}) collective-permute-start(f32[1,512]{1,0:T(1,128)S(1)} %add.9), channel_id=1, source_target_pairs={{0,2},{1,3},{2,0},{3,1},{4,6},{5,7},{6,4},{7,5},{8,10},{9,11},{10,... | collective-permute-start | bytes 6152 | tf_op jit(solution)/shard_map/ppermute | solution.py:632
  23.4 3.6 %collective-permute-start.6 = (f32[1,512]{1,0:T(1,128)S(1)}, f32[1,512]{1,0:T(1,128)S(1)}, u32[]{:S(2)}, u32[]{:S(2)}) collective-permute-start(f32[1,512]{1,0:T(1,128)S(1)} %add.10), channel_id=1, source_target_pairs={{0,4},{1,5},{2,6},{3,7},{4,0},{5,1},{6,2},{7,3},{8,12},{9,13},{10,... | collective-permute-start | bytes 6152 | tf_op jit(solution)/shard_map/ppermute | solution.py:632

commit v6 on v5

--- a/solution.py
+++ b/solution.py
@@ -106,16 +106,16 @@
     def gather(j, b):
         return windows(shift, x, b, slice(j * tile, (j + 1) * tile))
 
-    ready = gather(*steps[0])
+    ready = [gather(*step) for step in steps[:2]]
     if prepare is not None:
         prepare()
     to_end = [mm(split(rows[3 * hp : 4 * hp, blk(b)], 2), ex, 0, 0) for b in range(nb)]
     state = None
     for i, (j, b) in enumerate(steps):
         js = slice(j * tile, (j + 1) * tile)
-        sh = ready
-        if i + 1 < len(steps):
-            ready = gather(*steps[i + 1])
+        sh = ready.pop(0)
+        if i + 2 < len(steps):
+            ready.append(gather(*steps[i + 2]))
         act = conv_of(sh, x[blk(b), js], taps[:, js])
         if b == 0:
             top = act[0:TAIL]

time: 28.5 us -> 28.4 us (level)
  transfers between devices with their start and end apart: 7 -> 7, of which waited for: 7 -> 6; matrix products, arithmetic and copies ran while one was open for 0% -> 0% of each run, Pallas kernels for 19% -> 19%
where the time goes in v6:
time: 28.4 us; the launch traced here: 28.3 us
  Pallas kernels  9.89 us (35%)
  waiting for transfers between devices  9.87 us (35%)
  starting transfers between devices  8.45 us (30%)
    ppermute x4, starting transfers between devices, shift(): lax.ppermute(value, ('seq', 'head'), onward(peers, members, hops - 1))  7.34 us
    ppermute x3, waiting for transfers between devices, per_device(): lax.ppermute(sums, 'head', [(i, i ^ step) for i in range(members)])  7.28 us
    pallas_call x1, Pallas kernels, per_device(): first(*[hbm(v) for v in (x_in, bc_in, conv_bc, conv_x, dt, alog, skip, se...  2.84 us
    pallas_call x2, Pallas kernels, run_local(): call(functools.partial(local_kernel, hp, c * per_chunk, late), [VMEM] * (...  2.83 us
    ppermute x4, waiting for transfers between devices, shift(): lax.ppermute(value, ('seq', 'head'), onward(peers, members, hops - 1))  2.58 us
    pallas_call x1, Pallas kernels, per_device(): pl.pallas_call(functools.partial(norm_kernel, nch), out_shape=jax.ShapeDt...  1.29 us
    pallas_call x1, Pallas kernels, per_device(): call(functools.partial(next_kernel, hp, per_chunk), [VMEM] * 8, [((STATE,...  1.24 us
    ppermute x3, starting transfers between devices, per_device(): lax.ppermute(sums, 'head', [(i, i ^ step) for i in range(members)])  1.1 us
  transfers between devices with their start and end apart: 7, of which 6 were waited for; matrix products, arithmetic and copies ran while one was open for 0% of the time, Pallas kernels for 19%

profile of v6, /device:TPU:14, one launch (start us, length us, event | category | flops | bytes accessed | tf_op | source)
XLA Modules:
  0.0 28.3 jit_solution(6618754188520772081)
XLA Ops:
  0.0 2.8 %first.1 = (bf16[136,512]{1,0:T(8,128)(2,1)S(1)}, bf16[512,512]{1,0:T(8,128)(2,1)S(1)}, bf16[384,512]{1,0:T(8,128)(2,1)S(1)}, f32[16,512]{1,0:T(8,128)S(1)}, bf1...) custom-call(bf16[512,1024]{1,0:T(8,128)(2,1)} %x_any.1, ...), custom_call_target="tpu_custom_call" | custom-call | tf_op jit(solution)/shard_map/first/pallas_call | solution.py:563
  2.8 1.6 %collective-permute-start = (bf16[136,512]{1,0:T(8,128)(2,1)S(1)}, bf16[136,512]{1,0:T(8,128)(2,1)S(1)}, u32[]{:S(2)}, u32[]{:S(2)}) collective-permute-start(bf16[136,512]{1,0:T(8,128)(2,1)S(1)} %get-tuple-element.49), channel_id=1, source_target_pairs={{0,8},{1,9},{2,10},{3,11},{4,12},{5,13},{6,14},{7,15},{8,16},{9,17... | collective-permute-start | bytes 417800 | tf_op jit(solution)/shard_map/ppermute | solution.py:522
  4.5 1.2 %next.1 = (bf16[128,512]{1,0:T(8,128)(2,1)S(1)}, bf16[512,512]{1,0:T(8,128)(2,1)S(1)}, bf16[384,512]{1,0:T(8,128)(2,1)S(1)}, f32[16,512]{1,0:T(8,128)S(1)}, bf16[512,128]{1,0:T(8,128)(2,1)S(1)}) custom-call(bf16[512,512]{1,0:T(8,128)(2,1)S(1)} %get-tuple-element.40.xbuf, f32[4,1024]{1,0:T(4,128)S(1)} %get-tuple-element.41.tapx, ...), custom_call_target="tpu_custom_call" | custom-call | tf_op jit(solution)/shard_map/next/pallas_call | solution.py:567
  5.7 1.6 %collective-permute-start.1 = (bf16[128,512]{1,0:T(8,128)(2,1)S(1)}, bf16[128,512]{1,0:T(8,128)(2,1)S(1)}, u32[]{:S(2)}, u32[]{:S(2)}) collective-permute-start(bf16[128,512]{1,0:T(8,128)(2,1)S(1)} %get-tuple-element.60), channel_id=1, source_target_pairs={{0,8},{1,9},{2,10},{3,11},{4,12},{5,13},{6,14},{7,15},{8,16},{9,17... | collective-permute-start | bytes 393224 | tf_op jit(solution)/shard_map/ppermute | solution.py:522
  7.4 1.3 %local0.1 = (f32[512,512]{1,0:T(8,128)S(1)}, f32[512,512]{1,0:T(8,128)S(1)}, f32[8,512]{1,0:T(8,128)S(1)}) custom-call(bf16[512,1024]{1,0:T(8,128)(2,1)S(1)} %copy-done, bf16[512,512]{1,0:T(8,128)(2,1)S(1)} %get-tuple-element.55.refs_1_, bf16[384,512]{1,0:T(8,128)(2,1)S(1)} %get-tuple-element.56.refs_2_, f32[16,512]{1,0:T(8,128)S(1)} %get-tuple-element.53.refs_3_.refs_0_, ...), custom_call_target="tpu_custom_call" | custom-call | tf_op jit(solution)/shard_map/local0/pallas_call | solution.py:580
  8.7 0.0 collective-permute-done.recv.refs_6_
  8.7 0.4 %relay_first.1 = (bf16[128,512]{1,0:T(8,128)(2,1)S(1)}, bf16[16,1024]{1,0:T(8,128)(2,1)S(1)}, f32[8,1024]{1,0:T(8,128)S(1)}, bf16[16,128]{1,0:T(8,128)(2,1)S(1)}...) custom-call(bf16[136,512]{1,0:T(8,128)(2,1)S(1)} %collective-permute-done.recv.refs_6_, ...), custom_call_target="tpu_custom_call" | custom-call | tf_op jit(solution)/shard_map/relay_first/pallas_call | solution.py:588
  9.1 1.6 %collective-permute-start.2 = (bf16[128,512]{1,0:T(8,128)(2,1)S(1)}, bf16[128,512]{1,0:T(8,128)(2,1)S(1)}, u32[]{:S(2)}, u32[]{:S(2)}) collective-permute-start(bf16[128,512]{1,0:T(8,128)(2,1)S(1)} %get-tuple-element.70), channel_id=1, source_target_pairs={{0,1},{1,0},{2,3},{3,2},{4,5},{5,4},{6,7},{7,6},{8,16},{9,17},{10,... | collective-permute-start | bytes 393224 | tf_op jit(solution)/shard_map/ppermute | solution.py:522
  10.7 0.4 %collective-permute-done.1.recv.refs_9_ = bf16[128,512]{1,0:T(8,128)(2,1)S(1)} collective-permute-done((bf16[128,512]{1,0:T(8,128)(2,1)S(1)}, bf16[128,512]{1,0:T(8,128)(2,1)S(1)}, u32[]{:S(2)}, u32[]{:S(2)}) %collective-permute-start.1) | collective-permute-done | bytes 131104 | tf_op jit(solution)/shard_map/ppermute | solution.py:522
  11.1 0.2 relay_next.1.order.refs_13_
  11.3 2.4 %collective-permute-start.3 = (bf16[128,512]{1,0:T(8,128)(2,1)S(1)}, bf16[128,512]{1,0:T(8,128)(2,1)S(1)}, u32[]{:S(2)}, u32[]{:S(2)}) collective-permute-start(bf16[128,512]{1,0:T(8,128)(2,1)S(1)} %relay_next.1.order.refs_13_), channel_id=1, source_target_pairs={{0,1},{1,0},{2,3},{3,2},{4,5},{5,4},{6,7},{7,6},{8,16},{9,17},{10,... | collective-permute-start | bytes 393224 | tf_op jit(solution)/shard_map/ppermute | solution.py:522
  13.8 0.2 rank.1.refs_8_.refs_0_
  14.0 1.5 %local1.1 = (f32[512,512]{1,0:T(8,128)S(1)}, f32[512,512]{1,0:T(8,128)S(1)}) custom-call(bf16[512,1024]{1,0:T(8,128)(2,1)S(1)} %copy-done, bf16[512,512]{1,0:T(8,128)(2,1)S(1)} %get-tuple-element.63.refs_1_, bf16[384,512]{1,0:T(8,128)(2,1)S(1)} %get-tuple-element.64.refs_2_, f32[16,512]{1,0:T(8,128)S(1)} %get-tuple-element.54.refs_1_.krows.refs_3_, ...), custom_call_target="tpu_custom_call" | custom-call | tf_op jit(solution)/shard_map/local1/pallas_call | solution.py:580
  15.5 1.3 %collective-permute-done.2.refs_5_ = bf16[128,512]{1,0:T(8,128)(2,1)S(1)} collective-permute-done((bf16[128,512]{1,0:T(8,128)(2,1)S(1)}, bf16[128,512]{1,0:T(8,128)(2,1)S(1)}, u32[]{:S(2)}, u32[]{:S(2)}) %collective-permute-start.2) | collective-permute-done | bytes 131104 | tf_op jit(solution)/shard_map/ppermute | solution.py:522
  16.8 0.6 %gate0.1 = (f32[512,512]{1,0:T(8,128)S(1)}, f32[1,512]{1,0:T(1,128)S(1)}) custom-call(bf16[512,256]{1,0:T(8,128)(2,1)S(1)} %rank.1.refs_8_.refs_0_, f32[8,128]{1,0:T(8,128)S(1)} %get-tuple-element.62.flag.refs_12_.refs_1_, f32[512,512]{1,0:T(8,128)S(1)} %get-tuple-element.68.refs_2_, f32[512,512]{1,0:T(8,128)S(1)} %get-tuple-element.69.refs_3_, ...), custom_call_target="tpu_custom_call" | custom-call | tf_op jit(solution)/shard_map/gate0/pallas_call | solution.py:625
  17.4 0.8 %collective-permute-done.3.refs_5_ = bf16[128,512]{1,0:T(8,128)(2,1)S(1)} collective-permute-done((bf16[128,512]{1,0:T(8,128)(2,1)S(1)}, bf16[128,512]{1,0:T(8,128)(2,1)S(1)}, u32[]{:S(2)}, u32[]{:S(2)}) %collective-permute-start.3) | collective-permute-done | bytes 131104 | tf_op jit(solution)/shard_map/ppermute | solution.py:522
  18.2 0.4 %gate1.1 = (f32[512,512]{1,0:T(8,128)S(1)}, f32[1,512]{1,0:T(1,128)S(1)}) custom-call(bf16[512,256]{1,0:T(8,128)(2,1)S(1)} %rank.1.refs_8_.refs_0_, f32[8,128]{1,0:T(8,128)S(1)} %get-tuple-element.62.flag.refs_12_.refs_1_, f32[512,512]{1,0:T(8,128)S(1)} %get-tuple-element.66.refs_2_, f32[512,512]{1,0:T(8,128)S(1)} %get-tuple-element.67.refs_3_, ...), custom_call_target="tpu_custom_call" | custom-call | tf_op jit(solution)/shard_map/gate1/pallas_call | solution.py:625
  18.6 0.1 collective-permute-start.4
  18.7 1.1 %collective-permute-done.4 = f32[1,512]{1,0:T(1,128)S(1)} collective-permute-done((f32[1,512]{1,0:T(1,128)S(1)}, f32[1,512]{1,0:T(1,128)S(1)}, u32[]{:S(2)}, u32[]{:S(2)}) %collective-permute-start.4) | collective-permute-done | bytes 2080 | tf_op jit(solution)/shard_map/ppermute | solution.py:632
  19.8 0.5 %collective-permute-start.5 = (f32[1,512]{1,0:T(1,128)S(1)}, f32[1,512]{1,0:T(1,128)S(1)}, u32[]{:S(2)}, u32[]{:S(2)}) collective-permute-start(f32[1,512]{1,0:T(1,128)S(1)} %add.9), channel_id=1, source_target_pairs={{0,2},{1,3},{2,0},{3,1},{4,6},{5,7},{6,4},{7,5},{8,10},{9,11},{10,... | collective-permute-start | bytes 6152 | tf_op jit(solution)/shard_map/ppermute | solution.py:632
  20.3 3.1 %collective-permute-done.5 = f32[1,512]{1,0:T(1,128)S(1)} collective-permute-done((f32[1,512]{1,0:T(1,128)S(1)}, f32[1,512]{1,0:T(1,128)S(1)}, u32[]{:S(2)}, u32[]{:S(2)}) %collective-permute-start.5) | collective-permute-done | bytes 2080 | tf_op jit(solution)/shard_map/ppermute | solution.py:632
  23.4 0.5 %collective-permute-start.6 = (f32[1,512]{1,0:T(1,128)S(1)}, f32[1,512]{1,0:T(1,128)S(1)}, u32[]{:S(2)}, u32[]{:S(2)}) collective-permute-start(f32[1,512]{1,0:T(1,128)S(1)} %add.10), channel_id=1, source_target_pairs={{0,4},{1,5},{2,6},{3,7},{4,0},{5,1},{6,2},{7,3},{8,12},{9,13},{10,... | collective-permute-start | bytes 6152 | tf_op jit(solution)/shard_map/ppermute | solution.py:632
  23.9 3.1 %collective-permute-done.6 = f32[1,512]{1,0:T(1,128)S(1)} collective-permute-done((f32[1,512]{1,0:T(1,128)S(1)}, f32[1,512]{1,0:T(1,128)S(1)}, u32[]{:S(2)}, u32[]{:S(2)}) %collective-permute-start.6) | collective-permute-done | bytes 2080 | tf_op jit(solution)/shard_map/ppermute | solution.py:632
  27.0 1.3 %norm.1 = bf16[512,1024]{1,0:T(8,128)(2,1)} custom-call(f32[1,512]{1,0:T(1,128)S(1)} %add.11.sums, f32[1,1024]{1,0:T(1,128)S(1)} %bitcast.4, f32[512,512]{1,0:T(8,128)S(1)} %get-tuple-element.73.refs_0_, f32[512,512]{1,0:T(8,128)S(1)} %get-tuple-element.74.refs_1_), custom_call_target="tpu_custom_call" | custom-call | tf_op jit(solution)/shard_map/norm/pallas_call | solution.py:637
  (8 shorter events, 0.0 us)
Async XLA Ops:
  0.0 7.4 %copy-start = (bf16[512,1024]{1,0:T(8,128)(2,1)S(1)}, bf16[512,1024]{1,0:T(8,128)(2,1)}, u32[]{:S(2)}) copy-start(bf16[512,1024]{1,0:T(8,128)(2,1)} %refs_0_.3) | copy-start | bytes 3145732
  2.8 5.9 %collective-permute-start = (bf16[136,512]{1,0:T(8,128)(2,1)S(1)}, bf16[136,512]{1,0:T(8,128)(2,1)S(1)}, u32[]{:S(2)}, u32[]{:S(2)}) collective-permute-start(bf16[136,512]{1,0:T(8,128)(2,1)S(1)} %get-tuple-element.49), channel_id=1, source_target_pairs={{0,8},{1,9},{2,10},{3,11},{4,12},{5,13},{6,14},{7,15},{8,16},{9,17... | collective-permute-start | bytes 417800 | tf_op jit(solution)/shard_map/ppermute | solution.py:522
  5.7 5.4 %collective-permute-start.1 = (bf16[128,512]{1,0:T(8,128)(2,1)S(1)}, bf16[128,512]{1,0:T(8,128)(2,1)S(1)}, u32[]{:S(2)}, u32[]{:S(2)}) collective-permute-start(bf16[128,512]{1,0:T(8,128)(2,1)S(1)} %get-tuple-element.60), channel_id=1, source_target_pairs={{0,8},{1,9},{2,10},{3,11},{4,12},{5,13},{6,14},{7,15},{8,16},{9,17... | collective-permute-start | bytes 393224 | tf_op jit(solution)/shard_map/ppermute | solution.py:522
  9.1 7.7 %collective-permute-start.2 = (bf16[128,512]{1,0:T(8,128)(2,1)S(1)}, bf16[128,512]{1,0:T(8,128)(2,1)S(1)}, u32[]{:S(2)}, u32[]{:S(2)}) collective-permute-start(bf16[128,512]{1,0:T(8,128)(2,1)S(1)} %get-tuple-element.70), channel_id=1, source_target_pairs={{0,1},{1,0},{2,3},{3,2},{4,5},{5,4},{6,7},{7,6},{8,16},{9,17},{10,... | collective-permute-start | bytes 393224 | tf_op jit(solution)/shard_map/ppermute | solution.py:522
  11.3 6.8 %collective-permute-start.3 = (bf16[128,512]{1,0:T(8,128)(2,1)S(1)}, bf16[128,512]{1,0:T(8,128)(2,1)S(1)}, u32[]{:S(2)}, u32[]{:S(2)}) collective-permute-start(bf16[128,512]{1,0:T(8,128)(2,1)S(1)} %relay_next.1.order.refs_13_), channel_id=1, source_target_pairs={{0,1},{1,0},{2,3},{3,2},{4,5},{5,4},{6,7},{7,6},{8,16},{9,17},{10,... | collective-permute-start | bytes 393224 | tf_op jit(solution)/shard_map/ppermute | solution.py:522
  16.8 10.2 %copy-start.1 = (f32[1024]{0:T(1024)S(1)}, f32[1024]{0:T(1024)}, u32[]{:S(2)}) copy-start(f32[1024]{0:T(1024)} %param.18) | copy-start | bytes 12292
  18.6 1.2 %collective-permute-start.4 = (f32[1,512]{1,0:T(1,128)S(1)}, f32[1,512]{1,0:T(1,128)S(1)}, u32[]{:S(2)}, u32[]{:S(2)}) collective-permute-start(f32[1,512]{1,0:T(1,128)S(1)} %get-tuple-element.72), channel_id=1, source_target_pairs={{0,1},{1,0},{2,3},{3,2},{4,5},{5,4},{6,7},{7,6},{8,9},{9,8},{10,11... | collective-permute-start | bytes 6152 | tf_op jit(solution)/shard_map/ppermute | solution.py:632
  19.8 3.6 %collective-permute-start.5 = (f32[1,512]{1,0:T(1,128)S(1)}, f32[1,512]{1,0:T(1,128)S(1)}, u32[]{:S(2)}, u32[]{:S(2)}) collective-permute-start(f32[1,512]{1,0:T(1,128)S(1)} %add.9), channel_id=1, source_target_pairs={{0,2},{1,3},{2,0},{3,1},{4,6},{5,7},{6,4},{7,5},{8,10},{9,11},{10,... | collective-permute-start | bytes 6152 | tf_op jit(solution)/shard_map/ppermute | solution.py:632
  23.4 3.6 %collective-permute-start.6 = (f32[1,512]{1,0:T(1,128)S(1)}, f32[1,512]{1,0:T(1,128)S(1)}, u32[]{:S(2)}, u32[]{:S(2)}) collective-permute-start(f32[1,512]{1,0:T(1,128)S(1)} %add.10), channel_id=1, source_target_pairs={{0,4},{1,5},{2,6},{3,7},{4,0},{5,1},{6,2},{7,3},{8,12},{9,13},{10,... | collective-permute-start | bytes 6152 | tf_op jit(solution)/shard_map/ppermute | solution.py:632
